TPU v7x, 128 devices: a whole 4x4x4 slice. The times are simulated.
128 devices in a mesh: ti: 8 (over x_lo, z), tj: 16 (over y, x_hi, core).
Axes of the slice: x: 4 (x_hi: 2, x_lo: 2; x = x_hi * 2 + x_lo), y: 4, z: 4, core: 2. Of those that a mesh axis runs over, the one named last changes fastest.
Arguments:
- alignment_source: float32 [64, 256, 64], P('tj', 'ti'), may hold values from -6 to 6
- couple_source: float32 [256, 256, 128], P('ti', 'tj'), may hold values from -6 to 6
- tensor_operand_matrix: float32 [64, 64], replicated, may hold values from -0.75 to 0.75
- tensor_final_matrix: float32 [1024, 128], replicated, may hold values from -0.75 to 0.75
- mixing_content_matrix: float32 [64, 256], replicated, may hold values from -0.75 to 0.75
- mixing_switch_matrix: float32 [64, 256], replicated, may hold values from -0.75 to 0.75
- mixing_score_matrix: float32 [128, 8], replicated, may hold values from -48 to 48, as said below
- mixing_final_matrix: float32 [256, 64], replicated, may hold values from -0.375 to 0.375
- alignment_expand_matrix: float32 [64, 512], replicated, may hold values from -0.75 to 0.75
- alignment_shrink_matrix: float32 [256, 64], replicated, may hold values from -0.375 to 0.375
- couple_expand_matrix: float32 [128, 1024], replicated, may hold values from -0.5 to 0.5
- couple_shrink_matrix: float32 [512, 128], replicated, may hold values from -0.25 to 0.25
Outputs:
- alignment_result: float32 [64, 256, 64], P('tj', 'ti')
- couple_result: float32 [256, 256, 128], P('ti', 'tj')
Inputs may be any that keep to these rules, and one draw needn't show every extreme that they name: `mixing_score_matrix`: each column is one head's logit projection.
All inputs are finite; a program needn't handle non-finite values.
Results may differ from a plain program's by a relative error of at most 0.00026.
Values sent between devices are 32-bit elements; how exact they have to be, the bound alone decides.
No kernel may reach another device: no remote copies, remote signals or barrier semaphores. Data moves between devices by JAX's collectives and lax.ppermute only.
A program may use at most 64 MiB of HBM per device.

v0:
```python
import math

import jax
import jax.numpy as jnp
from jax import lax
from jax.sharding import PartitionSpec as P

C_Z = 128
FACTOR_WIDTH = 32
MEAN_GROUPS = 8
GROUP_FEATURES = 32


exact_arithmetic = lax.Precision.HIGHEST
epsilon = 1e-05


def in_order(parts, dim):
    parts = jnp.moveaxis(parts, 0, dim)
    dims = parts.shape
    return parts.reshape(*dims[:dim], dims[dim] * dims[dim + 1], *dims[dim + 2 :])


def copy_for_each(x, axis):
    length = lax.axis_size(axis)
    return lax.all_to_all(jnp.broadcast_to(x[None], (length, *x.shape)), axis, 0, 0, tiled=True)


def gathered_copies(x, axis, dim):
    return in_order(copy_for_each(x, axis), dim)


def feature_standardize(inputs):
    mean_val = jnp.mean(inputs, axis=-1, keepdims=True)
    centred = inputs - mean_val
    variance = jnp.mean(centred * centred, axis=-1, keepdims=True)
    return centred * lax.rsqrt(variance + epsilon)


def feedforward_block(inputs, gate_up, down):
    hidden = jnp.einsum("...c,cd->...d", inputs, gate_up, precision=exact_arithmetic)
    half_width = down.shape[0]
    activated = jax.nn.silu(hidden[..., :half_width]) * hidden[..., half_width:]
    return jnp.einsum("...c,cd->...d", activated, down, precision=exact_arithmetic)


def shards(
    alignment_source,
    couple_source,
    tensor_operand_matrix,
    tensor_final_matrix,
    mixing_content_matrix,
    mixing_switch_matrix,
    mixing_score_matrix,
    mixing_final_matrix,
    alignment_expand_matrix,
    alignment_shrink_matrix,
    couple_expand_matrix,
    couple_shrink_matrix,
):
    sequence_index = alignment_source.shape[0]
    residue_index = alignment_source.shape[1]
    col_count = couple_source.shape[1]
    tj_count = lax.axis_size("tj")
    sequence_count_all = sequence_index * tj_count
    alignment_standardized = feature_standardize(alignment_source)
    tensor_operands = jnp.einsum(
        "zji,in->zjn", alignment_standardized, tensor_operand_matrix, precision=exact_arithmetic
    )
    left_proj = tensor_operands[..., :FACTOR_WIDTH]
    right_proj = tensor_operands[..., FACTOR_WIDTH:]
    left_all = gathered_copies(left_proj, "tj", 0)
    right_wide = gathered_copies(right_proj, "ti", 1)
    right_all = lax.all_to_all(right_wide, "tj", split_axis=1, concat_axis=0, tiled=True)
    block_size = math.gcd(residue_index, 32)
    block_count = residue_index // block_size
    left_blocks = left_all.reshape(
        sequence_count_all, block_count, block_size, FACTOR_WIDTH
    ).transpose(1, 0, 2, 3)
    pair_blocks = couple_source.reshape(block_count, block_size, col_count, C_Z)

    def pair_block(inputs_pair):
        left_block, pair_rows = inputs_pair
        outer_prod = (
            jnp.einsum("sia,sjb->ijab", left_block, right_all, precision=exact_arithmetic)
            / sequence_count_all
        )
        flattened = outer_prod.reshape(-1, FACTOR_WIDTH * FACTOR_WIDTH)
        update = jnp.dot(
            flattened,
            tensor_final_matrix,
            precision=exact_arithmetic,
            preferred_element_type=jnp.float32,
        )
        pair_mid = pair_rows + update.reshape(pair_rows.shape)
        pair_normed = feature_standardize(pair_mid)
        logits = jnp.einsum(
            "ijc,ch->hij", pair_normed, mixing_score_matrix, precision=exact_arithmetic
        )
        pair_next = pair_mid + feedforward_block(
            pair_normed, couple_expand_matrix, couple_shrink_matrix
        )
        return (pair_next, logits)

    pair_next, logit_blocks = lax.map(pair_block, (left_blocks, pair_blocks))
    couple_result = pair_next.reshape(residue_index, col_count, C_Z)
    local_logits = logit_blocks.transpose(1, 0, 2, 3).reshape(MEAN_GROUPS, residue_index, col_count)
    logits_all = gathered_copies(local_logits, "tj", 2)
    row_max = jnp.max(logits_all, axis=2, keepdims=True)
    exp_terms = jnp.exp(logits_all - row_max)
    weights = exp_terms / jnp.sum(exp_terms, axis=2, keepdims=True)
    sigmoid_switch = jax.nn.sigmoid(
        jnp.einsum(
            "zji,in->zjn", alignment_standardized, mixing_switch_matrix, precision=exact_arithmetic
        )
    )
    sequence_slice = gathered_copies(alignment_standardized, "ti", 1)
    seg_values = jnp.einsum(
        "jzb,bq->jzq", sequence_slice, mixing_content_matrix, precision=exact_arithmetic
    )
    seg_values = seg_values.reshape(
        sequence_index, sequence_slice.shape[1], MEAN_GROUPS, GROUP_FEATURES
    )
    group_mixed = jnp.einsum("hij,sjhc->sihc", weights, seg_values, precision=exact_arithmetic)
    group_mixed = group_mixed.reshape(sequence_index, residue_index, MEAN_GROUPS * GROUP_FEATURES)
    alignment_between = alignment_source + jnp.einsum(
        "xvr,rq->xvq", sigmoid_switch * group_mixed, mixing_final_matrix, precision=exact_arithmetic
    )
    alignment_result = alignment_between + feedforward_block(
        feature_standardize(alignment_between), alignment_expand_matrix, alignment_shrink_matrix
    )
    return (alignment_result, couple_result)


def solution(mesh):
    in_specs = (
        P("tj", "ti", None),
        P("ti", "tj", None),
        P(),
        P(),
        P(),
        P(),
        P(),
        P(),
        P(),
        P(),
        P(),
        P(),
    )
    out_specs = (P("tj", "ti", None), P("ti", "tj", None))
    return jax.shard_map(shards, mesh=mesh, in_specs=in_specs, out_specs=out_specs, check_vma=False)
```

profile of v0, /device:TPU:1, one launch (start us, length us, event | category | flops | bytes accessed | tf_op | source)
XLA Modules:
  0.0 114.7 jit_solution(3051346174646826219)
XLA Ops:
  0.6 0.0 copy-start
  0.6 1.0 reduce_sum.65
  1.6 1.0 multiply_reduce_fusion.2
  2.7 0.9 subtract_multiply_fusion
  3.6 1.0 fusion.45
  4.6 0.1 fusion.52
  4.7 0.1 copy.28
  4.8 0.1 broadcast_bitcast_fusion.2
  4.8 0.9 reshape.95
  5.7 6.8 %all-to-all-start.1 = ((f32[8,1,4096]{2,1,0:T(1,128)}), f32[8,1,4096]{2,1,0:T(1,128)S(1)}, u32[]{:S(2)}, u32[]{:S(2)}) async-start(f32[8,1,4096]{2,1,0:T(1,128)} %reshape.95), calls=%async_computation.1 | async-start | bytes 262144 | tf_op jit(solution)/shard_map/all_to_all | solution.py:26
  12.5 0.1 broadcast_in_dim.14
  12.6 1.0 reshape.91
  13.6 4.3 %all-to-all-done.1 = f32[8,1,4096]{2,1,0:T(1,128)S(1)} async-done(((f32[8,1,4096]{2,1,0:T(1,128)}), f32[8,1,4096]{2,1,0:T(1,128)S(1)}, u32[]{:S(2)}, u32[]{:S(2)}) %all-to-all-start.1) | async-done | bytes 131104 | tf_op jit(solution)/shard_map/all_to_all | solution.py:26
  17.9 3.4 %all-to-all-start = ((f32[8,1,8192]{2,1,0:T(1,128)}), f32[8,1,8192]{2,1,0:T(1,128)S(1)}, u32[]{:S(2)}, u32[]{:S(2)}) async-start(f32[8,1,8192]{2,1,0:T(1,128)} %reshape.91), calls=%async_computation | async-start | bytes 524288 | tf_op jit(solution)/shard_map/all_to_all | solution.py:26
  21.4 0.5 broadcast.108
  21.9 1.0 reduce.4
  22.8 0.2 reshape.96
  23.1 0.2 copy.46
  23.3 1.0 reshape.97
  24.3 3.1 %all-to-all-done = f32[8,1,8192]{2,1,0:T(1,128)S(1)} async-done(((f32[8,1,8192]{2,1,0:T(1,128)}), f32[8,1,8192]{2,1,0:T(1,128)S(1)}, u32[]{:S(2)}, u32[]{:S(2)}) %all-to-all-start) | async-done | bytes 262176 | tf_op jit(solution)/shard_map/all_to_all | solution.py:26
  27.4 9.9 %all-to-all-start.2 = ((f32[16,1,2048]{2,1,0:T(1,128)}), f32[16,1,2048]{2,1,0:T(1,128)S(1)}, u32[]{:S(2)}, u32[]{:S(2)}) async-start(f32[16,1,2048]{2,1,0:T(1,128)} %reshape.97), calls=%async_computation.2 | async-start | bytes 262144 | tf_op jit(solution)/shard_map/all_to_all | solution.py:74
  37.3 0.2 broadcast_bitcast_fusion.1
  37.5 1.4 %reshape.93 = f32[16,1,4096]{2,1,0:T(1,128)} reshape(f32[16,32,4,32]{3,2,1,0:T(4,128)S(1)} %broadcast_bitcast_fusion.1) | data formatting | bytes 524288
  38.8 0.1 copy.26
  38.9 1.3 %reduce.2 = f32[8,8192]{1,0:T(8,128)S(1)} reduce(f32[8,1,8192]{2,1,0:T(1,128)S(1)} %all-to-all-done, f32[]{:T(128)} %broadcast.108), dimensions={1}, to_apply=%all_to_all.23.reduce_sub_computation | reduce | bytes 524292 | tf_op jit(solution)/shard_map/all_to_all | solution.py:26
  40.2 0.2 reshape.92
  40.5 4.4 %all-to-all-done.2 = f32[16,1,2048]{2,1,0:T(1,128)S(1)} async-done(((f32[16,1,2048]{2,1,0:T(1,128)}), f32[16,1,2048]{2,1,0:T(1,128)S(1)}, u32[]{:S(2)}, u32[]{:S(2)}) %all-to-all-start.2) | async-done | bytes 131104 | tf_op jit(solution)/shard_map/all_to_all | solution.py:74
  44.9 4.0 %all-to-all-start.3 = ((f32[16,1,4096]{2,1,0:T(1,128)}), f32[16,1,4096]{2,1,0:T(1,128)S(1)}, u32[]{:S(2)}, u32[]{:S(2)}) async-start(f32[16,1,4096]{2,1,0:T(1,128)} %reshape.93), calls=%async_computation.3 | async-start | bytes 524288 | tf_op jit(solution)/shard_map/all_to_all | solution.py:26
  48.9 2.0 %fusion.55 = f32[4,256,8,32]{1,3,0,2:T(8,128)} fusion(f32[4,256,64,1]{2,1,0,3:T(8,128)S(1)} %bitcast.111, f32[8,32,64,1]{2,1,3,0:T(8,128)S(1)} %bitcast.113), kind=kOutput, calls=%fused_computation.83 | convolution fusion | flops 201326592 | bytes 1376256 | tf_op jit(solution)/shard_map/jzb,bq->jzq/dot_general | solution.py:118
  50.9 0.9 reduce.5
  51.9 0.3 reshape.98
  52.1 5.5 %all-to-all-done.3 = f32[16,1,4096]{2,1,0:T(1,128)S(1)} async-done(((f32[16,1,4096]{2,1,0:T(1,128)}), f32[16,1,4096]{2,1,0:T(1,128)S(1)}, u32[]{:S(2)}, u32[]{:S(2)}) %all-to-all-start.3) | async-done | bytes 262176 | tf_op jit(solution)/shard_map/all_to_all | solution.py:26
  57.6 1.3 %reduce.3 = f32[16,4096]{1,0:T(8,128)S(1)} reduce(f32[16,1,4096]{2,1,0:T(1,128)S(1)} %all-to-all-done.3, f32[]{:T(128)} %broadcast.108), dimensions={1}, to_apply=%all_to_all.28.reduce_sub_computation | reduce | bytes 524292 | tf_op jit(solution)/shard_map/all_to_all | solution.py:26
  58.9 0.5 reshape.94
  59.4 9.6 %fusion = f32[32,16,32,32]{2,3,0,1:T(8,128)} fusion(f32[16,4,32,32]{3,1,2,0:T(4,128)S(1)} %bitcast.108, f32[4,16,16,32]{3,0,2,1:T(4,128)S(1)} %bitcast.109), kind=kOutput, calls=%fused_computation.1 | convolution fusion | flops 403177472 | bytes 2490368 | tf_op jit(solution)/shard_map/while/body/eval_jaxpr/sia,sjb->ijab/dot_general | solution.py:85
  69.0 8.9 %copy.35 = f32[32,16,32,32]{3,2,1,0:T(8,128)} copy(f32[32,16,32,32]{2,3,0,1:T(8,128)} %fusion) | data formatting | bytes 4194304 | tf_op jit(solution)/shard_map/while/body/eval_jaxpr/div | solution.py:85
  78.0 6.9 %dot_general.55 = f32[32,16,1024]{2,1,0:T(8,128)S(1)} reshape(f32[32,16,32,32]{3,2,1,0:T(8,128)} %copy.35) | data formatting | bytes 4194304 | tf_op jit(solution)/shard_map/while/body/eval_jaxpr/dot_general | solution.py:89
  84.9 2.8 %fusion.53 = (f32[32,16]{1,0:T(8,128)S(1)}, f32[32,16,128]{2,1,0:T(8,128)S(1)}) fusion(f32[32,16,128]{2,1,0:T(8,128)} %param.13, f32[32,16,1024]{2,1,0:T(8,128)S(1)} %dot_general.55, f32[1024,128]{1,0:T(8,128)S(1)} %copy-done.3), kind=kOutput, calls=%fused_computation.76 | convolution fusion | flops 805436928 | bytes 3147776 | tf_op jit(solution)/shard_map/while/body/eval_jaxpr/dot_general | solution.py:89
  87.8 0.2 multiply_reduce_fusion
  88.0 3.2 %fusion.17 = f32[32,16,1024]{2,1,0:T(8,128)} fusion(f32[128,1024]{1,0:T(8,128)S(1)} %copy-done, f32[32,16,128]{2,1,0:T(8,128)S(1)} %get-tuple-element.25, f32[32,16]{1,0:T(8,128)S(1)} %add_rsqrt_fusion, f32[32,16]{1,0:T(8,128)S(1)} %broadcast_multiply_fusion), kind=kOutput, calls=%fused_computation.28 | convolution fusion | flops 805437440 | bytes 2887680 | tf_op jit(solution)/shard_map/while/body/eval_jaxpr/...c,cd->...d/dot_general | solution.py:41
  91.2 2.0 %convolution_bitcast_fusion.1 = f32[8,32,16]{2,0,1:T(8,128)S(1)} fusion(f32[32,16,128]{2,1,0:T(8,128)S(1)} %get-tuple-element.25, f32[32,16]{1,0:T(8,128)S(1)} %add_rsqrt_fusion, f32[32,16]{1,0:T(8,128)S(1)} %broadcast_multiply_fusion, f32[128,8]{0,1:T(8,128)S(1)} %copy-done.10), kind=kOutput, calls=%fused_computation.5 | convolution fusion | flops 6422528 | bytes 286720 | tf_op jit(solution)/shard_map/while/body/eval_jaxpr/ijc,ch->hij/dot_general | solution.py:97
  93.3 0.1 copy.36
  93.4 0.1 broadcast_bitcast_fusion
  93.5 1.2 %reshape.99 = f32[16,1,4096]{2,1,0:T(1,128)} reshape(f32[16,8,16,32]{3,2,1,0:T(8,128)S(1)} %broadcast_bitcast_fusion) | data formatting | bytes 524288
  94.7 4.3 %all-to-all-start.4 = ((f32[16,1,4096]{2,1,0:T(1,128)}), f32[16,1,4096]{2,1,0:T(1,128)S(1)}, u32[]{:S(2)}, u32[]{:S(2)}) async-start(f32[16,1,4096]{2,1,0:T(1,128)} %reshape.99), calls=%async_computation.4 | async-start | bytes 524288 | tf_op jit(solution)/shard_map/all_to_all | solution.py:26
  99.0 3.4 %convolution_add_fusion.1 = f32[32,16,128]{2,1,0:T(8,128)} fusion(f32[32,16,128]{2,1,0:T(8,128)S(1)} %get-tuple-element.25, f32[32,16,1024]{2,1,0:T(8,128)} %fusion.17, f32[512,128]{1,0:T(8,128)S(1)} %copy-done.7), kind=kOutput, calls=%fused_computation.4 | convolution fusion | flops 404029440 | bytes 2883584 | tf_op jit(solution)/shard_map/while/body/eval_jaxpr/...c,cd->...d/dot_general | solution.py:44
  102.4 5.4 %all-to-all-done.4 = f32[16,1,4096]{2,1,0:T(1,128)S(1)} async-done(((f32[16,1,4096]{2,1,0:T(1,128)}), f32[16,1,4096]{2,1,0:T(1,128)S(1)}, u32[]{:S(2)}, u32[]{:S(2)}) %all-to-all-start.4) | async-done | bytes 262176 | tf_op jit(solution)/shard_map/all_to_all | solution.py:26
  107.7 1.3 %reduce.6 = f32[16,4096]{1,0:T(8,128)S(1)} reduce(f32[16,1,4096]{2,1,0:T(1,128)S(1)} %all-to-all-done.4, f32[]{:T(128)} %broadcast.108), dimensions={1}, to_apply=%all_to_all.29.reduce_sub_computation | reduce | bytes 524292 | tf_op jit(solution)/shard_map/all_to_all | solution.py:26
  109.0 0.3 reshape.100
  109.3 0.1 bitcast_reduce_fusion
  109.4 0.1 bitcast_bitcast_fusion
  109.5 0.2 exponential_reduce_fusion
  109.7 0.1 copy.37
  109.8 0.2 fusion.7
  110.0 1.0 copy-done.1
  110.9 1.2 %convolution_bitcast_fusion = f32[4,32,8,32]{1,3,0,2:T(8,128)S(1)} fusion(f32[4,256,8,32]{1,3,0,2:T(8,128)S(1)} %copy-done.1, f32[8,32,256]{1,2,0:T(8,128)S(1)} %fusion.7), kind=kOutput, calls=%fused_computation.2 | convolution fusion | flops 100663296 | bytes 1441792 | tf_op jit(solution)/shard_map/hij,sjhc->sihc/dot_general | solution.py:124
  112.1 0.0 copy-start.9
  112.1 0.2 copy.39
  112.4 0.2 reshape.75
  112.5 0.3 fusion.4
  112.8 0.3 fusion.54
  113.2 0.2 multiply_reduce_fusion.1
  113.4 0.4 fusion.27
  113.8 0.9 convolution_add_fusion.2
  (28 shorter events, 0.2 us)
Async XLA Ops:
  0.6 87.4 %copy-start = (f32[128,1024]{1,0:T(8,128)S(1)}, f32[128,1024]{1,0:T(8,128)}, u32[]{:S(2)}) copy-start(f32[128,1024]{1,0:T(8,128)} %param.22) | copy-start | bytes 1572868
  5.7 12.2 %all-to-all-start.1 = ((f32[8,1,4096]{2,1,0:T(1,128)}), f32[8,1,4096]{2,1,0:T(1,128)S(1)}, u32[]{:S(2)}, u32[]{:S(2)}) async-start(f32[8,1,4096]{2,1,0:T(1,128)} %reshape.95), calls=%async_computation.1 | async-start | bytes 262144 | tf_op jit(solution)/shard_map/all_to_all | solution.py:26
  17.9 9.4 %all-to-all-start = ((f32[8,1,8192]{2,1,0:T(1,128)}), f32[8,1,8192]{2,1,0:T(1,128)S(1)}, u32[]{:S(2)}, u32[]{:S(2)}) async-start(f32[8,1,8192]{2,1,0:T(1,128)} %reshape.91), calls=%async_computation | async-start | bytes 524288 | tf_op jit(solution)/shard_map/all_to_all | solution.py:26
  23.0 15.8 %copy-start.5 = (f32[64,256]{1,0:T(8,128)S(1)}, f32[64,256]{1,0:T(8,128)}, u32[]{:S(2)}) copy-start(f32[64,256]{1,0:T(8,128)} %param.16) | copy-start | bytes 196612
  27.4 17.5 %all-to-all-start.2 = ((f32[16,1,2048]{2,1,0:T(1,128)}), f32[16,1,2048]{2,1,0:T(1,128)S(1)}, u32[]{:S(2)}, u32[]{:S(2)}) async-start(f32[16,1,2048]{2,1,0:T(1,128)} %reshape.97), calls=%async_computation.2 | async-start | bytes 262144 | tf_op jit(solution)/shard_map/all_to_all | solution.py:74
  44.9 12.7 %all-to-all-start.3 = ((f32[16,1,4096]{2,1,0:T(1,128)}), f32[16,1,4096]{2,1,0:T(1,128)S(1)}, u32[]{:S(2)}, u32[]{:S(2)}) async-start(f32[16,1,4096]{2,1,0:T(1,128)} %reshape.93), calls=%async_computation.3 | async-start | bytes 524288 | tf_op jit(solution)/shard_map/all_to_all | solution.py:26
  78.0 6.9 %copy-start.3 = (f32[1024,128]{1,0:T(8,128)S(1)}, f32[1024,128]{1,0:T(8,128)}, u32[]{:S(2)}) copy-start(f32[1024,128]{1,0:T(8,128)} %param.15) | copy-start | bytes 1572868
  87.7 3.5 %copy-start.10 = (f32[128,8]{0,1:T(8,128)S(1)}, f32[128,8]{0,1:T(8,128)}, u32[]{:S(2)}) copy-start(f32[128,8]{0,1:T(8,128)} %param.18) | copy-start | bytes 12292
  91.2 7.7 %copy-start.7 = (f32[512,128]{1,0:T(8,128)S(1)}, f32[512,128]{1,0:T(8,128)}, u32[]{:S(2)}) copy-start(f32[512,128]{1,0:T(8,128)} %param.23) | copy-start | bytes 786436
  94.7 13.1 %all-to-all-start.4 = ((f32[16,1,4096]{2,1,0:T(1,128)}), f32[16,1,4096]{2,1,0:T(1,128)S(1)}, u32[]{:S(2)}, u32[]{:S(2)}) async-start(f32[16,1,4096]{2,1,0:T(1,128)} %reshape.99), calls=%async_computation.4 | async-start | bytes 524288 | tf_op jit(solution)/shard_map/all_to_all | solution.py:26
  109.7 1.2 %copy-start.1 = (f32[4,256,8,32]{1,3,0,2:T(8,128)S(1)}, f32[4,256,8,32]{1,3,0,2:T(8,128)}, u32[]{:S(2)}) copy-start(f32[4,256,8,32]{1,3,0,2:T(8,128)} %fusion.55) | copy-start | bytes 3145732
  110.9 1.6 %copy-start.8 = (f32[64,256]{1,0:T(8,128)S(1)}, f32[64,256]{1,0:T(8,128)}, u32[]{:S(2)}) copy-start(f32[64,256]{1,0:T(8,128)} %param.17) | copy-start | bytes 196612
  110.9 1.9 %copy-start.2 = (f32[4,32,64]{2,1,0:T(8,128)S(1)}, f32[4,32,64]{2,1,0:T(8,128)}, u32[]{:S(2)}) copy-start(f32[4,32,64]{2,1,0:T(8,128)} %param.12) | copy-start | bytes 98308
  110.9 1.9 %copy-start.6 = (f32[256,64]{0,1:T(8,128)S(1)}, f32[256,64]{0,1:T(8,128)}, u32[]{:S(2)}) copy-start(f32[256,64]{0,1:T(8,128)} %param.19) | copy-start | bytes 196612
  110.9 2.4 %copy-start.4 = (f32[64,512]{1,0:T(8,128)S(1)}, f32[64,512]{1,0:T(8,128)}, u32[]{:S(2)}) copy-start(f32[64,512]{1,0:T(8,128)} %param.20) | copy-start | bytes 393220
  112.1 1.7 %copy-start.9 = (f32[256,64]{0,1:T(8,128)S(1)}, f32[256,64]{0,1:T(8,128)}, u32[]{:S(2)}) copy-start(f32[256,64]{0,1:T(8,128)} %param.21) | copy-start | bytes 196612
where the time goes:
time: 116 us; the launch traced here: 115 us
  starting transfers between devices  28.4 us (24%)
  matrix products  27.1 us (23%)
  local copies, waits for them, and re-layouts  26.1 us (22%)
  waiting for transfers between devices  22.7 us (20%)
  other arithmetic  9.49 us (8%)
    all_to_all x4, starting transfers between devices, copy_for_each(): lax.all_to_all(jnp.broadcast_to(x[None], (length, *x.shape)), axis, 0, 0,...  18.5 us
    all_to_all x4, waiting for transfers between devices, copy_for_each(): lax.all_to_all(jnp.broadcast_to(x[None], (length, *x.shape)), axis, 0, 0,...  18.2 us
    all_to_all x1, starting transfers between devices, shards(): lax.all_to_all(right_wide, 'tj', split_axis=1, concat_axis=0, tiled=True)  9.89 us
    dot_general x1, matrix products, pair_block(): jnp.einsum('sia,sjb->ijab', left_block, right_all, precision=exact_arithm...  9.6 us
    div x1, local copies, waits for them, and re-layouts, pair_block(): jnp.einsum('sia,sjb->ijab', left_block, right_all, precision=exact_arithm...  8.95 us
    unnamed x36, local copies, waits for them, and re-layouts  8.43 us
    dot_general x1, local copies, waits for them, and re-layouts, pair_block(): jnp.dot(flattened, tensor_final_matrix, precision=exact_arithmetic, prefe...  6.91 us
    all_to_all x4, other arithmetic, copy_for_each(): lax.all_to_all(jnp.broadcast_to(x[None], (length, *x.shape)), axis, 0, 0,...  4.74 us
  transfers between devices with their start and end apart: 5, of which 5 were waited for; matrix products, arithmetic and copies ran while one was open for 12% of the time, Pallas kernels for 0%

commit v1 on v0

v1 whole, which is shorter than its diff:
```python
import functools

import jax
import jax.numpy as jnp
from jax import lax
from jax.experimental import pallas as pl
from jax.experimental.pallas import tpu as pltpu
from jax.sharding import PartitionSpec as P

F32 = jnp.float32
BF16 = jnp.bfloat16
EPS = 1e-05
TI = 8
TJ = 16
ROWS = 4
TOK = 32
COLS = 16
NN = (((1,), (0,)), ((), ()))
NT = (((1,), (1,)), ((), ()))


def dot(a, b, dims=NN):
    return lax.dot_general(a, b, dims, preferred_element_type=F32)


def split(x):
    hi = x.astype(BF16)
    return hi, (x - hi.astype(F32)).astype(BF16)


def dot3(a, b, dims=NN):
    (ah, al), (bh, bl) = a, b
    return dot(ah, bh, dims) + dot(ah, bl, dims) + dot(al, bh, dims)


def iota(shape, dim):
    return lax.broadcasted_iota(jnp.int32, shape, dim)


def normed(x):
    centred = x - jnp.mean(x, axis=-1, keepdims=True)
    var = jnp.mean(centred * centred, axis=-1, keepdims=True)
    return centred * lax.rsqrt(var + EPS)


def spread_heads(w):
    n, l = iota((256, 1024), 0), iota((256, 1024), 1)
    place = (n == (l // 128) * 32 + l % 32).astype(BF16)
    wide = dot(w, place)
    tall = jnp.concatenate([wide] * 4, axis=0)
    keep = iota((256, 1024), 0) // 64 == (iota((256, 1024), 1) // 32) % 4
    return jnp.where(keep, tall, 0.0)


def first_kernel(x_ref, send_ref):
    x = normed(x_ref[...])
    low = jnp.concatenate([x[0], x[1]], axis=1)
    high = jnp.concatenate([x[2], x[3]], axis=1)
    for d in range(TI):
        send_ref[d, :TOK, :] = low
        send_ref[d, TOK:, :] = high


def left_kernel(own_ref, w_ref, left_ref, wr_hi_ref, wr_lo_ref):
    x = jnp.concatenate([own_ref[0, :TOK, :], own_ref[0, TOK:, :]], axis=1)
    xs = split(jnp.concatenate([x] * 4, axis=0))
    ws = split(w_ref[...])
    pick = (iota((128, 64), 0) // 4 == iota((128, 64), 1)).astype(BF16)
    tile_k = (iota((64, 256), 0) == iota((64, 256), 1) % 64).astype(BF16)
    keep = iota((128, 256), 0) % 4 == iota((128, 256), 1) // 64
    wl = []
    for part in ws:
        rows = dot(pick, part, NT).astype(BF16)
        wl.append(jnp.where(keep, dot(rows, tile_k), 0.0).astype(BF16))
    prod = dot3(tuple(wl), xs, NT) * (1.0 / 64.0)
    group = iota((16, 128), 1) // 32
    for half in range(2):
        out = jnp.zeros((16, 128), F32)
        for q in range(4):
            at = half * 64 + q * 16
            out = jnp.where(group == q, prod[at : at + 16], out)
        left_ref[half * 16 : half * 16 + 16, :] = out
    tile_b = (iota((64, 128), 0) == 32 + iota((64, 128), 1) % 32).astype(BF16)
    keep_r = iota((256, 128), 0) // 64 == iota((256, 128), 1) // 32
    for part, ref in zip(ws, (wr_hi_ref, wr_lo_ref)):
        tall = jnp.concatenate([dot(part, tile_b)] * 4, axis=0)
        ref[...] = jnp.where(keep_r, tall, 0.0).astype(BF16)


def all_tokens(recv_ref):
    return (
        recv_ref[:, :TOK, :].reshape(TI * TOK, 128),
        recv_ref[:, TOK:, :].reshape(TI * TOK, 128),
    )


def right_kernel(recv_ref, left_ref, wr_hi_ref, wr_lo_ref, send_ref):
    low, high = all_tokens(recv_ref)
    wh, wl = wr_hi_ref[...], wr_lo_ref[...]
    right = dot3(split(low), (wh[:128], wl[:128])) + dot3(split(high), (wh[128:], wl[128:]))
    left = left_ref[...]
    for d in range(TJ):
        send_ref[d, :32, :] = left
        send_ref[d, 32:, :] = right[d * COLS : (d + 1) * COLS]


def values_kernel(recv_ref, wv_ref, t_ref, score_ref, v_ref, t_out_ref, score_out_ref):
    low, high = all_tokens(recv_ref)
    wv = [spread_heads(part).astype(BF16) for part in split(wv_ref[...])]
    xs = split(jnp.concatenate([low, high], axis=1))
    for h in range(8):
        cols = slice(h * 128, (h + 1) * 128)
        vh, vl = split(dot3(xs, (wv[0][:, cols], wv[1][:, cols])))
        for d in range(TJ):
            at = (d * 8 + h) * COLS
            v_ref[at : at + COLS, :128] = vh[d * COLS : (d + 1) * COLS]
            v_ref[at : at + COLS, 128:] = vl[d * COLS : (d + 1) * COLS]
    th, tl = split(t_ref[...])
    t_out_ref[:, :128] = th
    t_out_ref[:, 128:] = tl
    score = score_ref[...]
    tall = jnp.concatenate([jnp.broadcast_to(score[h : h + 1], (16, 128)) for h in range(8)], axis=0)
    sh, sl = split(tall.T)
    score_out_ref[:, :128] = sh
    score_out_ref[:, 128:] = sl


def pair_kernel(recv_ref, pair_ref, t_ref, score_ref, mid_ref, send_ref, f_hi, f_lo):
    rows = [
        jnp.concatenate([recv_ref[:, r, :], recv_ref[:, 16 + r, :]], axis=1) for r in range(16)
    ]
    left = jnp.concatenate(rows, axis=0).T
    lh, ll = split(left)
    left3 = jnp.concatenate([lh, lh, ll], axis=1)
    group = iota((16, 128), 1) // 32
    zero = jnp.zeros((16, 128), BF16)
    for pair in range(COLS // 2):
        blocks = []
        for j in (2 * pair, 2 * pair + 1):
            right = recv_ref[:, 32 + j, :]
            turned = [split(pltpu.roll(right, 32 * d, 1) if d else right) for d in range(4)]
            parts = []
            for which in range(2):
                tiles = [
                    jnp.where(group == a, turned[(a - s) % 4][which], zero)
                    for a in range(4)
                    for s in range(4)
                ]
                parts.append(jnp.concatenate(tiles, axis=0))
            blocks.append(jnp.concatenate([parts[0], parts[1], parts[0]], axis=0))
        outer = dot(left3, jnp.concatenate(blocks, axis=1))
        oh, ol = split(outer)
        for q in range(2):
            at = (2 * pair + q) * TOK
            for g in range(8):
                take = (slice(g * 32, g * 32 + 32), slice(q * 128, q * 128 + 128))
                f_hi[at : at + TOK, g * 128 : g * 128 + 128] = oh[take]
                f_lo[at : at + TOK, g * 128 : g * 128 + 128] = ol[take]
    wide = dot(f_hi[...], t_ref[...])
    update = wide[:, :128] + wide[:, 128:] + dot(f_lo[...], t_ref[:, :128])
    normal = []
    for j in range(COLS):
        mid = pair_ref[:, j, :] + update[j * TOK : (j + 1) * TOK]
        mid_ref[j] = mid
        normal.append(normed(mid))
    nh, nl = split(jnp.concatenate(normal, axis=0))
    wide = dot(nh, score_ref[...])
    logits = wide[:, :128] + wide[:, 128:] + dot(nl, score_ref[:, :128])
    column = iota((TOK, 128), 1) % 16
    tile = jnp.zeros((TOK, 128), F32)
    for j in range(COLS):
        tile = jnp.where(column == j, logits[j * TOK : (j + 1) * TOK], tile)
    for d in range(TJ):
        send_ref[d] = tile


def pair_transition_kernel(mid_ref, expand_ref, shrink_ref, out_ref):
    eh, el = split(expand_ref[...])
    expand3 = jnp.concatenate([eh, eh, el], axis=0)
    sh, sl = split(shrink_ref[...])
    shrink2 = jnp.concatenate([sh, sl], axis=1)
    step = 4
    for at in range(0, COLS, step):
        mid = mid_ref[at : at + step].reshape(step * TOK, 128)
        nh, nl = split(normed(mid))
        hidden = dot(jnp.concatenate([nh, nl, nh], axis=1), expand3)
        gate = hidden[:, :512]
        act = gate / (1.0 + jnp.exp(-gate)) * hidden[:, 512:]
        ah, al = split(act)
        wide = dot(ah, shrink2)
        out = mid + wide[:, :128] + wide[:, 128:] + dot(al, sh)
        for j in range(step):
            out_ref[:, at + j, :] = out[j * TOK : (j + 1) * TOK]


def gates_kernel(own_ref, wg_ref, wf_ref, gate_ref, wf_hi_ref, wf_lo_ref):
    x = jnp.concatenate([own_ref[0, :TOK, :], own_ref[0, TOK:, :]], axis=1)
    wg = tuple(spread_heads(part).astype(BF16) for part in split(wg_ref[...]))
    logit = dot3(split(x), wg)
    gate_ref[...] = 1.0 / (1.0 + jnp.exp(-logit))
    for part, ref in zip(split(wf_ref[...]), (wf_hi_ref, wf_lo_ref)):
        ref[...] = spread_heads(part).T.astype(BF16)


def group_all(x, op):
    lane = iota(x.shape, 1)
    for d in (8, 4, 2, 1):
        other = jnp.where((lane & d) == 0, pltpu.roll(x, 128 - d, 1), pltpu.roll(x, d, 1))
        x = op(x, other)
    return x


def last_kernel(
    recv_ref, v_ref, gate_ref, wf_hi_ref, wf_lo_ref, x_ref, expand_ref, shrink_ref, out_ref, w_hi, w_lo
):
    top = recv_ref[0]
    for d in range(1, TJ):
        top = jnp.maximum(top, recv_ref[d])
    top = group_all(top, jnp.maximum)
    terms = [jnp.exp(recv_ref[d] - top) for d in range(TJ)]
    total = terms[0]
    for d in range(1, TJ):
        total = total + terms[d]
    inv = 1.0 / group_all(total, jnp.add)
    head = iota((TOK, 128), 1) // 16
    zero = jnp.zeros((TOK, 128), BF16)
    for d in range(TJ):
        wh, wl = split(terms[d] * inv)
        for h in range(8):
            w_hi[h * TOK : (h + 1) * TOK, d * 128 : d * 128 + 128] = jnp.where(head == h, wh, zero)
            w_lo[h * TOK : (h + 1) * TOK, d * 128 : d * 128 + 128] = jnp.where(head == h, wl, zero)
    wide = dot(w_hi[...], v_ref[...])
    mixed = wide[:, :128] + wide[:, 128:] + dot(w_lo[...], v_ref[:, :128])
    gated = gate_ref[...] * jnp.concatenate([mixed[h * TOK : (h + 1) * TOK] for h in range(8)], axis=1)
    update = dot3(split(gated), (wf_hi_ref[...], wf_lo_ref[...]))
    mid = jnp.concatenate(
        [x_ref[s] + update[:, s * 64 : (s + 1) * 64] for s in range(ROWS)], axis=0
    )
    hidden = dot3(split(normed(mid)), split(expand_ref[...]))
    gate = hidden[:, :256]
    act = gate / (1.0 + jnp.exp(-gate)) * hidden[:, 256:]
    out = mid + dot3(split(act), split(shrink_ref[...]), NT)
    out_ref[...] = out.reshape(ROWS, TOK, 64)


def call(kernel, outs, *args, specs=None, scratch=(), flops=0):
    vmem = pl.BlockSpec(memory_space=pltpu.VMEM)
    in_specs = [vmem] * len(args) if specs is None else [s or vmem for s in specs]
    single = not isinstance(outs, (list, tuple))
    outs = [outs] if single else list(outs)
    moved = sum(a.size * a.dtype.itemsize for a in args) + sum(
        o.size * o.dtype.itemsize for o in outs
    )
    res = pl.pallas_call(
        kernel,
        out_shape=outs,
        in_specs=in_specs,
        out_specs=[vmem] * len(outs),
        scratch_shapes=list(scratch),
        compiler_params=pltpu.CompilerParams(vmem_limit_bytes=24 << 20),
        cost_estimate=pl.CostEstimate(flops=flops, bytes_accessed=moved, transcendentals=0),
    )(*args)
    return res[0] if single else res


def shape(dims, dtype=F32):
    return jax.ShapeDtypeStruct(dims, dtype)


def shards(
    alignment_source,
    couple_source,
    tensor_operand_matrix,
    tensor_final_matrix,
    mixing_content_matrix,
    mixing_switch_matrix,
    mixing_score_matrix,
    mixing_final_matrix,
    alignment_expand_matrix,
    alignment_shrink_matrix,
    couple_expand_matrix,
    couple_shrink_matrix,
):
    exchange = functools.partial(lax.all_to_all, split_axis=0, concat_axis=0, tiled=True)
    own = call(first_kernel, shape((TI, 64, 128)), alignment_source)
    tokens = exchange(own, "ti")
    left, wr_hi, wr_lo = call(
        left_kernel,
        [shape((32, 128)), shape((256, 128), BF16), shape((256, 128), BF16)],
        own,
        tensor_operand_matrix,
        flops=100_000_000,
    )
    factors = call(right_kernel, shape((TJ, 48, 128)), tokens, left, wr_hi, wr_lo)
    factors = exchange(factors, "tj")
    values, final2, score2 = call(
        values_kernel,
        [shape((2048, 256), BF16), shape((1024, 256), BF16), shape((128, 256), BF16)],
        tokens,
        mixing_content_matrix,
        tensor_final_matrix,
        mixing_score_matrix.T,
        flops=1_000_000_000,
    )
    mid, logits = call(
        pair_kernel,
        [shape((COLS, TOK, 128)), shape((TJ, TOK, 128))],
        factors,
        couple_source,
        final2,
        score2,
        scratch=[pltpu.VMEM((512, 1024), BF16), pltpu.VMEM((512, 1024), BF16)],
        flops=2_000_000_000,
    )
    logits = exchange(logits, "tj")
    couple_result = call(
        pair_transition_kernel,
        shape((TOK, COLS, 128)),
        mid,
        couple_expand_matrix,
        couple_shrink_matrix,
        flops=1_000_000_000,
    )
    gates, wf_hi, wf_lo = call(
        gates_kernel,
        [shape((32, 1024)), shape((1024, 256), BF16), shape((1024, 256), BF16)],
        own,
        mixing_switch_matrix,
        mixing_final_matrix.T,
        flops=500_000_000,
    )
    alignment_result = call(
        last_kernel,
        shape((ROWS, TOK, 64)),
        logits,
        values,
        gates,
        wf_hi,
        wf_lo,
        alignment_source,
        alignment_expand_matrix,
        alignment_shrink_matrix.T,
        scratch=[pltpu.VMEM((256, 2048), BF16), pltpu.VMEM((256, 2048), BF16)],
        flops=500_000_000,
    )
    return (alignment_result, couple_result)


def solution(mesh):
    rows, pairs = P("tj", "ti", None), P("ti", "tj", None)
    return jax.shard_map(
        shards,
        mesh=mesh,
        in_specs=(rows, pairs) + (P(),) * 10,
        out_specs=(rows, pairs),
        check_vma=False,
    )
```

time: 116 us -> 55.4 us (0.48)
  matrix products: 27.1 us -> 0 us
  local copies, waits for them, and re-layouts: 26.1 us -> 0.89 us
  Pallas kernels: 0 us -> 15.4 us
  other arithmetic: 9.49 us -> 0 us
  starting transfers between devices: 28.4 us -> 20.4 us
  waiting for transfers between devices: 22.7 us -> 17.3 us
    dot_general x12 -> x0, matrix products: 27.1 us -> none  [the longest x1 9.6 us: pair_block(): jnp.einsum('sia,sjb->ijab', left_block, right_all, precision=exact_arithm...]
    pallas_call x0 -> x8, Pallas kernels: none -> 15.4 us  [call(): pl.pallas_call(kernel, out_shape=outs, in_specs=in_specs, out_specs=[vmem...]
    div x1 -> x0, local copies, waits for them, and re-layouts: 8.95 us -> none  [pair_block(): jnp.einsum('sia,sjb->ijab', left_block, right_all, precision=exact_arithm...]
    all_to_all x5 -> x3, starting transfers between devices: 28.4 us -> 20.4 us  [the longest x1 8.85 us: shards(): factors = exchange(factors, 'tj')]
    unnamed x36 -> x26, local copies, waits for them, and re-layouts: 8.43 us -> 0.89 us
    dot_general x2 -> x0, local copies, waits for them, and re-layouts: 7.02 us -> none  [the longest x1 6.91 us: pair_block(): jnp.dot(flattened, tensor_final_matrix, precision=exact_arithmetic, prefe...]
    all_to_all x5 -> x0, other arithmetic: 5.69 us -> none  [the longest x4 4.74 us: copy_for_each(): lax.all_to_all(jnp.broadcast_to(x[None], (length, *x.shape)), axis, 0, 0,...]
    all_to_all x5 -> x3, waiting for transfers between devices: 22.7 us -> 17.3 us  [the longest x1 8.5 us: shards(): factors = exchange(factors, 'tj')]
  transfers between devices with their start and end apart: 5 -> 3, of which waited for: 5 -> 3; matrix products, arithmetic and copies ran while one was open for 12% -> 0% of each run, Pallas kernels for 0% -> 13%
where the time goes in v1:
time: 55.4 us; the launch traced here: 54.8 us
  starting transfers between devices  20.4 us (37%)
  waiting for transfers between devices  17.3 us (31%)
  Pallas kernels  15.4 us (28%)
  local copies, waits for them, and re-layouts  0.89 us (2%)
  between operations  0.76 us (1%)
    pallas_call x8, Pallas kernels, call(): pl.pallas_call(kernel, out_shape=outs, in_specs=in_specs, out_specs=[vmem...  15.4 us
    all_to_all x1, starting transfers between devices, shards(): factors = exchange(factors, 'tj')  8.85 us
    all_to_all x1, waiting for transfers between devices, shards(): factors = exchange(factors, 'tj')  8.5 us
    all_to_all x1, starting transfers between devices, shards(): tokens = exchange(own, 'ti')  6.92 us
    all_to_all x1, waiting for transfers between devices, shards(): tokens = exchange(own, 'ti')  4.67 us
    all_to_all x1, starting transfers between devices, shards(): logits = exchange(logits, 'tj')  4.62 us
    all_to_all x1, waiting for transfers between devices, shards(): logits = exchange(logits, 'tj')  4.14 us
  transfers between devices with their start and end apart: 3, of which 3 were waited for; matrix products, arithmetic and copies ran while one was open for 0% of the time, Pallas kernels for 13%

profile of v1, /device:TPU:1, one launch (start us, length us, event | category | flops | bytes accessed | tf_op | source)
XLA Modules:
  0.0 54.8 jit_solution(11693655049097891176)
XLA Ops:
  0.6 0.0 copy-start
  0.6 0.8 %copy-done = f32[4,32,64]{2,1,0:T(8,128)S(1)} copy-done((f32[4,32,64]{2,1,0:T(8,128)S(1)}, f32[4,32,64]{2,1,0:T(8,128)}, u32[]{:S(2)}) %copy-start) | copy-done | bytes 32792
  1.5 0.9 %shard_map.131.own_ref = f32[8,64,128]{2,1,0:T(8,128)} custom-call(f32[4,32,64]{2,1,0:T(8,128)S(1)} %copy-done), custom_call_target="tpu_custom_call" | custom-call | bytes 294912 | tf_op jit(solution)/shard_map/pallas_call | solution.py:254
  2.4 0.0 copy-start.11
  2.4 6.9 %all-to-all-start = ((f32[8,64,128]{2,1,0:T(8,128)}), f32[8,64,128]{2,1,0:T(8,128)S(1)}, u32[]{:S(2)}, u32[]{:S(2)}) async-start(f32[8,64,128]{2,1,0:T(8,128)} %shard_map.131.own_ref), calls=%async_computation | async-start | bytes 524288 | tf_op jit(solution)/shard_map/all_to_all | solution.py:286
  9.3 0.0 copy-done.11
  9.4 1.4 %shard_map.132 = (f32[32,128]{1,0:T(8,128)S(1)}, bf16[256,128]{1,0:T(8,128)(2,1)S(1)}, bf16[256,128]{1,0:T(8,128)(2,1)S(1)}) custom-call(f32[8,64,128]{2,1,0:T(8,128)} %shard_map.131.own_ref, f32[64,64]{1,0:T(8,128)S(1)} %copy-done.11), custom_call_target="tpu_custom_call" | custom-call | flops 100000000 | bytes 425984 | tf_op jit(solution)/shard_map/pallas_call | solution.py:254
  10.8 4.7 %all-to-all-done.recv_ref = f32[8,64,128]{2,1,0:T(8,128)S(1)} async-done(((f32[8,64,128]{2,1,0:T(8,128)}), f32[8,64,128]{2,1,0:T(8,128)S(1)}, u32[]{:S(2)}, u32[]{:S(2)}) %all-to-all-start) | async-done | bytes 262176 | tf_op jit(solution)/shard_map/all_to_all | solution.py:286
  15.5 1.0 %shard_map.133 = f32[16,48,128]{2,1,0:T(8,128)} custom-call(f32[8,64,128]{2,1,0:T(8,128)S(1)} %all-to-all-done.recv_ref, f32[32,128]{1,0:T(8,128)S(1)} %get-tuple-element.13.left_ref, bf16[256,128]{1,0:T(8,128)(2,1)S(1)} %get-tuple-element.14.wr_hi_ref, bf16[256,128]{1,0:T(8,128)(2,1)S(1)} %get-tuple-element.15.wr_lo_ref), custom_call_target="tpu_custom_call" | custom-call | bytes 802816 | tf_op jit(solution)/shard_map/pallas_call | solution.py:254
  16.5 0.0 copy-start.4
  16.5 0.0 copy-start.8
  16.5 0.0 copy-start.12
  16.5 8.9 %all-to-all-start.1 = ((f32[16,48,128]{2,1,0:T(8,128)}), f32[16,48,128]{2,1,0:T(8,128)S(1)}, u32[]{:S(2)}, u32[]{:S(2)}) async-start(f32[16,48,128]{2,1,0:T(8,128)} %shard_map.133), calls=%async_computation.1 | async-start | bytes 786432 | tf_op jit(solution)/shard_map/all_to_all | solution.py:295
  25.3 0.0 copy-done.4
  25.3 0.0 copy-done.8
  25.3 0.0 copy-done.12
  25.3 0.0 copy-start.6
  25.4 1.4 %shard_map.134 = (bf16[2048,256]{1,0:T(8,128)(2,1)S(1)}, bf16[1024,256]{1,0:T(8,128)(2,1)S(1)}, bf16[128,256]{1,0:T(8,128)(2,1)S(1)}) custom-call(f32[8,64,128]{2,1,0:T(8,128)S(1)} %all-to-all-done.recv_ref, f32[64,256]{1,0:T(8,128)S(1)} %copy-done.8, f32[1024,128]{1,0:T(8,128)S(1)} %copy-done.4, f32[8,128]{1,0:T(8,128)S(1)} %bitcast.5), custom_call_target="tpu_custom_call" | custom-call | flops 1000000000 | bytes 2494464 | tf_op jit(solution)/shard_map/pallas_call | solution.py:254
  26.7 8.5 %all-to-all-done.1.recv_ref = f32[16,48,128]{2,1,0:T(8,128)S(1)} async-done(((f32[16,48,128]{2,1,0:T(8,128)}), f32[16,48,128]{2,1,0:T(8,128)S(1)}, u32[]{:S(2)}, u32[]{:S(2)}) %all-to-all-start.1) | async-done | bytes 393248 | tf_op jit(solution)/shard_map/all_to_all | solution.py:295
  35.2 0.0 copy-done.6
  35.2 3.0 %shard_map.135 = (f32[16,32,128]{2,1,0:T(8,128)S(1)}, f32[16,32,128]{2,1,0:T(8,128)}) custom-call(f32[16,48,128]{2,1,0:T(8,128)S(1)} %all-to-all-done.1.recv_ref, f32[32,16,128]{2,1,0:T(8,128)S(1)} %copy-done.6, bf16[1024,256]{1,0:T(8,128)(2,1)S(1)} %get-tuple-element.16.t_ref, bf16[128,256]{1,0:T(8,128)(2,1)S(1)} %get-tuple-element.17.score_ref), custom_call_target="tpu_custom_call" | custom-call | flops 2000000000 | bytes 1769472 | tf_op jit(solution)/shard_map/pallas_call | solution.py:254
  38.3 0.0 copy-start.9
  38.3 0.0 copy-start.10
  38.3 4.6 %all-to-all-start.2 = ((f32[16,32,128]{2,1,0:T(8,128)}), f32[16,32,128]{2,1,0:T(8,128)S(1)}, u32[]{:S(2)}, u32[]{:S(2)}) async-start(f32[16,32,128]{2,1,0:T(8,128)} %get-tuple-element.18), calls=%async_computation.2 | async-start | bytes 524288 | tf_op jit(solution)/shard_map/all_to_all | solution.py:315
  42.9 0.0 copy-done.9
  42.9 0.0 copy-done.10
  42.9 0.0 copy-start.5
  42.9 0.0 copy-start.7
  42.9 2.2 %shard_map.136 = (f32[32,1024]{1,0:T(8,128)S(1)}, bf16[1024,256]{1,0:T(8,128)(2,1)S(1)}, bf16[1024,256]{1,0:T(8,128)(2,1)S(1)}) custom-call(f32[8,64,128]{2,1,0:T(8,128)} %shard_map.131.own_ref, f32[64,256]{1,0:T(8,128)S(1)} %copy-done.9, f32[64,256]{1,0:T(8,128)S(1)} %bitcast.4), custom_call_target="tpu_custom_call" | custom-call | flops 500000000 | bytes 1572864 | tf_op jit(solution)/shard_map/pallas_call | solution.py:254
  45.1 0.0 copy-done.5
  45.1 0.0 copy-done.7
  45.1 0.0 copy-start.1
  45.1 0.0 copy-start.2
  45.1 0.0 copy-start.3
  45.1 2.3 %shard_map.138 = f32[32,16,128]{2,1,0:T(8,128)} custom-call(f32[16,32,128]{2,1,0:T(8,128)S(1)} %get-tuple-element.23.mid_ref, f32[128,1024]{1,0:T(8,128)S(1)} %copy-done.5, f32[512,128]{1,0:T(8,128)S(1)} %copy-done.7), custom_call_target="tpu_custom_call" | custom-call | flops 1000000000 | bytes 1310720 | tf_op jit(solution)/shard_map/pallas_call | solution.py:254
  47.5 4.1 %all-to-all-done.2.recv_ref = f32[16,32,128]{2,1,0:T(8,128)S(1)} async-done(((f32[16,32,128]{2,1,0:T(8,128)}), f32[16,32,128]{2,1,0:T(8,128)S(1)}, u32[]{:S(2)}, u32[]{:S(2)}) %all-to-all-start.2) | async-done | bytes 262176 | tf_op jit(solution)/shard_map/all_to_all | solution.py:315
  51.6 0.0 copy-done.1
  51.6 0.0 copy-done.2
  51.6 0.0 copy-done.3
  51.6 3.1 %shard_map.137 = f32[4,32,64]{2,1,0:T(8,128)} custom-call(f32[16,32,128]{2,1,0:T(8,128)S(1)} %all-to-all-done.2.recv_ref, bf16[2048,256]{1,0:T(8,128)(2,1)S(1)} %get-tuple-element.19.v_ref, f32[32,1024]{1,0:T(8,128)S(1)} %get-tuple-element.20.gate_ref, bf16[1024,256]{1,0:T(8,128)(2,1)S(1)} %get-tuple-element.21.wf_hi_ref, ...), custom_call_target="tpu_custom_call" | custom-call | flops 500000000 | bytes 2752512 | tf_op jit(solution)/shard_map/pallas_call | solution.py:254
Async XLA Ops:
  0.6 0.8 %copy-start = (f32[4,32,64]{2,1,0:T(8,128)S(1)}, f32[4,32,64]{2,1,0:T(8,128)}, u32[]{:S(2)}) copy-start(f32[4,32,64]{2,1,0:T(8,128)} %x_ref.3) | copy-start | bytes 98308
  2.4 6.9 %copy-start.11 = (f32[64,64]{1,0:T(8,128)S(1)}, f32[64,64]{1,0:T(8,128)}, u32[]{:S(2)}) copy-start(f32[64,64]{1,0:T(8,128)} %w_ref.1) | copy-start | bytes 49156
  2.4 13.0 %all-to-all-start = ((f32[8,64,128]{2,1,0:T(8,128)}), f32[8,64,128]{2,1,0:T(8,128)S(1)}, u32[]{:S(2)}, u32[]{:S(2)}) async-start(f32[8,64,128]{2,1,0:T(8,128)} %shard_map.131.own_ref), calls=%async_computation | async-start | bytes 524288 | tf_op jit(solution)/shard_map/all_to_all | solution.py:286
  16.5 8.9 %copy-start.4 = (f32[1024,128]{1,0:T(8,128)S(1)}, f32[1024,128]{1,0:T(8,128)}, u32[]{:S(2)}) copy-start(f32[1024,128]{1,0:T(8,128)} %t_ref.1) | copy-start | bytes 1572868
  16.5 8.9 %copy-start.8 = (f32[64,256]{1,0:T(8,128)S(1)}, f32[64,256]{1,0:T(8,128)}, u32[]{:S(2)}) copy-start(f32[64,256]{1,0:T(8,128)} %wv_ref.1) | copy-start | bytes 196612
  16.5 8.9 %copy-start.12 = (f32[128,8]{0,1:T(8,128)S(1)}, f32[128,8]{0,1:T(8,128)}, u32[]{:S(2)}) copy-start(f32[128,8]{0,1:T(8,128)} %param.18) | copy-start | bytes 12292
  16.5 18.7 %all-to-all-start.1 = ((f32[16,48,128]{2,1,0:T(8,128)}), f32[16,48,128]{2,1,0:T(8,128)S(1)}, u32[]{:S(2)}, u32[]{:S(2)}) async-start(f32[16,48,128]{2,1,0:T(8,128)} %shard_map.133), calls=%async_computation.1 | async-start | bytes 786432 | tf_op jit(solution)/shard_map/all_to_all | solution.py:295
  25.3 9.9 %copy-start.6 = (f32[32,16,128]{2,1,0:T(8,128)S(1)}, f32[32,16,128]{2,1,0:T(8,128)}, u32[]{:S(2)}) copy-start(f32[32,16,128]{2,1,0:T(8,128)} %pair_ref.1) | copy-start | bytes 786436
  38.3 4.6 %copy-start.9 = (f32[64,256]{1,0:T(8,128)S(1)}, f32[64,256]{1,0:T(8,128)}, u32[]{:S(2)}) copy-start(f32[64,256]{1,0:T(8,128)} %wg_ref.1) | copy-start | bytes 196612
  38.3 4.6 %copy-start.10 = (f32[256,64]{0,1:T(8,128)S(1)}, f32[256,64]{0,1:T(8,128)}, u32[]{:S(2)}) copy-start(f32[256,64]{0,1:T(8,128)} %param.19) | copy-start | bytes 196612
  38.3 13.3 %all-to-all-start.2 = ((f32[16,32,128]{2,1,0:T(8,128)}), f32[16,32,128]{2,1,0:T(8,128)S(1)}, u32[]{:S(2)}, u32[]{:S(2)}) async-start(f32[16,32,128]{2,1,0:T(8,128)} %get-tuple-element.18), calls=%async_computation.2 | async-start | bytes 524288 | tf_op jit(solution)/shard_map/all_to_all | solution.py:315
  42.9 2.2 %copy-start.5 = (f32[128,1024]{1,0:T(8,128)S(1)}, f32[128,1024]{1,0:T(8,128)}, u32[]{:S(2)}) copy-start(f32[128,1024]{1,0:T(8,128)} %expand_ref.3) | copy-start | bytes 1572868
  42.9 2.2 %copy-start.7 = (f32[512,128]{1,0:T(8,128)S(1)}, f32[512,128]{1,0:T(8,128)}, u32[]{:S(2)}) copy-start(f32[512,128]{1,0:T(8,128)} %shrink_ref.1) | copy-start | bytes 786436
  45.1 6.5 %copy-start.1 = (f32[4,32,64]{2,1,0:T(8,128)S(1)}, f32[4,32,64]{2,1,0:T(8,128)}, u32[]{:S(2)}) copy-start(f32[4,32,64]{2,1,0:T(8,128)} %x_ref.3) | copy-start | bytes 98308
  45.1 6.5 %copy-start.2 = (f32[64,512]{1,0:T(8,128)S(1)}, f32[64,512]{1,0:T(8,128)}, u32[]{:S(2)}) copy-start(f32[64,512]{1,0:T(8,128)} %expand_ref.2) | copy-start | bytes 393220
  45.1 6.5 %copy-start.3 = (f32[256,64]{0,1:T(8,128)S(1)}, f32[256,64]{0,1:T(8,128)}, u32[]{:S(2)}) copy-start(f32[256,64]{0,1:T(8,128)} %param.21) | copy-start | bytes 196612

commit v2 on v1

--- a/solution.py
+++ b/solution.py
@@ -43,27 +43,52 @@
     return centred * lax.rsqrt(var + EPS)
 
 
-def spread_heads(w):
-    n, l = iota((256, 1024), 0), iota((256, 1024), 1)
-    place = (n == (l // 128) * 32 + l % 32).astype(BF16)
-    wide = dot(w, place)
-    tall = jnp.concatenate([wide] * 4, axis=0)
-    keep = iota((256, 1024), 0) // 64 == (iota((256, 1024), 1) // 32) % 4
-    return jnp.where(keep, tall, 0.0)
-
-
-def first_kernel(x_ref, send_ref):
+def head_tiles(w):
+    group = iota((64, 128), 1) // 32
+    tiles = []
+    for half in range(2):
+        part = w[:, half * 128 : half * 128 + 128]
+        turned = [pltpu.roll(part, 32 * d, 1) if d else part for d in range(4)]
+        for q in range(4):
+            tile = turned[(3 - q) % 4]
+            for s in range(3):
+                tile = jnp.where(group == s, turned[(s - q) % 4], tile)
+            tiles.append(tile)
+    return tiles
+
+
+def head_weights(w):
+    group = iota((64, 128), 1) // 32
+    zero = jnp.zeros((64, 128), BF16)
+    out = []
+    for tile in head_tiles(w):
+        out.append(
+            tuple(
+                jnp.concatenate([jnp.where(group == s, part, zero) for s in range(ROWS)], axis=0)
+                for part in split(tile)
+            )
+        )
+    return out
+
+
+def first_kernel(x_ref, send_ref, own_ref):
     x = normed(x_ref[...])
     low = jnp.concatenate([x[0], x[1]], axis=1)
     high = jnp.concatenate([x[2], x[3]], axis=1)
+    own_ref[:, :128] = low
+    own_ref[:, 128:] = high
     for d in range(TI):
         send_ref[d, :TOK, :] = low
         send_ref[d, TOK:, :] = high
 
 
-def left_kernel(own_ref, w_ref, left_ref, wr_hi_ref, wr_lo_ref):
-    x = jnp.concatenate([own_ref[0, :TOK, :], own_ref[0, TOK:, :]], axis=1)
-    xs = split(jnp.concatenate([x] * 4, axis=0))
+def prepare_kernel(
+    own_ref, w_ref, t_ref, score_ref, wg_ref, wf_ref,
+    left_ref, wr_hi_ref, wr_lo_ref, t_out_ref, score_out_ref, gate_ref, wf_hi_ref, wf_lo_ref,
+):
+    x = own_ref[...]
+    one = split(x)
+    xs = tuple(jnp.concatenate([part] * 4, axis=0) for part in one)
     ws = split(w_ref[...])
     pick = (iota((128, 64), 0) // 4 == iota((128, 64), 1)).astype(BF16)
     tile_k = (iota((64, 256), 0) == iota((64, 256), 1) % 64).astype(BF16)
@@ -85,6 +110,24 @@
     for part, ref in zip(ws, (wr_hi_ref, wr_lo_ref)):
         tall = jnp.concatenate([dot(part, tile_b)] * 4, axis=0)
         ref[...] = jnp.where(keep_r, tall, 0.0).astype(BF16)
+    th, tl = split(t_ref[...])
+    t_out_ref[:, :128] = th
+    t_out_ref[:, 128:] = tl
+    score = score_ref[...]
+    tall = jnp.concatenate([jnp.broadcast_to(score[h : h + 1], (16, 128)) for h in range(8)], axis=0)
+    sh, sl = split(tall.T)
+    score_out_ref[:, :128] = sh
+    score_out_ref[:, 128:] = sl
+    for h, wg in enumerate(head_weights(wg_ref[...])):
+        gate_ref[:, h * 128 : h * 128 + 128] = 1.0 / (1.0 + jnp.exp(-dot3(one, wg)))
+    row = iota((32, 256), 1) // 64
+    zero = jnp.zeros((32, 256), BF16)
+    for part, ref in zip(split(wf_ref[...].T), (wf_hi_ref, wf_lo_ref)):
+        wide = dot(part, tile_k).astype(BF16)
+        for h in range(8):
+            for s in range(ROWS):
+                at = h * 128 + s * 32
+                ref[at : at + 32, :] = jnp.where(row == s, wide[h * 32 : h * 32 + 32], zero)
 
 
 def all_tokens(recv_ref):
@@ -104,25 +147,15 @@
         send_ref[d, 32:, :] = right[d * COLS : (d + 1) * COLS]
 
 
-def values_kernel(recv_ref, wv_ref, t_ref, score_ref, v_ref, t_out_ref, score_out_ref):
+def values_kernel(recv_ref, wv_ref, v_ref):
     low, high = all_tokens(recv_ref)
-    wv = [spread_heads(part).astype(BF16) for part in split(wv_ref[...])]
     xs = split(jnp.concatenate([low, high], axis=1))
-    for h in range(8):
-        cols = slice(h * 128, (h + 1) * 128)
-        vh, vl = split(dot3(xs, (wv[0][:, cols], wv[1][:, cols])))
+    for h, wv in enumerate(head_weights(wv_ref[...])):
+        vh, vl = split(dot3(xs, wv))
         for d in range(TJ):
             at = (d * 8 + h) * COLS
             v_ref[at : at + COLS, :128] = vh[d * COLS : (d + 1) * COLS]
             v_ref[at : at + COLS, 128:] = vl[d * COLS : (d + 1) * COLS]
-    th, tl = split(t_ref[...])
-    t_out_ref[:, :128] = th
-    t_out_ref[:, 128:] = tl
-    score = score_ref[...]
-    tall = jnp.concatenate([jnp.broadcast_to(score[h : h + 1], (16, 128)) for h in range(8)], axis=0)
-    sh, sl = split(tall.T)
-    score_out_ref[:, :128] = sh
-    score_out_ref[:, 128:] = sl
 
 
 def pair_kernel(recv_ref, pair_ref, t_ref, score_ref, mid_ref, send_ref, f_hi, f_lo):
@@ -193,15 +226,6 @@
             out_ref[:, at + j, :] = out[j * TOK : (j + 1) * TOK]
 
 
-def gates_kernel(own_ref, wg_ref, wf_ref, gate_ref, wf_hi_ref, wf_lo_ref):
-    x = jnp.concatenate([own_ref[0, :TOK, :], own_ref[0, TOK:, :]], axis=1)
-    wg = tuple(spread_heads(part).astype(BF16) for part in split(wg_ref[...]))
-    logit = dot3(split(x), wg)
-    gate_ref[...] = 1.0 / (1.0 + jnp.exp(-logit))
-    for part, ref in zip(split(wf_ref[...]), (wf_hi_ref, wf_lo_ref)):
-        ref[...] = spread_heads(part).T.astype(BF16)
-
-
 def group_all(x, op):
     lane = iota(x.shape, 1)
     for d in (8, 4, 2, 1):
@@ -225,13 +249,20 @@
     head = iota((TOK, 128), 1) // 16
     zero = jnp.zeros((TOK, 128), BF16)
     for d in range(TJ):
-        wh, wl = split(terms[d] * inv)
+        wh, wl = split(terms[d])
         for h in range(8):
             w_hi[h * TOK : (h + 1) * TOK, d * 128 : d * 128 + 128] = jnp.where(head == h, wh, zero)
             w_lo[h * TOK : (h + 1) * TOK, d * 128 : d * 128 + 128] = jnp.where(head == h, wl, zero)
     wide = dot(w_hi[...], v_ref[...])
     mixed = wide[:, :128] + wide[:, 128:] + dot(w_lo[...], v_ref[:, :128])
-    gated = gate_ref[...] * jnp.concatenate([mixed[h * TOK : (h + 1) * TOK] for h in range(8)], axis=1)
+    gated = jnp.concatenate(
+        [
+            mixed[h * TOK : (h + 1) * TOK]
+            * (gate_ref[:, h * 128 : h * 128 + 128] * inv[:, h * 16 : h * 16 + 1])
+            for h in range(8)
+        ],
+        axis=1,
+    )
     update = dot3(split(gated), (wf_hi_ref[...], wf_lo_ref[...]))
     mid = jnp.concatenate(
         [x_ref[s] + update[:, s * 64 : (s + 1) * 64] for s in range(ROWS)], axis=0
@@ -282,26 +313,24 @@
     couple_shrink_matrix,
 ):
     exchange = functools.partial(lax.all_to_all, split_axis=0, concat_axis=0, tiled=True)
-    own = call(first_kernel, shape((TI, 64, 128)), alignment_source)
-    tokens = exchange(own, "ti")
-    left, wr_hi, wr_lo = call(
-        left_kernel,
-        [shape((32, 128)), shape((256, 128), BF16), shape((256, 128), BF16)],
+    send, own = call(first_kernel, [shape((TI, 64, 128)), shape((TOK, 256))], alignment_source)
+    tokens = exchange(send, "ti")
+    prepared = call(
+        prepare_kernel,
+        [shape((32, 128)), shape((256, 128), BF16), shape((256, 128), BF16)]
+        + [shape((1024, 256), BF16), shape((128, 256), BF16), shape((32, 1024))]
+        + [shape((1024, 256), BF16), shape((1024, 256), BF16)],
         own,
         tensor_operand_matrix,
-        flops=100_000_000,
-    )
+        tensor_final_matrix,
+        mixing_score_matrix.T,
+        mixing_switch_matrix,
+        mixing_final_matrix.T,
+        flops=500_000_000,
+    )
+    left, wr_hi, wr_lo, final2, score2, gates, wf_hi, wf_lo = prepared
     factors = call(right_kernel, shape((TJ, 48, 128)), tokens, left, wr_hi, wr_lo)
     factors = exchange(factors, "tj")
-    values, final2, score2 = call(
-        values_kernel,
-        [shape((2048, 256), BF16), shape((1024, 256), BF16), shape((128, 256), BF16)],
-        tokens,
-        mixing_content_matrix,
-        tensor_final_matrix,
-        mixing_score_matrix.T,
-        flops=1_000_000_000,
-    )
     mid, logits = call(
         pair_kernel,
         [shape((COLS, TOK, 128)), shape((TJ, TOK, 128))],
@@ -312,6 +341,7 @@
         scratch=[pltpu.VMEM((512, 1024), BF16), pltpu.VMEM((512, 1024), BF16)],
         flops=2_000_000_000,
     )
+    mid, tokens = lax.optimization_barrier((mid, tokens))
     logits = exchange(logits, "tj")
     couple_result = call(
         pair_transition_kernel,
@@ -321,13 +351,8 @@
         couple_shrink_matrix,
         flops=1_000_000_000,
     )
-    gates, wf_hi, wf_lo = call(
-        gates_kernel,
-        [shape((32, 1024)), shape((1024, 256), BF16), shape((1024, 256), BF16)],
-        own,
-        mixing_switch_matrix,
-        mixing_final_matrix.T,
-        flops=500_000_000,
+    values = call(
+        values_kernel, shape((2048, 256), BF16), tokens, mixing_content_matrix, flops=1_000_000_000
     )
     alignment_result = call(
         last_kernel,

time: 55.4 us -> 54.1 us (0.977)
  blocking collectives: 0 us -> 18.5 us
  waiting for transfers between devices: 17.3 us -> 8.27 us
  starting transfers between devices: 20.4 us -> 11.5 us
  Pallas kernels: 15.4 us -> 11.3 us
  local copies, waits for them, and re-layouts: 0.89 us -> 3.15 us
    all_to_all x0 -> x1, blocking collectives: none -> 18.5 us  [shards(): factors = exchange(factors, 'tj')]
    all_to_all x2 -> x1, waiting for transfers between devices: 13.2 us -> 3.01 us  [shards(): tokens = exchange(send, 'ti')]
    all_to_all x2 -> x1, starting transfers between devices: 15.8 us -> 6.92 us  [shards(): tokens = exchange(send, 'ti')]
    pallas_call x8 -> x7, Pallas kernels: 15.4 us -> 11.3 us  [call(): pl.pallas_call(kernel, out_shape=outs, in_specs=in_specs, out_specs=[vmem...]
    unnamed x26, local copies, waits for them, and re-layouts: 0.89 us -> 3.15 us
    all_to_all x1, waiting for transfers between devices: 4.14 us -> 5.26 us  [shards(): logits = exchange(logits, 'tj')]
  transfers between devices with their start and end apart: 3 -> 2, of which waited for: 3 -> 2; matrix products, arithmetic and copies ran while one was open for 0% -> 0% of each run, Pallas kernels for 13% -> 8%
where the time goes in v2:
time: 54.1 us; the launch traced here: 53.5 us
  blocking collectives  18.5 us (34%)
  starting transfers between devices  11.5 us (21%)
  Pallas kernels  11.3 us (21%)
  waiting for transfers between devices  8.27 us (15%)
  local copies, waits for them, and re-layouts  3.15 us (6%)
  between operations  0.75 us (1%)
    all_to_all x1, blocking collectives, shards(): factors = exchange(factors, 'tj')  18.5 us
    pallas_call x7, Pallas kernels, call(): pl.pallas_call(kernel, out_shape=outs, in_specs=in_specs, out_specs=[vmem...  11.3 us
    all_to_all x1, starting transfers between devices, shards(): tokens = exchange(send, 'ti')  6.92 us
    all_to_all x1, waiting for transfers between devices, shards(): logits = exchange(logits, 'tj')  5.26 us
    all_to_all x1, starting transfers between devices, shards(): logits = exchange(logits, 'tj')  4.61 us
    unnamed x26, local copies, waits for them, and re-layouts  3.15 us
    all_to_all x1, waiting for transfers between devices, shards(): tokens = exchange(send, 'ti')  3.01 us
  transfers between devices with their start and end apart: 2, of which 2 were waited for; matrix products, arithmetic and copies ran while one was open for 0% of the time, Pallas kernels for 8%

profile of v2, /device:TPU:1, one launch (start us, length us, event | category | flops | bytes accessed | tf_op | source)
XLA Modules:
  0.0 53.5 jit_solution(10607882025636404622)
XLA Ops:
  0.6 0.0 copy-start
  0.6 0.8 %copy-done = f32[4,32,64]{2,1,0:T(8,128)S(1)} copy-done((f32[4,32,64]{2,1,0:T(8,128)S(1)}, f32[4,32,64]{2,1,0:T(8,128)}, u32[]{:S(2)}) %copy-start) | copy-done | bytes 32792
  1.5 0.0 copy-start.4
  1.5 1.0 %shard_map.131 = (f32[8,64,128]{2,1,0:T(8,128)}, f32[32,256]{1,0:T(8,128)S(1)}) custom-call(f32[4,32,64]{2,1,0:T(8,128)S(1)} %copy-done), custom_call_target="tpu_custom_call" | custom-call | bytes 327680 | tf_op jit(solution)/shard_map/pallas_call | solution.py:285
  2.4 0.0 copy-start.8
  2.4 6.9 %all-to-all-start = ((f32[8,64,128]{2,1,0:T(8,128)}), f32[8,64,128]{2,1,0:T(8,128)S(1)}, u32[]{:S(2)}, u32[]{:S(2)}) async-start(f32[8,64,128]{2,1,0:T(8,128)} %get-tuple-element.16), calls=%async_computation | async-start | bytes 524288 | tf_op jit(solution)/shard_map/all_to_all | solution.py:317
  9.4 0.0 copy-start.12
  9.4 0.0 copy-done.4
  9.4 0.0 copy-done.8
  9.4 0.7 %copy-done.12 = f32[128,8]{0,1:T(8,128)S(1)} copy-done((f32[128,8]{0,1:T(8,128)S(1)}, f32[128,8]{0,1:T(8,128)}, u32[]{:S(2)}) %copy-start.12) | copy-done | bytes 4120
  10.0 0.0 copy-start.9
  10.0 0.8 %copy-done.9 = f32[256,64]{0,1:T(8,128)S(1)} copy-done((f32[256,64]{0,1:T(8,128)S(1)}, f32[256,64]{0,1:T(8,128)}, u32[]{:S(2)}) %copy-start.9) | copy-done | bytes 65560
  10.9 0.0 copy-start.11
  10.9 0.8 %copy-done.11 = f32[64,64]{1,0:T(8,128)S(1)} copy-done((f32[64,64]{1,0:T(8,128)S(1)}, f32[64,64]{1,0:T(8,128)}, u32[]{:S(2)}) %copy-start.11) | copy-done | bytes 16408
  11.6 0.8 %shard_map.132 = (f32[32,128]{1,0:T(8,128)S(1)}, bf16[256,128]{1,0:T(8,128)(2,1)S(1)}, bf16[256,128]{1,0:T(8,128)(2,1)S(1)}, bf16[1024,256]{1,0:T(8,128)(2,1)S(1...) custom-call(f32[32,256]{1,0:T(8,128)S(1)} %get-tuple-element.17.own_, ...), custom_call_target="tpu_custom_call" | custom-call | flops 500000000 | bytes 2625536 | tf_op jit(solution)/shard_map/pallas_call | solution.py:285
  12.4 3.0 %all-to-all-done.recv_ref = f32[8,64,128]{2,1,0:T(8,128)S(1)} async-done(((f32[8,64,128]{2,1,0:T(8,128)}), f32[8,64,128]{2,1,0:T(8,128)S(1)}, u32[]{:S(2)}, u32[]{:S(2)}) %all-to-all-start) | async-done | bytes 262176 | tf_op jit(solution)/shard_map/all_to_all | solution.py:317
  15.5 0.3 shard_map.133
  15.7 0.0 copy-start.6
  15.7 18.5 %all_to_all.15.recv_ref = f32[16,48,128]{2,1,0:T(8,128)S(1)} all-to-all(f32[16,48,128]{2,1,0:T(8,128)S(1)} %shard_map.133), channel_id=1, replica_groups=mesh['ti'=8,'tj'=16] {'tj'}, dimensions={0} | all-to-all | bytes 786432 | tf_op jit(solution)/shard_map/all_to_all | solution.py:333
  34.3 0.0 copy-done.6
  34.3 3.0 %shard_map.134 = (f32[16,32,128]{2,1,0:T(8,128)S(1)}, f32[16,32,128]{2,1,0:T(8,128)}) custom-call(f32[16,48,128]{2,1,0:T(8,128)S(1)} %all_to_all.15.recv_ref, f32[32,16,128]{2,1,0:T(8,128)S(1)} %copy-done.6, bf16[1024,256]{1,0:T(8,128)(2,1)S(1)} %get-tuple-element.21.t_ref, bf16[128,256]{1,0:T(8,128)(2,1)S(1)} %get-tuple-element.22.score_ref), custom_call_target="tpu_custom_call" | custom-call | flops 2000000000 | bytes 1769472 | tf_op jit(solution)/shard_map/pallas_call | solution.py:285
  37.3 0.0 copy-start.10
  37.3 4.6 %all-to-all-start.2 = ((f32[16,32,128]{2,1,0:T(8,128)}), f32[16,32,128]{2,1,0:T(8,128)S(1)}, u32[]{:S(2)}, u32[]{:S(2)}) async-start(f32[16,32,128]{2,1,0:T(8,128)} %get-tuple-element.23), calls=%async_computation.2 | async-start | bytes 524288 | tf_op jit(solution)/shard_map/all_to_all | solution.py:345
  41.9 0.0 copy-done.10
  41.9 0.0 copy-start.5
  41.9 0.0 copy-start.7
  41.9 1.1 %shard_map.135.v_ref = bf16[2048,256]{1,0:T(8,128)(2,1)S(1)} custom-call(f32[8,64,128]{2,1,0:T(8,128)S(1)} %all-to-all-done.recv_ref, f32[64,256]{1,0:T(8,128)S(1)} %copy-done.10), custom_call_target="tpu_custom_call" | custom-call | flops 1000000000 | bytes 1376256 | tf_op jit(solution)/shard_map/pallas_call | solution.py:285
  43.0 0.0 copy-done.5
  43.0 0.0 copy-done.7
  43.0 0.0 copy-start.1
  43.0 0.0 copy-start.2
  43.1 0.0 copy-start.3
  43.1 2.3 %shard_map.137 = f32[32,16,128]{2,1,0:T(8,128)} custom-call(f32[16,32,128]{2,1,0:T(8,128)S(1)} %get-tuple-element.29.mid_ref, f32[128,1024]{1,0:T(8,128)S(1)} %copy-done.5, f32[512,128]{1,0:T(8,128)S(1)} %copy-done.7), custom_call_target="tpu_custom_call" | custom-call | flops 1000000000 | bytes 1310720 | tf_op jit(solution)/shard_map/pallas_call | solution.py:285
  45.4 5.3 %all-to-all-done.2.recv_ref = f32[16,32,128]{2,1,0:T(8,128)S(1)} async-done(((f32[16,32,128]{2,1,0:T(8,128)}), f32[16,32,128]{2,1,0:T(8,128)S(1)}, u32[]{:S(2)}, u32[]{:S(2)}) %all-to-all-start.2) | async-done | bytes 262176 | tf_op jit(solution)/shard_map/all_to_all | solution.py:345
  50.7 0.0 copy-done.1
  50.7 0.0 copy-done.2
  50.7 0.0 copy-done.3
  50.7 2.8 %shard_map.136 = f32[4,32,64]{2,1,0:T(8,128)} custom-call(f32[16,32,128]{2,1,0:T(8,128)S(1)} %all-to-all-done.2.recv_ref, bf16[2048,256]{1,0:T(8,128)(2,1)S(1)} %shard_map.135.v_ref, f32[32,1024]{1,0:T(8,128)S(1)} %get-tuple-element.26.gate_ref, bf16[1024,256]{1,0:T(8,128)(2,1)S(1)} %get-tuple-element.27.wf_hi_ref, ...), custom_call_target="tpu_custom_call" | custom-call | flops 500000000 | bytes 2752512 | tf_op jit(solution)/shard_map/pallas_call | solution.py:285
Async XLA Ops:
  0.6 0.8 %copy-start = (f32[4,32,64]{2,1,0:T(8,128)S(1)}, f32[4,32,64]{2,1,0:T(8,128)}, u32[]{:S(2)}) copy-start(f32[4,32,64]{2,1,0:T(8,128)} %x_ref.3) | copy-start | bytes 98308
  1.5 7.9 %copy-start.4 = (f32[1024,128]{1,0:T(8,128)S(1)}, f32[1024,128]{1,0:T(8,128)}, u32[]{:S(2)}) copy-start(f32[1024,128]{1,0:T(8,128)} %t_ref.1) | copy-start | bytes 1572868
  2.4 6.9 %copy-start.8 = (f32[64,256]{1,0:T(8,128)S(1)}, f32[64,256]{1,0:T(8,128)}, u32[]{:S(2)}) copy-start(f32[64,256]{1,0:T(8,128)} %wg_ref.1) | copy-start | bytes 196612
  2.4 13.0 %all-to-all-start = ((f32[8,64,128]{2,1,0:T(8,128)}), f32[8,64,128]{2,1,0:T(8,128)S(1)}, u32[]{:S(2)}, u32[]{:S(2)}) async-start(f32[8,64,128]{2,1,0:T(8,128)} %get-tuple-element.16), calls=%async_computation | async-start | bytes 524288 | tf_op jit(solution)/shard_map/all_to_all | solution.py:317
  9.4 0.7 %copy-start.12 = (f32[128,8]{0,1:T(8,128)S(1)}, f32[128,8]{0,1:T(8,128)}, u32[]{:S(2)}) copy-start(f32[128,8]{0,1:T(8,128)} %param.18) | copy-start | bytes 12292
  10.0 0.8 %copy-start.9 = (f32[256,64]{0,1:T(8,128)S(1)}, f32[256,64]{0,1:T(8,128)}, u32[]{:S(2)}) copy-start(f32[256,64]{0,1:T(8,128)} %param.19) | copy-start | bytes 196612
  10.9 0.8 %copy-start.11 = (f32[64,64]{1,0:T(8,128)S(1)}, f32[64,64]{1,0:T(8,128)}, u32[]{:S(2)}) copy-start(f32[64,64]{1,0:T(8,128)} %w_ref.1) | copy-start | bytes 49156
  15.7 18.6 %copy-start.6 = (f32[32,16,128]{2,1,0:T(8,128)S(1)}, f32[32,16,128]{2,1,0:T(8,128)}, u32[]{:S(2)}) copy-start(f32[32,16,128]{2,1,0:T(8,128)} %pair_ref.1) | copy-start | bytes 786436
  37.3 4.6 %copy-start.10 = (f32[64,256]{1,0:T(8,128)S(1)}, f32[64,256]{1,0:T(8,128)}, u32[]{:S(2)}) copy-start(f32[64,256]{1,0:T(8,128)} %wv_ref.1) | copy-start | bytes 196612
  37.3 13.3 %all-to-all-start.2 = ((f32[16,32,128]{2,1,0:T(8,128)}), f32[16,32,128]{2,1,0:T(8,128)S(1)}, u32[]{:S(2)}, u32[]{:S(2)}) async-start(f32[16,32,128]{2,1,0:T(8,128)} %get-tuple-element.23), calls=%async_computation.2 | async-start | bytes 524288 | tf_op jit(solution)/shard_map/all_to_all | solution.py:345
  41.9 1.1 %copy-start.5 = (f32[128,1024]{1,0:T(8,128)S(1)}, f32[128,1024]{1,0:T(8,128)}, u32[]{:S(2)}) copy-start(f32[128,1024]{1,0:T(8,128)} %expand_ref.3) | copy-start | bytes 1572868
  41.9 1.1 %copy-start.7 = (f32[512,128]{1,0:T(8,128)S(1)}, f32[512,128]{1,0:T(8,128)}, u32[]{:S(2)}) copy-start(f32[512,128]{1,0:T(8,128)} %shrink_ref.1) | copy-start | bytes 786436
  43.0 7.6 %copy-start.1 = (f32[4,32,64]{2,1,0:T(8,128)S(1)}, f32[4,32,64]{2,1,0:T(8,128)}, u32[]{:S(2)}) copy-start(f32[4,32,64]{2,1,0:T(8,128)} %x_ref.3) | copy-start | bytes 98308
  43.0 7.6 %copy-start.2 = (f32[64,512]{1,0:T(8,128)S(1)}, f32[64,512]{1,0:T(8,128)}, u32[]{:S(2)}) copy-start(f32[64,512]{1,0:T(8,128)} %expand_ref.2) | copy-start | bytes 393220
  43.1 7.6 %copy-start.3 = (f32[256,64]{0,1:T(8,128)S(1)}, f32[256,64]{0,1:T(8,128)}, u32[]{:S(2)}) copy-start(f32[256,64]{0,1:T(8,128)} %param.21) | copy-start | bytes 196612

commit v3 on v2

--- a/solution.py
+++ b/solution.py
@@ -83,8 +83,8 @@
 
 
 def prepare_kernel(
-    own_ref, w_ref, t_ref, score_ref, wg_ref, wf_ref,
-    left_ref, wr_hi_ref, wr_lo_ref, t_out_ref, score_out_ref, gate_ref, wf_hi_ref, wf_lo_ref,
+    own_ref, w_ref, t_ref, score_ref, wg_ref,
+    left_ref, wr_hi_ref, wr_lo_ref, t_out_ref, score_out_ref, gate_ref,
 ):
     x = own_ref[...]
     one = split(x)
@@ -120,14 +120,6 @@
     score_out_ref[:, 128:] = sl
     for h, wg in enumerate(head_weights(wg_ref[...])):
         gate_ref[:, h * 128 : h * 128 + 128] = 1.0 / (1.0 + jnp.exp(-dot3(one, wg)))
-    row = iota((32, 256), 1) // 64
-    zero = jnp.zeros((32, 256), BF16)
-    for part, ref in zip(split(wf_ref[...].T), (wf_hi_ref, wf_lo_ref)):
-        wide = dot(part, tile_k).astype(BF16)
-        for h in range(8):
-            for s in range(ROWS):
-                at = h * 128 + s * 32
-                ref[at : at + 32, :] = jnp.where(row == s, wide[h * 32 : h * 32 + 32], zero)
 
 
 def all_tokens(recv_ref):
@@ -158,7 +150,7 @@
             v_ref[at : at + COLS, 128:] = vl[d * COLS : (d + 1) * COLS]
 
 
-def pair_kernel(recv_ref, pair_ref, t_ref, score_ref, mid_ref, send_ref, f_hi, f_lo):
+def pair_kernel(recv_ref, pair_ref, t_ref, score_ref, mid_ref, send_ref):
     rows = [
         jnp.concatenate([recv_ref[:, r, :], recv_ref[:, 16 + r, :]], axis=1) for r in range(16)
     ]
@@ -167,6 +159,9 @@
     left3 = jnp.concatenate([lh, lh, ll], axis=1)
     group = iota((16, 128), 1) // 32
     zero = jnp.zeros((16, 128), BF16)
+    column = iota((TOK, 128), 1) % 16
+    tile = jnp.zeros((TOK, 128), F32)
+    fh, fl = [], []
     for pair in range(COLS // 2):
         blocks = []
         for j in (2 * pair, 2 * pair + 1):
@@ -184,13 +179,14 @@
         outer = dot(left3, jnp.concatenate(blocks, axis=1))
         oh, ol = split(outer)
         for q in range(2):
-            at = (2 * pair + q) * TOK
-            for g in range(8):
-                take = (slice(g * 32, g * 32 + 32), slice(q * 128, q * 128 + 128))
-                f_hi[at : at + TOK, g * 128 : g * 128 + 128] = oh[take]
-                f_lo[at : at + TOK, g * 128 : g * 128 + 128] = ol[take]
-    wide = dot(f_hi[...], t_ref[...])
-    update = wide[:, :128] + wide[:, 128:] + dot(f_lo[...], t_ref[:, :128])
+            for part, keep in ((oh, fh), (ol, fl)):
+                keep.append(
+                    jnp.concatenate(
+                        [part[g * 32 : g * 32 + 32, q * 128 : q * 128 + 128] for g in range(8)], axis=1
+                    )
+                )
+    wide = dot(jnp.concatenate(fh, axis=0), t_ref[...])
+    update = wide[:, :128] + wide[:, 128:] + dot(jnp.concatenate(fl, axis=0), t_ref[:, :128])
     normal = []
     for j in range(COLS):
         mid = pair_ref[:, j, :] + update[j * TOK : (j + 1) * TOK]
@@ -199,8 +195,6 @@
     nh, nl = split(jnp.concatenate(normal, axis=0))
     wide = dot(nh, score_ref[...])
     logits = wide[:, :128] + wide[:, 128:] + dot(nl, score_ref[:, :128])
-    column = iota((TOK, 128), 1) % 16
-    tile = jnp.zeros((TOK, 128), F32)
     for j in range(COLS):
         tile = jnp.where(column == j, logits[j * TOK : (j + 1) * TOK], tile)
     for d in range(TJ):
@@ -234,8 +228,27 @@
     return x
 
 
+def three(a, b):
+    (ah, al), (bh, bl) = a, b
+    return dot(jnp.concatenate([ah, ah, al], axis=1), jnp.concatenate([bh, bl, bh], axis=1), NT)
+
+
+def swap_groups(tiles):
+    group = iota(tiles[0].shape, 1) // 32
+    for d in (2, 1):
+        low = (group & d) == 0
+        out = list(tiles)
+        for t in range(4):
+            if t & d == 0:
+                a, b = tiles[t], tiles[t | d]
+                out[t] = jnp.where(low, a, pltpu.roll(b, 32 * d, 1))
+                out[t | d] = jnp.where(low, pltpu.roll(a, 128 - 32 * d, 1), b)
+        tiles = out
+    return tiles
+
+
 def last_kernel(
-    recv_ref, v_ref, gate_ref, wf_hi_ref, wf_lo_ref, x_ref, expand_ref, shrink_ref, out_ref, w_hi, w_lo
+    recv_ref, v_ref, gate_ref, wf_ref, x_ref, expand_ref, shrink_ref, out_ref, w_hi, w_lo
 ):
     top = recv_ref[0]
     for d in range(1, TJ):
@@ -255,22 +268,26 @@
             w_lo[h * TOK : (h + 1) * TOK, d * 128 : d * 128 + 128] = jnp.where(head == h, wl, zero)
     wide = dot(w_hi[...], v_ref[...])
     mixed = wide[:, :128] + wide[:, 128:] + dot(w_lo[...], v_ref[:, :128])
-    gated = jnp.concatenate(
-        [
-            mixed[h * TOK : (h + 1) * TOK]
-            * (gate_ref[:, h * 128 : h * 128 + 128] * inv[:, h * 16 : h * 16 + 1])
-            for h in range(8)
-        ],
-        axis=1,
-    )
-    update = dot3(split(gated), (wf_hi_ref[...], wf_lo_ref[...]))
-    mid = jnp.concatenate(
-        [x_ref[s] + update[:, s * 64 : (s + 1) * 64] for s in range(ROWS)], axis=0
-    )
-    hidden = dot3(split(normed(mid)), split(expand_ref[...]))
+    gated = [
+        mixed[h * TOK : (h + 1) * TOK]
+        * (gate_ref[:, h * 128 : h * 128 + 128] * inv[:, h * 16 : h * 16 + 1])
+        for h in range(8)
+    ]
+    halves = [swap_groups(gated[:4]), swap_groups(gated[4:])]
+    rows = jnp.concatenate(
+        [jnp.concatenate([halves[0][s], halves[1][s]], axis=1) for s in range(ROWS)], axis=0
+    )
+    mid = x_ref[...].reshape(ROWS * TOK, 64) + three(split(rows), split(wf_ref[...]))
+    nh, nl = split(normed(mid))
+    eh, el = split(expand_ref[...])
+    hidden = dot(jnp.concatenate([nh, nl, nh], axis=1), jnp.concatenate([eh, eh, el], axis=0))
     gate = hidden[:, :256]
     act = gate / (1.0 + jnp.exp(-gate)) * hidden[:, 256:]
-    out = mid + dot3(split(act), split(shrink_ref[...]), NT)
+    ah, al = split(act)
+    sh, sl = split(shrink_ref[...])
+    out = mid + dot(
+        jnp.concatenate([ah, ah, al], axis=1), jnp.concatenate([sh, sl, sh], axis=1), NT
+    )
     out_ref[...] = out.reshape(ROWS, TOK, 64)
 
 
@@ -318,17 +335,15 @@
     prepared = call(
         prepare_kernel,
         [shape((32, 128)), shape((256, 128), BF16), shape((256, 128), BF16)]
-        + [shape((1024, 256), BF16), shape((128, 256), BF16), shape((32, 1024))]
-        + [shape((1024, 256), BF16), shape((1024, 256), BF16)],
+        + [shape((1024, 256), BF16), shape((128, 256), BF16), shape((32, 1024))],
         own,
         tensor_operand_matrix,
         tensor_final_matrix,
         mixing_score_matrix.T,
         mixing_switch_matrix,
-        mixing_final_matrix.T,
         flops=500_000_000,
     )
-    left, wr_hi, wr_lo, final2, score2, gates, wf_hi, wf_lo = prepared
+    left, wr_hi, wr_lo, final2, score2, gates = prepared
     factors = call(right_kernel, shape((TJ, 48, 128)), tokens, left, wr_hi, wr_lo)
     factors = exchange(factors, "tj")
     mid, logits = call(
@@ -338,7 +353,6 @@
         couple_source,
         final2,
         score2,
-        scratch=[pltpu.VMEM((512, 1024), BF16), pltpu.VMEM((512, 1024), BF16)],
         flops=2_000_000_000,
     )
     mid, tokens = lax.optimization_barrier((mid, tokens))
@@ -360,8 +374,7 @@
         logits,
         values,
         gates,
-        wf_hi,
-        wf_lo,
+        mixing_final_matrix.T,
         alignment_source,
         alignment_expand_matrix,
         alignment_shrink_matrix.T,

time: 54.1 us -> 53.7 us (level)
  waiting for transfers between devices: 8.27 us -> 9.81 us
  local copies, waits for them, and re-layouts: 3.15 us -> 1.65 us
    all_to_all x1, waiting for transfers between devices: 3.01 us -> 4.57 us  [shards(): tokens = exchange(send, 'ti')]
    unnamed x26, local copies, waits for them, and re-layouts: 3.15 us -> 1.65 us
where the time goes in v3:
time: 53.7 us; the launch traced here: 53.1 us
  blocking collectives  18.5 us (34%)
  starting transfers between devices  11.5 us (21%)
  Pallas kernels  10.8 us (20%)
  waiting for transfers between devices  9.81 us (18%)
  local copies, waits for them, and re-layouts  1.65 us (3%)
  between operations  0.78 us (1%)
    all_to_all x1, blocking collectives, shards(): factors = exchange(factors, 'tj')  18.5 us
    pallas_call x7, Pallas kernels, call(): pl.pallas_call(kernel, out_shape=outs, in_specs=in_specs, out_specs=[vmem...  10.8 us
    all_to_all x1, starting transfers between devices, shards(): tokens = exchange(send, 'ti')  6.92 us
    all_to_all x1, waiting for transfers between devices, shards(): logits = exchange(logits, 'tj')  5.24 us
    all_to_all x1, starting transfers between devices, shards(): logits = exchange(logits, 'tj')  4.62 us
    all_to_all x1, waiting for transfers between devices, shards(): tokens = exchange(send, 'ti')  4.57 us
    unnamed x26, local copies, waits for them, and re-layouts  1.65 us
  transfers between devices with their start and end apart: 2, of which 2 were waited for; matrix products, arithmetic and copies ran while one was open for 0% of the time, Pallas kernels for 8%

profile of v3, /device:TPU:1, one launch (start us, length us, event | category | flops | bytes accessed | tf_op | source)
XLA Modules:
  0.0 53.1 jit_solution(12574678364397619589)
XLA Ops:
  0.6 0.0 copy-start
  0.6 0.8 %copy-done = f32[4,32,64]{2,1,0:T(8,128)S(1)} copy-done((f32[4,32,64]{2,1,0:T(8,128)S(1)}, f32[4,32,64]{2,1,0:T(8,128)}, u32[]{:S(2)}) %copy-start) | copy-done | bytes 32792
  1.5 0.0 copy-start.2
  1.5 1.0 %shard_map.131 = (f32[8,64,128]{2,1,0:T(8,128)}, f32[32,256]{1,0:T(8,128)S(1)}) custom-call(f32[4,32,64]{2,1,0:T(8,128)S(1)} %copy-done), custom_call_target="tpu_custom_call" | custom-call | bytes 327680 | tf_op jit(solution)/shard_map/pallas_call | solution.py:302
  2.4 0.0 copy-start.7
  2.4 0.0 copy-start.12
  2.4 6.9 %all-to-all-start = ((f32[8,64,128]{2,1,0:T(8,128)}), f32[8,64,128]{2,1,0:T(8,128)S(1)}, u32[]{:S(2)}, u32[]{:S(2)}) async-start(f32[8,64,128]{2,1,0:T(8,128)} %get-tuple-element.14), calls=%async_computation | async-start | bytes 524288 | tf_op jit(solution)/shard_map/all_to_all | solution.py:334
  9.4 0.0 copy-done.2
  9.4 0.0 copy-done.7
  9.4 0.0 copy-done.12
  9.4 0.0 copy-start.11
  9.4 0.7 %copy-done.11 = f32[64,64]{1,0:T(8,128)S(1)} copy-done((f32[64,64]{1,0:T(8,128)S(1)}, f32[64,64]{1,0:T(8,128)}, u32[]{:S(2)}) %copy-start.11) | copy-done | bytes 16408
  10.1 0.7 %shard_map.132 = (f32[32,128]{1,0:T(8,128)S(1)}, bf16[256,128]{1,0:T(8,128)(2,1)S(1)}, bf16[256,128]{1,0:T(8,128)(2,1)S(1)}, bf16[1024,256]{1,0:T(8,128)(2,1)S(1...) custom-call(f32[32,256]{1,0:T(8,128)S(1)} %get-tuple-element.15.own_ref, f32[64,64]{1,0:T(8,128)S(1)} %copy-done.11, ...), custom_call_target="tpu_custom_call" | custom-call | flops 500000000 | bytes 1511424 | tf_op jit(solution)/shard_map/pallas_call | solution.py:302
  10.9 4.6 %all-to-all-done.recv_ref = f32[8,64,128]{2,1,0:T(8,128)S(1)} async-done(((f32[8,64,128]{2,1,0:T(8,128)}), f32[8,64,128]{2,1,0:T(8,128)S(1)}, u32[]{:S(2)}, u32[]{:S(2)}) %all-to-all-start) | async-done | bytes 262176 | tf_op jit(solution)/shard_map/all_to_all | solution.py:334
  15.5 0.3 shard_map.133
  15.7 0.0 copy-start.4
  15.7 18.5 %all_to_all.15.recv_ref = f32[16,48,128]{2,1,0:T(8,128)S(1)} all-to-all(f32[16,48,128]{2,1,0:T(8,128)S(1)} %shard_map.133), channel_id=1, replica_groups=mesh['ti'=8,'tj'=16] {'tj'}, dimensions={0} | all-to-all | bytes 786432 | tf_op jit(solution)/shard_map/all_to_all | solution.py:348
  34.3 0.0 copy-done.4
  34.3 2.9 %shard_map.134 = (f32[16,32,128]{2,1,0:T(8,128)S(1)}, f32[16,32,128]{2,1,0:T(8,128)}) custom-call(f32[16,48,128]{2,1,0:T(8,128)S(1)} %all_to_all.15.recv_ref, f32[32,16,128]{2,1,0:T(8,128)S(1)} %copy-done.4, bf16[1024,256]{1,0:T(8,128)(2,1)S(1)} %get-tuple-element.19.t_ref, bf16[128,256]{1,0:T(8,128)(2,1)S(1)} %get-tuple-element.20.score_ref), custom_call_target="tpu_custom_call" | custom-call | flops 2000000000 | bytes 1769472 | tf_op jit(solution)/shard_map/pallas_call | solution.py:302
  37.2 0.0 copy-start.8
  37.2 4.6 %all-to-all-start.2 = ((f32[16,32,128]{2,1,0:T(8,128)}), f32[16,32,128]{2,1,0:T(8,128)S(1)}, u32[]{:S(2)}, u32[]{:S(2)}) async-start(f32[16,32,128]{2,1,0:T(8,128)} %get-tuple-element.21), calls=%async_computation.2 | async-start | bytes 524288 | tf_op jit(solution)/shard_map/all_to_all | solution.py:359
  41.8 0.0 copy-done.8
  41.8 0.0 copy-start.3
  41.8 0.0 copy-start.5
  41.9 1.1 %shard_map.135.v_ref = bf16[2048,256]{1,0:T(8,128)(2,1)S(1)} custom-call(f32[8,64,128]{2,1,0:T(8,128)S(1)} %all-to-all-done.recv_ref, f32[64,256]{1,0:T(8,128)S(1)} %copy-done.8), custom_call_target="tpu_custom_call" | custom-call | flops 1000000000 | bytes 1376256 | tf_op jit(solution)/shard_map/pallas_call | solution.py:302
  42.9 0.0 copy-done.3
  42.9 0.0 copy-done.5
  42.9 0.0 copy-start.1
  43.0 0.0 copy-start.6
  43.0 0.0 copy-start.9
  43.0 0.0 copy-start.10
  43.0 2.3 %shard_map.137 = f32[32,16,128]{2,1,0:T(8,128)} custom-call(f32[16,32,128]{2,1,0:T(8,128)S(1)} %get-tuple-element.25.mid_ref, f32[128,1024]{1,0:T(8,128)S(1)} %copy-done.3, f32[512,128]{1,0:T(8,128)S(1)} %copy-done.5), custom_call_target="tpu_custom_call" | custom-call | flops 1000000000 | bytes 1310720 | tf_op jit(solution)/shard_map/pallas_call | solution.py:302
  45.3 5.2 %all-to-all-done.2.recv_ref = f32[16,32,128]{2,1,0:T(8,128)S(1)} async-done(((f32[16,32,128]{2,1,0:T(8,128)}), f32[16,32,128]{2,1,0:T(8,128)S(1)}, u32[]{:S(2)}, u32[]{:S(2)}) %all-to-all-start.2) | async-done | bytes 262176 | tf_op jit(solution)/shard_map/all_to_all | solution.py:359
  50.6 0.0 copy-done.1
  50.6 0.0 copy-done.6
  50.6 0.0 copy-done.9
  50.6 0.0 copy-done.10
  50.6 2.6 %shard_map.136 = f32[4,32,64]{2,1,0:T(8,128)} custom-call(f32[16,32,128]{2,1,0:T(8,128)S(1)} %all-to-all-done.2.recv_ref, bf16[2048,256]{1,0:T(8,128)(2,1)S(1)} %shard_map.135.v_ref, f32[32,1024]{1,0:T(8,128)S(1)} %get-tuple-element.24.gate_ref, f32[64,256]{1,0:T(8,128)S(1)} %bitcast.3, f32[4,32,64]{2,1,0:T(8,128)S(1)} %copy-done.1, ...), custom_call_target="tpu_custom_call" | custom-call | flops 500000000 | bytes 1769472 | tf_op jit(solution)/shard_map/pallas_call | solution.py:302
Async XLA Ops:
  0.6 0.8 %copy-start = (f32[4,32,64]{2,1,0:T(8,128)S(1)}, f32[4,32,64]{2,1,0:T(8,128)}, u32[]{:S(2)}) copy-start(f32[4,32,64]{2,1,0:T(8,128)} %x_ref.3) | copy-start | bytes 98308
  1.5 7.9 %copy-start.2 = (f32[1024,128]{1,0:T(8,128)S(1)}, f32[1024,128]{1,0:T(8,128)}, u32[]{:S(2)}) copy-start(f32[1024,128]{1,0:T(8,128)} %t_ref.1) | copy-start | bytes 1572868
  2.4 6.9 %copy-start.7 = (f32[64,256]{1,0:T(8,128)S(1)}, f32[64,256]{1,0:T(8,128)}, u32[]{:S(2)}) copy-start(f32[64,256]{1,0:T(8,128)} %wg_ref.1) | copy-start | bytes 196612
  2.4 6.9 %copy-start.12 = (f32[128,8]{0,1:T(8,128)S(1)}, f32[128,8]{0,1:T(8,128)}, u32[]{:S(2)}) copy-start(f32[128,8]{0,1:T(8,128)} %param.18) | copy-start | bytes 12292
  2.4 13.0 %all-to-all-start = ((f32[8,64,128]{2,1,0:T(8,128)}), f32[8,64,128]{2,1,0:T(8,128)S(1)}, u32[]{:S(2)}, u32[]{:S(2)}) async-start(f32[8,64,128]{2,1,0:T(8,128)} %get-tuple-element.14), calls=%async_computation | async-start | bytes 524288 | tf_op jit(solution)/shard_map/all_to_all | solution.py:334
  9.4 0.8 %copy-start.11 = (f32[64,64]{1,0:T(8,128)S(1)}, f32[64,64]{1,0:T(8,128)}, u32[]{:S(2)}) copy-start(f32[64,64]{1,0:T(8,128)} %w_ref.1) | copy-start | bytes 49156
  15.7 18.6 %copy-start.4 = (f32[32,16,128]{2,1,0:T(8,128)S(1)}, f32[32,16,128]{2,1,0:T(8,128)}, u32[]{:S(2)}) copy-start(f32[32,16,128]{2,1,0:T(8,128)} %pair_ref.1) | copy-start | bytes 786436
  37.2 4.6 %copy-start.8 = (f32[64,256]{1,0:T(8,128)S(1)}, f32[64,256]{1,0:T(8,128)}, u32[]{:S(2)}) copy-start(f32[64,256]{1,0:T(8,128)} %wv_ref.1) | copy-start | bytes 196612
  37.2 13.3 %all-to-all-start.2 = ((f32[16,32,128]{2,1,0:T(8,128)}), f32[16,32,128]{2,1,0:T(8,128)S(1)}, u32[]{:S(2)}, u32[]{:S(2)}) async-start(f32[16,32,128]{2,1,0:T(8,128)} %get-tuple-element.21), calls=%async_computation.2 | async-start | bytes 524288 | tf_op jit(solution)/shard_map/all_to_all | solution.py:359
  41.8 1.1 %copy-start.3 = (f32[128,1024]{1,0:T(8,128)S(1)}, f32[128,1024]{1,0:T(8,128)}, u32[]{:S(2)}) copy-start(f32[128,1024]{1,0:T(8,128)} %expand_ref.3) | copy-start | bytes 1572868
  41.8 1.1 %copy-start.5 = (f32[512,128]{1,0:T(8,128)S(1)}, f32[512,128]{1,0:T(8,128)}, u32[]{:S(2)}) copy-start(f32[512,128]{1,0:T(8,128)} %shrink_ref.1) | copy-start | bytes 786436
  42.9 7.6 %copy-start.1 = (f32[4,32,64]{2,1,0:T(8,128)S(1)}, f32[4,32,64]{2,1,0:T(8,128)}, u32[]{:S(2)}) copy-start(f32[4,32,64]{2,1,0:T(8,128)} %x_ref.3) | copy-start | bytes 98308
  43.0 7.6 %copy-start.6 = (f32[64,512]{1,0:T(8,128)S(1)}, f32[64,512]{1,0:T(8,128)}, u32[]{:S(2)}) copy-start(f32[64,512]{1,0:T(8,128)} %expand_ref.2) | copy-start | bytes 393220
  43.0 7.6 %copy-start.9 = (f32[256,64]{0,1:T(8,128)S(1)}, f32[256,64]{0,1:T(8,128)}, u32[]{:S(2)}) copy-start(f32[256,64]{0,1:T(8,128)} %param.19) | copy-start | bytes 196612
  43.0 7.6 %copy-start.10 = (f32[256,64]{0,1:T(8,128)S(1)}, f32[256,64]{0,1:T(8,128)}, u32[]{:S(2)}) copy-start(f32[256,64]{0,1:T(8,128)} %param.21) | copy-start | bytes 196612

commit v4 on v3

--- a/solution.py
+++ b/solution.py
@@ -82,64 +82,50 @@
         send_ref[d, TOK:, :] = high
 
 
-def prepare_kernel(
-    own_ref, w_ref, t_ref, score_ref, wg_ref,
-    left_ref, wr_hi_ref, wr_lo_ref, t_out_ref, score_out_ref, gate_ref,
-):
-    x = own_ref[...]
-    one = split(x)
-    xs = tuple(jnp.concatenate([part] * 4, axis=0) for part in one)
-    ws = split(w_ref[...])
+def all_tokens(recv_ref):
+    return (
+        recv_ref[:, :TOK, :].reshape(TI * TOK, 128),
+        recv_ref[:, TOK:, :].reshape(TI * TOK, 128),
+    )
+
+
+def factors_kernel(recv_ref, own_ref, w_ref, send_ref):
+    w = w_ref[...]
+    group = iota((64, 128), 1) // 32
+    twice = jnp.concatenate([w, w], axis=1)
+    wide = split(jnp.where(group % 2 == 1, twice, pltpu.roll(twice, 96, 1)))
+    zero = jnp.zeros((64, 128), BF16)
+    wr = [[jnp.where(group == s, part, zero) for s in range(ROWS)] for part in wide]
+    low, high = (split(x) for x in all_tokens(recv_ref))
+    wr_low = tuple(jnp.concatenate(tiles[:2], axis=0) for tiles in wr)
+    wr_high = tuple(jnp.concatenate(tiles[2:], axis=0) for tiles in wr)
+    right = dot3(low, wr_low) + dot3(high, wr_high)
+    xs = tuple(jnp.concatenate([part] * 4, axis=0) for part in split(own_ref[...]))
     pick = (iota((128, 64), 0) // 4 == iota((128, 64), 1)).astype(BF16)
-    tile_k = (iota((64, 256), 0) == iota((64, 256), 1) % 64).astype(BF16)
     keep = iota((128, 256), 0) % 4 == iota((128, 256), 1) // 64
     wl = []
-    for part in ws:
-        rows = dot(pick, part, NT).astype(BF16)
-        wl.append(jnp.where(keep, dot(rows, tile_k), 0.0).astype(BF16))
+    for part in split(w):
+        rows = dot(pick, part, NT)
+        wl.append(jnp.where(keep, jnp.concatenate([rows] * 4, axis=1), 0.0).astype(BF16))
     prod = dot3(tuple(wl), xs, NT) * (1.0 / 64.0)
     group = iota((16, 128), 1) // 32
+    left = []
     for half in range(2):
         out = jnp.zeros((16, 128), F32)
         for q in range(4):
             at = half * 64 + q * 16
             out = jnp.where(group == q, prod[at : at + 16], out)
-        left_ref[half * 16 : half * 16 + 16, :] = out
-    tile_b = (iota((64, 128), 0) == 32 + iota((64, 128), 1) % 32).astype(BF16)
-    keep_r = iota((256, 128), 0) // 64 == iota((256, 128), 1) // 32
-    for part, ref in zip(ws, (wr_hi_ref, wr_lo_ref)):
-        tall = jnp.concatenate([dot(part, tile_b)] * 4, axis=0)
-        ref[...] = jnp.where(keep_r, tall, 0.0).astype(BF16)
-    th, tl = split(t_ref[...])
-    t_out_ref[:, :128] = th
-    t_out_ref[:, 128:] = tl
-    score = score_ref[...]
-    tall = jnp.concatenate([jnp.broadcast_to(score[h : h + 1], (16, 128)) for h in range(8)], axis=0)
-    sh, sl = split(tall.T)
-    score_out_ref[:, :128] = sh
-    score_out_ref[:, 128:] = sl
+        left.append(out)
+    for d in range(TJ):
+        send_ref[d, :16, :] = left[0]
+        send_ref[d, 16:32, :] = left[1]
+        send_ref[d, 32:, :] = right[d * COLS : (d + 1) * COLS]
+
+
+def values_kernel(recv_ref, wv_ref, own_ref, wg_ref, v_ref, gate_ref):
+    own = split(own_ref[...])
     for h, wg in enumerate(head_weights(wg_ref[...])):
-        gate_ref[:, h * 128 : h * 128 + 128] = 1.0 / (1.0 + jnp.exp(-dot3(one, wg)))
-
-
-def all_tokens(recv_ref):
-    return (
-        recv_ref[:, :TOK, :].reshape(TI * TOK, 128),
-        recv_ref[:, TOK:, :].reshape(TI * TOK, 128),
-    )
-
-
-def right_kernel(recv_ref, left_ref, wr_hi_ref, wr_lo_ref, send_ref):
-    low, high = all_tokens(recv_ref)
-    wh, wl = wr_hi_ref[...], wr_lo_ref[...]
-    right = dot3(split(low), (wh[:128], wl[:128])) + dot3(split(high), (wh[128:], wl[128:]))
-    left = left_ref[...]
-    for d in range(TJ):
-        send_ref[d, :32, :] = left
-        send_ref[d, 32:, :] = right[d * COLS : (d + 1) * COLS]
-
-
-def values_kernel(recv_ref, wv_ref, v_ref):
+        gate_ref[:, h * 128 : h * 128 + 128] = 1.0 / (1.0 + jnp.exp(-dot3(own, wg)))
     low, high = all_tokens(recv_ref)
     xs = split(jnp.concatenate([low, high], axis=1))
     for h, wv in enumerate(head_weights(wv_ref[...])):
@@ -161,6 +147,7 @@
     zero = jnp.zeros((16, 128), BF16)
     column = iota((TOK, 128), 1) % 16
     tile = jnp.zeros((TOK, 128), F32)
+    th, tl = split(t_ref[...])
     fh, fl = [], []
     for pair in range(COLS // 2):
         blocks = []
@@ -185,16 +172,17 @@
                         [part[g * 32 : g * 32 + 32, q * 128 : q * 128 + 128] for g in range(8)], axis=1
                     )
                 )
-    wide = dot(jnp.concatenate(fh, axis=0), t_ref[...])
-    update = wide[:, :128] + wide[:, 128:] + dot(jnp.concatenate(fl, axis=0), t_ref[:, :128])
+    wide = dot(jnp.concatenate(fh, axis=0), jnp.concatenate([th, tl], axis=1))
+    update = wide[:, :128] + wide[:, 128:] + dot(jnp.concatenate(fl, axis=0), th)
     normal = []
     for j in range(COLS):
         mid = pair_ref[:, j, :] + update[j * TOK : (j + 1) * TOK]
         mid_ref[j] = mid
         normal.append(normed(mid))
     nh, nl = split(jnp.concatenate(normal, axis=0))
-    wide = dot(nh, score_ref[...])
-    logits = wide[:, :128] + wide[:, 128:] + dot(nl, score_ref[:, :128])
+    score = score_ref[...]
+    score = [jnp.broadcast_to(score[h : h + 1], (16, 128)) for h in range(8)]
+    logits = dot3((nh, nl), split(jnp.concatenate(score, axis=0)), NT)
     for j in range(COLS):
         tile = jnp.where(column == j, logits[j * TOK : (j + 1) * TOK], tile)
     for d in range(TJ):
@@ -332,27 +320,15 @@
     exchange = functools.partial(lax.all_to_all, split_axis=0, concat_axis=0, tiled=True)
     send, own = call(first_kernel, [shape((TI, 64, 128)), shape((TOK, 256))], alignment_source)
     tokens = exchange(send, "ti")
-    prepared = call(
-        prepare_kernel,
-        [shape((32, 128)), shape((256, 128), BF16), shape((256, 128), BF16)]
-        + [shape((1024, 256), BF16), shape((128, 256), BF16), shape((32, 1024))],
-        own,
-        tensor_operand_matrix,
-        tensor_final_matrix,
-        mixing_score_matrix.T,
-        mixing_switch_matrix,
-        flops=500_000_000,
-    )
-    left, wr_hi, wr_lo, final2, score2, gates = prepared
-    factors = call(right_kernel, shape((TJ, 48, 128)), tokens, left, wr_hi, wr_lo)
+    factors = call(factors_kernel, shape((TJ, 48, 128)), tokens, own, tensor_operand_matrix)
     factors = exchange(factors, "tj")
     mid, logits = call(
         pair_kernel,
         [shape((COLS, TOK, 128)), shape((TJ, TOK, 128))],
         factors,
         couple_source,
-        final2,
-        score2,
+        tensor_final_matrix,
+        mixing_score_matrix.T,
         flops=2_000_000_000,
     )
     mid, tokens = lax.optimization_barrier((mid, tokens))
@@ -365,8 +341,14 @@
         couple_shrink_matrix,
         flops=1_000_000_000,
     )
-    values = call(
-        values_kernel, shape((2048, 256), BF16), tokens, mixing_content_matrix, flops=1_000_000_000
+    values, gates = call(
+        values_kernel,
+        [shape((2048, 256), BF16), shape((TOK, 1024))],
+        tokens,
+        mixing_content_matrix,
+        own,
+        mixing_switch_matrix,
+        flops=1_000_000_000,
     )
     alignment_result = call(
         last_kernel,

time: 53.7 us -> 53 us (0.987)
  blocking collectives: 18.5 us -> 31.2 us
  starting transfers between devices: 11.5 us -> 4.62 us
  waiting for transfers between devices: 9.81 us -> 5.07 us
  Pallas kernels: 10.8 us -> 10 us
  local copies, waits for them, and re-layouts: 1.65 us -> 0.9 us
    all_to_all x0 -> x1, blocking collectives: none -> 12.7 us  [shards(): tokens = exchange(send, 'ti')]
    all_to_all x1 -> x0, starting transfers between devices: 6.92 us -> none  [shards(): tokens = exchange(send, 'ti')]
    all_to_all x1 -> x0, waiting for transfers between devices: 4.57 us -> none  [shards(): tokens = exchange(send, 'ti')]
    pallas_call x7 -> x6, Pallas kernels: 10.8 us -> 10 us  [call(): pl.pallas_call(kernel, out_shape=outs, in_specs=in_specs, out_specs=[vmem...]
    unnamed x26, local copies, waits for them, and re-layouts: 1.65 us -> 0.9 us
  transfers between devices with their start and end apart: 2 -> 1, of which waited for: 2 -> 1; matrix products, arithmetic and copies ran while one was open for 0% -> 0% of each run, Pallas kernels for 8% -> 7%
where the time goes in v4:
time: 53 us; the launch traced here: 52.6 us
  blocking collectives  31.2 us (59%)
  Pallas kernels  10 us (19%)
  waiting for transfers between devices  5.07 us (10%)
  starting transfers between devices  4.62 us (9%)
  local copies, waits for them, and re-layouts  0.9 us (2%)
  between operations  0.76 us (1%)
    all_to_all x1, blocking collectives, shards(): factors = exchange(factors, 'tj')  18.5 us
    all_to_all x1, blocking collectives, shards(): tokens = exchange(send, 'ti')  12.7 us
    pallas_call x6, Pallas kernels, call(): pl.pallas_call(kernel, out_shape=outs, in_specs=in_specs, out_specs=[vmem...  10 us
    all_to_all x1, waiting for transfers between devices, shards(): logits = exchange(logits, 'tj')  5.07 us
    all_to_all x1, starting transfers between devices, shards(): logits = exchange(logits, 'tj')  4.62 us
  transfers between devices with their start and end apart: 1, of which 1 were waited for; matrix products, arithmetic and copies ran while one was open for 0% of the time, Pallas kernels for 7%

profile of v4, /device:TPU:1, one launch (start us, length us, event | category | flops | bytes accessed | tf_op | source)
XLA Modules:
  0.0 52.6 jit_solution(9075054296644269210)
XLA Ops:
  0.6 0.0 copy-start
  0.6 0.8 %copy-done = f32[4,32,64]{2,1,0:T(8,128)S(1)} copy-done((f32[4,32,64]{2,1,0:T(8,128)S(1)}, f32[4,32,64]{2,1,0:T(8,128)}, u32[]{:S(2)}) %copy-start) | copy-done | bytes 32792
  1.5 0.2 shard_map.131
  1.7 0.0 copy-start.2
  1.7 12.7 %all_to_all.15.recv_ref = f32[8,64,128]{2,1,0:T(8,128)S(1)} all-to-all(f32[8,64,128]{2,1,0:T(8,128)S(1)} %get-tuple-element.10), channel_id=1, replica_groups=mesh['ti'=8,'tj'=16] {'ti'}, dimensions={0} | all-to-all | bytes 524288 | tf_op jit(solution)/shard_map/all_to_all | solution.py:322
  14.4 0.0 copy-done.2
  14.4 0.0 copy-start.12
  14.4 0.6 %shard_map.132 = f32[16,48,128]{2,1,0:T(8,128)S(1)} custom-call(f32[8,64,128]{2,1,0:T(8,128)S(1)} %all_to_all.15.recv_ref, f32[32,256]{1,0:T(8,128)S(1)} %get-tuple-element.11.own_ref, f32[64,64]{1,0:T(8,128)S(1)} %copy-done.2), custom_call_target="tpu_custom_call" | custom-call | bytes 704512 | tf_op jit(solution)/shard_map/pallas_call | solution.py:290
  15.1 0.0 copy-start.3
  15.1 0.0 copy-start.5
  15.1 18.5 %all_to_all.16.recv_ref = f32[16,48,128]{2,1,0:T(8,128)S(1)} all-to-all(f32[16,48,128]{2,1,0:T(8,128)S(1)} %shard_map.132), channel_id=1, replica_groups=mesh['ti'=8,'tj'=16] {'tj'}, dimensions={0} | all-to-all | bytes 786432 | tf_op jit(solution)/shard_map/all_to_all | solution.py:324
  33.6 0.0 copy-done.12
  33.6 0.0 copy-done.3
  33.6 0.0 copy-done.5
  33.6 0.0 copy-start.6
  33.6 3.0 %shard_map.133 = (f32[16,32,128]{2,1,0:T(8,128)S(1)}, f32[16,32,128]{2,1,0:T(8,128)}) custom-call(f32[16,48,128]{2,1,0:T(8,128)S(1)} %all_to_all.16.recv_ref, f32[32,16,128]{2,1,0:T(8,128)S(1)} %copy-done.5, f32[1024,128]{1,0:T(8,128)S(1)} %copy-done.3, f32[8,128]{1,0:T(8,128)S(1)} %bitcast.5), custom_call_target="tpu_custom_call" | custom-call | flops 2000000000 | bytes 1708032 | tf_op jit(solution)/shard_map/pallas_call | solution.py:290
  36.7 0.0 copy-start.4
  36.7 4.6 %all-to-all-start.2 = ((f32[16,32,128]{2,1,0:T(8,128)}), f32[16,32,128]{2,1,0:T(8,128)S(1)}, u32[]{:S(2)}, u32[]{:S(2)}) async-start(f32[16,32,128]{2,1,0:T(8,128)} %get-tuple-element.12), calls=%async_computation.2 | async-start | bytes 524288 | tf_op jit(solution)/shard_map/all_to_all | solution.py:335
  41.3 0.0 copy-done.6
  41.3 0.0 copy-done.4
  41.3 0.0 copy-start.8
  41.3 0.0 copy-start.9
  41.3 2.3 %shard_map.136 = f32[32,16,128]{2,1,0:T(8,128)} custom-call(f32[16,32,128]{2,1,0:T(8,128)S(1)} %get-tuple-element.17.mid_ref, f32[128,1024]{1,0:T(8,128)S(1)} %copy-done.4, f32[512,128]{1,0:T(8,128)S(1)} %copy-done.6), custom_call_target="tpu_custom_call" | custom-call | flops 1000000000 | bytes 1310720 | tf_op jit(solution)/shard_map/pallas_call | solution.py:290
  43.7 0.0 copy-done.8
  43.7 0.0 copy-done.9
  43.7 0.0 copy-start.1
  43.7 0.0 copy-start.7
  43.7 0.0 copy-start.10
  43.7 0.0 copy-start.11
  43.7 1.3 %shard_map.134 = (bf16[2048,256]{1,0:T(8,128)(2,1)S(1)}, f32[32,1024]{1,0:T(8,128)S(1)}) custom-call(f32[8,64,128]{2,1,0:T(8,128)S(1)} %all_to_all.15.recv_ref, f32[64,256]{1,0:T(8,128)S(1)} %copy-done.8, f32[32,256]{1,0:T(8,128)S(1)} %get-tuple-element.11.own_ref, f32[64,256]{1,0:T(8,128)S(1)} %copy-done.9), custom_call_target="tpu_custom_call" | custom-call | flops 1000000000 | bytes 1605632 | tf_op jit(solution)/shard_map/pallas_call | solution.py:290
  45.0 5.1 %all-to-all-done.2.recv_ref = f32[16,32,128]{2,1,0:T(8,128)S(1)} async-done(((f32[16,32,128]{2,1,0:T(8,128)}), f32[16,32,128]{2,1,0:T(8,128)S(1)}, u32[]{:S(2)}, u32[]{:S(2)}) %all-to-all-start.2) | async-done | bytes 262176 | tf_op jit(solution)/shard_map/all_to_all | solution.py:335
  50.0 0.0 copy-done.1
  50.0 0.0 copy-done.7
  50.0 0.0 copy-done.10
  50.0 0.0 copy-done.11
  50.1 2.6 %shard_map.135 = f32[4,32,64]{2,1,0:T(8,128)} custom-call(f32[16,32,128]{2,1,0:T(8,128)S(1)} %all-to-all-done.2.recv_ref, bf16[2048,256]{1,0:T(8,128)(2,1)S(1)} %get-tuple-element.15.v_ref, f32[32,1024]{1,0:T(8,128)S(1)} %get-tuple-element.16.gate_ref, f32[64,256]{1,0:T(8,128)S(1)} %bitcast.3, f32[4,32,64]{2,1,0:T(8,128)S(1)} %copy-done.1, ...), custom_call_target="tpu_custom_call" | custom-call | flops 500000000 | bytes 1769472 | tf_op jit(solution)/shard_map/pallas_call | solution.py:290
Async XLA Ops:
  0.6 0.8 %copy-start = (f32[4,32,64]{2,1,0:T(8,128)S(1)}, f32[4,32,64]{2,1,0:T(8,128)}, u32[]{:S(2)}) copy-start(f32[4,32,64]{2,1,0:T(8,128)} %x_ref.3) | copy-start | bytes 98308
  1.7 12.7 %copy-start.2 = (f32[64,64]{1,0:T(8,128)S(1)}, f32[64,64]{1,0:T(8,128)}, u32[]{:S(2)}) copy-start(f32[64,64]{1,0:T(8,128)} %w_ref.1) | copy-start | bytes 49156
  14.4 19.2 %copy-start.12 = (f32[128,8]{0,1:T(8,128)S(1)}, f32[128,8]{0,1:T(8,128)}, u32[]{:S(2)}) copy-start(f32[128,8]{0,1:T(8,128)} %param.18) | copy-start | bytes 12292
  15.1 18.6 %copy-start.3 = (f32[1024,128]{1,0:T(8,128)S(1)}, f32[1024,128]{1,0:T(8,128)}, u32[]{:S(2)}) copy-start(f32[1024,128]{1,0:T(8,128)} %t_ref.1) | copy-start | bytes 1572868
  15.1 18.6 %copy-start.5 = (f32[32,16,128]{2,1,0:T(8,128)S(1)}, f32[32,16,128]{2,1,0:T(8,128)}, u32[]{:S(2)}) copy-start(f32[32,16,128]{2,1,0:T(8,128)} %pair_ref.1) | copy-start | bytes 786436
  33.6 7.7 %copy-start.6 = (f32[512,128]{1,0:T(8,128)S(1)}, f32[512,128]{1,0:T(8,128)}, u32[]{:S(2)}) copy-start(f32[512,128]{1,0:T(8,128)} %shrink_ref.1) | copy-start | bytes 786436
  36.7 4.6 %copy-start.4 = (f32[128,1024]{1,0:T(8,128)S(1)}, f32[128,1024]{1,0:T(8,128)}, u32[]{:S(2)}) copy-start(f32[128,1024]{1,0:T(8,128)} %expand_ref.3) | copy-start | bytes 1572868
  36.7 13.3 %all-to-all-start.2 = ((f32[16,32,128]{2,1,0:T(8,128)}), f32[16,32,128]{2,1,0:T(8,128)S(1)}, u32[]{:S(2)}, u32[]{:S(2)}) async-start(f32[16,32,128]{2,1,0:T(8,128)} %get-tuple-element.12), calls=%async_computation.2 | async-start | bytes 524288 | tf_op jit(solution)/shard_map/all_to_all | solution.py:335
  41.3 2.3 %copy-start.8 = (f32[64,256]{1,0:T(8,128)S(1)}, f32[64,256]{1,0:T(8,128)}, u32[]{:S(2)}) copy-start(f32[64,256]{1,0:T(8,128)} %wv_ref.1) | copy-start | bytes 196612
  41.3 2.3 %copy-start.9 = (f32[64,256]{1,0:T(8,128)S(1)}, f32[64,256]{1,0:T(8,128)}, u32[]{:S(2)}) copy-start(f32[64,256]{1,0:T(8,128)} %wg_ref.1) | copy-start | bytes 196612
  43.7 6.4 %copy-start.1 = (f32[4,32,64]{2,1,0:T(8,128)S(1)}, f32[4,32,64]{2,1,0:T(8,128)}, u32[]{:S(2)}) copy-start(f32[4,32,64]{2,1,0:T(8,128)} %x_ref.3) | copy-start | bytes 98308
  43.7 6.4 %copy-start.7 = (f32[64,512]{1,0:T(8,128)S(1)}, f32[64,512]{1,0:T(8,128)}, u32[]{:S(2)}) copy-start(f32[64,512]{1,0:T(8,128)} %expand_ref.2) | copy-start | bytes 393220
  43.7 6.4 %copy-start.10 = (f32[256,64]{0,1:T(8,128)S(1)}, f32[256,64]{0,1:T(8,128)}, u32[]{:S(2)}) copy-start(f32[256,64]{0,1:T(8,128)} %param.19) | copy-start | bytes 196612
  43.7 6.4 %copy-start.11 = (f32[256,64]{0,1:T(8,128)S(1)}, f32[256,64]{0,1:T(8,128)}, u32[]{:S(2)}) copy-start(f32[256,64]{0,1:T(8,128)} %param.21) | copy-start | bytes 196612

commit v5 on v4

--- a/solution.py
+++ b/solution.py
@@ -1,5 +1,3 @@
-import functools
-
 import jax
 import jax.numpy as jnp
 from jax import lax
@@ -15,6 +13,8 @@
 ROWS = 4
 TOK = 32
 COLS = 16
+ORDER_TI = [k ^ 3 for k in range(8)]
+ORDER_TJ = [k ^ 11 for k in range(16)]
 NN = (((1,), (0,)), ((), ()))
 NT = (((1,), (1,)), ((), ()))
 
@@ -83,9 +83,10 @@
 
 
 def all_tokens(recv_ref):
+    slots = [ORDER_TI.index(d) for d in range(TI)]
     return (
-        recv_ref[:, :TOK, :].reshape(TI * TOK, 128),
-        recv_ref[:, TOK:, :].reshape(TI * TOK, 128),
+        jnp.concatenate([recv_ref[k, :TOK, :] for k in slots], axis=0),
+        jnp.concatenate([recv_ref[k, TOK:, :] for k in slots], axis=0),
     )
 
 
@@ -119,7 +120,8 @@
     for d in range(TJ):
         send_ref[d, :16, :] = left[0]
         send_ref[d, 16:32, :] = left[1]
-        send_ref[d, 32:, :] = right[d * COLS : (d + 1) * COLS]
+        at = ORDER_TJ[d] * COLS
+        send_ref[d, 32:, :] = right[at : at + COLS]
 
 
 def values_kernel(recv_ref, wv_ref, own_ref, wg_ref, v_ref, gate_ref):
@@ -131,9 +133,9 @@
     for h, wv in enumerate(head_weights(wv_ref[...])):
         vh, vl = split(dot3(xs, wv))
         for d in range(TJ):
-            at = (d * 8 + h) * COLS
-            v_ref[at : at + COLS, :128] = vh[d * COLS : (d + 1) * COLS]
-            v_ref[at : at + COLS, 128:] = vl[d * COLS : (d + 1) * COLS]
+            at, of = (d * 8 + h) * COLS, ORDER_TJ[d] * COLS
+            v_ref[at : at + COLS, :128] = vh[of : of + COLS]
+            v_ref[at : at + COLS, 128:] = vl[of : of + COLS]
 
 
 def pair_kernel(recv_ref, pair_ref, t_ref, score_ref, mid_ref, send_ref):
@@ -303,6 +305,10 @@
     return jax.ShapeDtypeStruct(dims, dtype)
 
 
+def exchange(x, axis, order):
+    return lax.all_to_all(x, axis, 0, 0, axis_index_groups=[order], tiled=True)
+
+
 def shards(
     alignment_source,
     couple_source,
@@ -317,11 +323,10 @@
     couple_expand_matrix,
     couple_shrink_matrix,
 ):
-    exchange = functools.partial(lax.all_to_all, split_axis=0, concat_axis=0, tiled=True)
     send, own = call(first_kernel, [shape((TI, 64, 128)), shape((TOK, 256))], alignment_source)
-    tokens = exchange(send, "ti")
+    tokens = exchange(send, "ti", ORDER_TI)
     factors = call(factors_kernel, shape((TJ, 48, 128)), tokens, own, tensor_operand_matrix)
-    factors = exchange(factors, "tj")
+    factors = exchange(factors, "tj", ORDER_TJ)
     mid, logits = call(
         pair_kernel,
         [shape((COLS, TOK, 128)), shape((TJ, TOK, 128))],
@@ -332,7 +337,7 @@
         flops=2_000_000_000,
     )
     mid, tokens = lax.optimization_barrier((mid, tokens))
-    logits = exchange(logits, "tj")
+    logits = exchange(logits, "tj", ORDER_TJ)
     couple_result = call(
         pair_transition_kernel,
         shape((TOK, COLS, 128)),

time: 53 us -> 46.6 us (0.88)
  blocking collectives: 31.2 us -> 26.4 us
  waiting for transfers between devices: 5.07 us -> 0.82 us
  starting transfers between devices: 4.62 us -> 7.29 us
    all_to_all x2, blocking collectives: 31.2 us -> 26.4 us  [exchange(): return lax.all_to_all(x, axis, 0, 0, axis_index_groups=[order], tiled=True)]
    all_to_all x1, waiting for transfers between devices: 5.07 us -> 0.82 us  [exchange(): return lax.all_to_all(x, axis, 0, 0, axis_index_groups=[order], tiled=True)]
    all_to_all x1, starting transfers between devices: 4.62 us -> 7.29 us  [exchange(): return lax.all_to_all(x, axis, 0, 0, axis_index_groups=[order], tiled=True)]
  transfers between devices with their start and end apart: 1 -> 1, of which waited for: 1 -> 1; matrix products, arithmetic and copies ran while one was open for 0% -> 0% of each run, Pallas kernels for 7% -> 8%
where the time goes in v5:
time: 46.6 us; the launch traced here: 46.2 us
  blocking collectives  26.4 us (57%)
  Pallas kernels  10 us (21%)
  starting transfers between devices  7.29 us (16%)
  local copies, waits for them, and re-layouts  0.9 us (2%)
  waiting for transfers between devices  0.82 us (2%)
  between operations  0.76 us (2%)
    all_to_all x2, blocking collectives, exchange(): return lax.all_to_all(x, axis, 0, 0, axis_index_groups=[order], tiled=True)  26.4 us
    pallas_call x6, Pallas kernels, call(): pl.pallas_call(kernel, out_shape=outs, in_specs=in_specs, out_specs=[vmem...  10 us
    all_to_all x1, starting transfers between devices, exchange(): return lax.all_to_all(x, axis, 0, 0, axis_index_groups=[order], tiled=True)  7.29 us
  transfers between devices with their start and end apart: 1, of which 1 were waited for; matrix products, arithmetic and copies ran while one was open for 0% of the time, Pallas kernels for 8%

profile of v5, /device:TPU:1, one launch (start us, length us, event | category | flops | bytes accessed | tf_op | source)
XLA Modules:
  0.0 46.2 jit_solution(17916747134932145225)
XLA Ops:
  0.6 0.0 copy-start
  0.6 0.8 %copy-done = f32[4,32,64]{2,1,0:T(8,128)S(1)} copy-done((f32[4,32,64]{2,1,0:T(8,128)S(1)}, f32[4,32,64]{2,1,0:T(8,128)}, u32[]{:S(2)}) %copy-start) | copy-done | bytes 32792
  1.5 0.2 shard_map.131
  1.7 0.0 copy-start.2
  1.7 11.1 %all_to_all.15.recv_ref = f32[8,64,128]{2,1,0:T(8,128)S(1)} all-to-all(f32[8,64,128]{2,1,0:T(8,128)S(1)} %get-tuple-element.10), channel_id=1, replica_groups={{48,32,16,0,112,96,80,64},{49,33,17,1,113,97,81,65},{50,34,18,2,114,98,..., dimensions={0} | all-to-all | bytes 524288 | tf_op jit(solution)/shard_map/all_to_all | solution.py:309
  12.9 0.0 copy-done.2
  12.9 0.0 copy-start.12
  12.9 0.6 %shard_map.132 = f32[16,48,128]{2,1,0:T(8,128)S(1)} custom-call(f32[8,64,128]{2,1,0:T(8,128)S(1)} %all_to_all.15.recv_ref, f32[32,256]{1,0:T(8,128)S(1)} %get-tuple-element.11.own_ref, f32[64,64]{1,0:T(8,128)S(1)} %copy-done.2), custom_call_target="tpu_custom_call" | custom-call | bytes 704512 | tf_op jit(solution)/shard_map/pallas_call | solution.py:292
  13.5 0.0 copy-start.3
  13.5 0.0 copy-start.5
  13.5 15.3 %all_to_all.16.recv_ref = f32[16,48,128]{2,1,0:T(8,128)S(1)} all-to-all(f32[16,48,128]{2,1,0:T(8,128)S(1)} %shard_map.132), channel_id=1, replica_groups={{11,10,9,8,15,14,13,12,3,2,1,0,7,6,5,4},{27,26,25,24,31,30,29,28,19,18,..., dimensions={0} | all-to-all | bytes 786432 | tf_op jit(solution)/shard_map/all_to_all | solution.py:309
  28.8 0.0 copy-done.12
  28.8 0.0 copy-done.3
  28.8 0.0 copy-done.5
  28.8 0.0 copy-start.6
  28.8 3.0 %shard_map.133 = (f32[16,32,128]{2,1,0:T(8,128)S(1)}, f32[16,32,128]{2,1,0:T(8,128)}) custom-call(f32[16,48,128]{2,1,0:T(8,128)S(1)} %all_to_all.16.recv_ref, f32[32,16,128]{2,1,0:T(8,128)S(1)} %copy-done.5, f32[1024,128]{1,0:T(8,128)S(1)} %copy-done.3, f32[8,128]{1,0:T(8,128)S(1)} %bitcast.5), custom_call_target="tpu_custom_call" | custom-call | flops 2000000000 | bytes 1708032 | tf_op jit(solution)/shard_map/pallas_call | solution.py:292
  31.9 0.0 copy-start.4
  31.9 7.3 %all-to-all-start.2 = ((f32[16,32,128]{2,1,0:T(8,128)}), f32[16,32,128]{2,1,0:T(8,128)S(1)}, u32[]{:S(2)}, u32[]{:S(2)}) async-start(f32[16,32,128]{2,1,0:T(8,128)} %get-tuple-element.12), calls=%async_computation.2 | async-start | bytes 524288 | tf_op jit(solution)/shard_map/all_to_all | solution.py:309
  39.2 0.0 copy-done.6
  39.2 0.0 copy-done.4
  39.2 0.0 copy-start.8
  39.2 0.0 copy-start.9
  39.2 2.3 %shard_map.136 = f32[32,16,128]{2,1,0:T(8,128)} custom-call(f32[16,32,128]{2,1,0:T(8,128)S(1)} %get-tuple-element.17.mid_ref, f32[128,1024]{1,0:T(8,128)S(1)} %copy-done.4, f32[512,128]{1,0:T(8,128)S(1)} %copy-done.6), custom_call_target="tpu_custom_call" | custom-call | flops 1000000000 | bytes 1310720 | tf_op jit(solution)/shard_map/pallas_call | solution.py:292
  41.5 0.0 copy-done.8
  41.5 0.0 copy-done.9
  41.5 0.0 copy-start.1
  41.5 0.0 copy-start.7
  41.5 0.0 copy-start.10
  41.6 0.0 copy-start.11
  41.6 1.3 %shard_map.134 = (bf16[2048,256]{1,0:T(8,128)(2,1)S(1)}, f32[32,1024]{1,0:T(8,128)S(1)}) custom-call(f32[8,64,128]{2,1,0:T(8,128)S(1)} %all_to_all.15.recv_ref, f32[64,256]{1,0:T(8,128)S(1)} %copy-done.8, f32[32,256]{1,0:T(8,128)S(1)} %get-tuple-element.11.own_ref, f32[64,256]{1,0:T(8,128)S(1)} %copy-done.9), custom_call_target="tpu_custom_call" | custom-call | flops 1000000000 | bytes 1605632 | tf_op jit(solution)/shard_map/pallas_call | solution.py:292
  42.8 0.8 %all-to-all-done.2.recv_ref = f32[16,32,128]{2,1,0:T(8,128)S(1)} async-done(((f32[16,32,128]{2,1,0:T(8,128)}), f32[16,32,128]{2,1,0:T(8,128)S(1)}, u32[]{:S(2)}, u32[]{:S(2)}) %all-to-all-start.2) | async-done | bytes 262176 | tf_op jit(solution)/shard_map/all_to_all | solution.py:309
  43.7 0.0 copy-done.1
  43.7 0.0 copy-done.7
  43.7 0.0 copy-done.10
  43.7 0.0 copy-done.11
  43.7 2.6 %shard_map.135 = f32[4,32,64]{2,1,0:T(8,128)} custom-call(f32[16,32,128]{2,1,0:T(8,128)S(1)} %all-to-all-done.2.recv_ref, bf16[2048,256]{1,0:T(8,128)(2,1)S(1)} %get-tuple-element.15.v_ref, f32[32,1024]{1,0:T(8,128)S(1)} %get-tuple-element.16.gate_ref, f32[64,256]{1,0:T(8,128)S(1)} %bitcast.3, f32[4,32,64]{2,1,0:T(8,128)S(1)} %copy-done.1, ...), custom_call_target="tpu_custom_call" | custom-call | flops 500000000 | bytes 1769472 | tf_op jit(solution)/shard_map/pallas_call | solution.py:292
Async XLA Ops:
  0.6 0.8 %copy-start = (f32[4,32,64]{2,1,0:T(8,128)S(1)}, f32[4,32,64]{2,1,0:T(8,128)}, u32[]{:S(2)}) copy-start(f32[4,32,64]{2,1,0:T(8,128)} %x_ref.3) | copy-start | bytes 98308
  1.7 11.2 %copy-start.2 = (f32[64,64]{1,0:T(8,128)S(1)}, f32[64,64]{1,0:T(8,128)}, u32[]{:S(2)}) copy-start(f32[64,64]{1,0:T(8,128)} %w_ref.1) | copy-start | bytes 49156
  12.9 15.9 %copy-start.12 = (f32[128,8]{0,1:T(8,128)S(1)}, f32[128,8]{0,1:T(8,128)}, u32[]{:S(2)}) copy-start(f32[128,8]{0,1:T(8,128)} %param.18) | copy-start | bytes 12292
  13.5 15.3 %copy-start.3 = (f32[1024,128]{1,0:T(8,128)S(1)}, f32[1024,128]{1,0:T(8,128)}, u32[]{:S(2)}) copy-start(f32[1024,128]{1,0:T(8,128)} %t_ref.1) | copy-start | bytes 1572868
  13.5 15.3 %copy-start.5 = (f32[32,16,128]{2,1,0:T(8,128)S(1)}, f32[32,16,128]{2,1,0:T(8,128)}, u32[]{:S(2)}) copy-start(f32[32,16,128]{2,1,0:T(8,128)} %pair_ref.1) | copy-start | bytes 786436
  28.8 10.3 %copy-start.6 = (f32[512,128]{1,0:T(8,128)S(1)}, f32[512,128]{1,0:T(8,128)}, u32[]{:S(2)}) copy-start(f32[512,128]{1,0:T(8,128)} %shrink_ref.1) | copy-start | bytes 786436
  31.9 7.3 %copy-start.4 = (f32[128,1024]{1,0:T(8,128)S(1)}, f32[128,1024]{1,0:T(8,128)}, u32[]{:S(2)}) copy-start(f32[128,1024]{1,0:T(8,128)} %expand_ref.3) | copy-start | bytes 1572868
  31.9 11.8 %all-to-all-start.2 = ((f32[16,32,128]{2,1,0:T(8,128)}), f32[16,32,128]{2,1,0:T(8,128)S(1)}, u32[]{:S(2)}, u32[]{:S(2)}) async-start(f32[16,32,128]{2,1,0:T(8,128)} %get-tuple-element.12), calls=%async_computation.2 | async-start | bytes 524288 | tf_op jit(solution)/shard_map/all_to_all | solution.py:309
  39.2 2.3 %copy-start.8 = (f32[64,256]{1,0:T(8,128)S(1)}, f32[64,256]{1,0:T(8,128)}, u32[]{:S(2)}) copy-start(f32[64,256]{1,0:T(8,128)} %wv_ref.1) | copy-start | bytes 196612
  39.2 2.3 %copy-start.9 = (f32[64,256]{1,0:T(8,128)S(1)}, f32[64,256]{1,0:T(8,128)}, u32[]{:S(2)}) copy-start(f32[64,256]{1,0:T(8,128)} %wg_ref.1) | copy-start | bytes 196612
  41.5 2.1 %copy-start.1 = (f32[4,32,64]{2,1,0:T(8,128)S(1)}, f32[4,32,64]{2,1,0:T(8,128)}, u32[]{:S(2)}) copy-start(f32[4,32,64]{2,1,0:T(8,128)} %x_ref.3) | copy-start | bytes 98308
  41.5 2.1 %copy-start.7 = (f32[64,512]{1,0:T(8,128)S(1)}, f32[64,512]{1,0:T(8,128)}, u32[]{:S(2)}) copy-start(f32[64,512]{1,0:T(8,128)} %expand_ref.2) | copy-start | bytes 393220
  41.5 2.1 %copy-start.10 = (f32[256,64]{0,1:T(8,128)S(1)}, f32[256,64]{0,1:T(8,128)}, u32[]{:S(2)}) copy-start(f32[256,64]{0,1:T(8,128)} %param.19) | copy-start | bytes 196612
  41.6 2.1 %copy-start.11 = (f32[256,64]{0,1:T(8,128)S(1)}, f32[256,64]{0,1:T(8,128)}, u32[]{:S(2)}) copy-start(f32[256,64]{0,1:T(8,128)} %param.21) | copy-start | bytes 196612

commit v6 on v5

--- a/solution.py
+++ b/solution.py
@@ -13,8 +13,9 @@
 ROWS = 4
 TOK = 32
 COLS = 16
-ORDER_TI = [k ^ 3 for k in range(8)]
+ORDER_TI = [k ^ 6 for k in range(8)]
 ORDER_TJ = [k ^ 11 for k in range(16)]
+ORDER_LOGITS = [k ^ 10 for k in range(16)]
 NN = (((1,), (0,)), ((), ()))
 NT = (((1,), (1,)), ((), ()))
 
@@ -133,7 +134,7 @@
     for h, wv in enumerate(head_weights(wv_ref[...])):
         vh, vl = split(dot3(xs, wv))
         for d in range(TJ):
-            at, of = (d * 8 + h) * COLS, ORDER_TJ[d] * COLS
+            at, of = (d * 8 + h) * COLS, ORDER_LOGITS[d] * COLS
             v_ref[at : at + COLS, :128] = vh[of : of + COLS]
             v_ref[at : at + COLS, 128:] = vl[of : of + COLS]
 
@@ -144,7 +145,7 @@
     ]
     left = jnp.concatenate(rows, axis=0).T
     lh, ll = split(left)
-    left3 = jnp.concatenate([lh, lh, ll], axis=1)
+    left2 = jnp.concatenate([lh, ll], axis=0)
     group = iota((16, 128), 1) // 32
     zero = jnp.zeros((16, 128), BF16)
     column = iota((TOK, 128), 1) % 16
@@ -164,8 +165,9 @@
                     for s in range(4)
                 ]
                 parts.append(jnp.concatenate(tiles, axis=0))
-            blocks.append(jnp.concatenate([parts[0], parts[1], parts[0]], axis=0))
-        outer = dot(left3, jnp.concatenate(blocks, axis=1))
+            blocks.append(parts)
+        both = dot(left2, jnp.concatenate([b[0] for b in blocks], axis=1))
+        outer = both[:256] + both[256:] + dot(lh, jnp.concatenate([b[1] for b in blocks], axis=1))
         oh, ol = split(outer)
         for q in range(2):
             for part, keep in ((oh, fh), (ol, fl)):
@@ -174,8 +176,8 @@
                         [part[g * 32 : g * 32 + 32, q * 128 : q * 128 + 128] for g in range(8)], axis=1
                     )
                 )
-    wide = dot(jnp.concatenate(fh, axis=0), jnp.concatenate([th, tl], axis=1))
-    update = wide[:, :128] + wide[:, 128:] + dot(jnp.concatenate(fl, axis=0), th)
+    wide = dot(jnp.concatenate(fh + fl, axis=0), jnp.concatenate([th, tl], axis=1))
+    update = wide[:512, :128] + wide[:512, 128:] + wide[512:, :128]
     normal = []
     for j in range(COLS):
         mid = pair_ref[:, j, :] + update[j * TOK : (j + 1) * TOK]
@@ -238,7 +240,7 @@
 
 
 def last_kernel(
-    recv_ref, v_ref, gate_ref, wf_ref, x_ref, expand_ref, shrink_ref, out_ref, w_hi, w_lo
+    recv_ref, v_ref, gate_ref, wf_ref, x_ref, expand_ref, shrink_ref, out_ref
 ):
     top = recv_ref[0]
     for d in range(1, TJ):
@@ -251,13 +253,12 @@
     inv = 1.0 / group_all(total, jnp.add)
     head = iota((TOK, 128), 1) // 16
     zero = jnp.zeros((TOK, 128), BF16)
+    high, low = [], []
     for d in range(TJ):
-        wh, wl = split(terms[d])
-        for h in range(8):
-            w_hi[h * TOK : (h + 1) * TOK, d * 128 : d * 128 + 128] = jnp.where(head == h, wh, zero)
-            w_lo[h * TOK : (h + 1) * TOK, d * 128 : d * 128 + 128] = jnp.where(head == h, wl, zero)
-    wide = dot(w_hi[...], v_ref[...])
-    mixed = wide[:, :128] + wide[:, 128:] + dot(w_lo[...], v_ref[:, :128])
+        for part, keep in zip(split(terms[d]), (high, low)):
+            keep.append(jnp.concatenate([jnp.where(head == h, part, zero) for h in range(8)], axis=0))
+    wide = dot(jnp.concatenate(high, axis=1), v_ref[...])
+    mixed = wide[:, :128] + wide[:, 128:] + dot(jnp.concatenate(low, axis=1), v_ref[:, :128])
     gated = [
         mixed[h * TOK : (h + 1) * TOK]
         * (gate_ref[:, h * 128 : h * 128 + 128] * inv[:, h * 16 : h * 16 + 1])
@@ -337,7 +338,7 @@
         flops=2_000_000_000,
     )
     mid, tokens = lax.optimization_barrier((mid, tokens))
-    logits = exchange(logits, "tj", ORDER_TJ)
+    logits = exchange(logits, "tj", ORDER_LOGITS)
     couple_result = call(
         pair_transition_kernel,
         shape((TOK, COLS, 128)),
@@ -365,7 +366,6 @@
         alignment_source,
         alignment_expand_matrix,
         alignment_shrink_matrix.T,
-        scratch=[pltpu.VMEM((256, 2048), BF16), pltpu.VMEM((256, 2048), BF16)],
         flops=500_000_000,
     )
     return (alignment_result, couple_result)

time: 46.6 us -> 46.3 us (level)
  no operation moved by 1% of the time
where the time goes in v6:
time: 46.3 us; the launch traced here: 45.9 us
  blocking collectives  26.1 us (56%)
  Pallas kernels  9.91 us (21%)
  starting transfers between devices  7.46 us (16%)
  local copies, waits for them, and re-layouts  0.9 us (2%)
  waiting for transfers between devices  0.78 us (2%)
  between operations  0.76 us (2%)
    all_to_all x2, blocking collectives, exchange(): return lax.all_to_all(x, axis, 0, 0, axis_index_groups=[order], tiled=True)  26.1 us
    pallas_call x6, Pallas kernels, call(): pl.pallas_call(kernel, out_shape=outs, in_specs=in_specs, out_specs=[vmem...  9.91 us
    all_to_all x1, starting transfers between devices, exchange(): return lax.all_to_all(x, axis, 0, 0, axis_index_groups=[order], tiled=True)  7.46 us
  transfers between devices with their start and end apart: 1, of which 1 were waited for; matrix products, arithmetic and copies ran while one was open for 0% of the time, Pallas kernels for 8%

profile of v6, /device:TPU:1, one launch (start us, length us, event | category | flops | bytes accessed | tf_op | source)
XLA Modules:
  0.0 45.9 jit_solution(941780178302337504)
XLA Ops:
  0.6 0.0 copy-start
  0.6 0.8 %copy-done = f32[4,32,64]{2,1,0:T(8,128)S(1)} copy-done((f32[4,32,64]{2,1,0:T(8,128)S(1)}, f32[4,32,64]{2,1,0:T(8,128)}, u32[]{:S(2)}) %copy-start) | copy-done | bytes 32792
  1.5 0.2 shard_map.131
  1.7 0.0 copy-start.2
  1.7 10.9 %all_to_all.15.recv_ref = f32[8,64,128]{2,1,0:T(8,128)S(1)} all-to-all(f32[8,64,128]{2,1,0:T(8,128)S(1)} %get-tuple-element.10), channel_id=1, replica_groups={{96,112,64,80,32,48,0,16},{97,113,65,81,33,49,1,17},{98,114,66,82,34,50..., dimensions={0} | all-to-all | bytes 524288 | tf_op jit(solution)/shard_map/all_to_all | solution.py:310
  12.6 0.0 copy-done.2
  12.6 0.0 copy-start.12
  12.7 0.6 %shard_map.132 = f32[16,48,128]{2,1,0:T(8,128)S(1)} custom-call(f32[8,64,128]{2,1,0:T(8,128)S(1)} %all_to_all.15.recv_ref, f32[32,256]{1,0:T(8,128)S(1)} %get-tuple-element.11.own_ref, f32[64,64]{1,0:T(8,128)S(1)} %copy-done.2), custom_call_target="tpu_custom_call" | custom-call | bytes 704512 | tf_op jit(solution)/shard_map/pallas_call | solution.py:293
  13.3 0.0 copy-start.3
  13.3 0.0 copy-start.5
  13.3 15.2 %all_to_all.16.recv_ref = f32[16,48,128]{2,1,0:T(8,128)S(1)} all-to-all(f32[16,48,128]{2,1,0:T(8,128)S(1)} %shard_map.132), channel_id=1, replica_groups={{11,10,9,8,15,14,13,12,3,2,1,0,7,6,5,4},{27,26,25,24,31,30,29,28,19,18,..., dimensions={0} | all-to-all | bytes 786432 | tf_op jit(solution)/shard_map/all_to_all | solution.py:310
  28.5 0.0 copy-done.12
  28.5 0.0 copy-done.3
  28.5 0.0 copy-done.5
  28.5 0.0 copy-start.6
  28.5 3.0 %shard_map.133 = (f32[16,32,128]{2,1,0:T(8,128)S(1)}, f32[16,32,128]{2,1,0:T(8,128)}) custom-call(f32[16,48,128]{2,1,0:T(8,128)S(1)} %all_to_all.16.recv_ref, f32[32,16,128]{2,1,0:T(8,128)S(1)} %copy-done.5, f32[1024,128]{1,0:T(8,128)S(1)} %copy-done.3, f32[8,128]{1,0:T(8,128)S(1)} %bitcast.5), custom_call_target="tpu_custom_call" | custom-call | flops 2000000000 | bytes 1708032 | tf_op jit(solution)/shard_map/pallas_call | solution.py:293
  31.5 0.0 copy-start.4
  31.5 7.5 %all-to-all-start.2 = ((f32[16,32,128]{2,1,0:T(8,128)}), f32[16,32,128]{2,1,0:T(8,128)S(1)}, u32[]{:S(2)}, u32[]{:S(2)}) async-start(f32[16,32,128]{2,1,0:T(8,128)} %get-tuple-element.12), calls=%async_computation.2 | async-start | bytes 524288 | tf_op jit(solution)/shard_map/all_to_all | solution.py:310
  38.9 0.0 copy-done.6
  38.9 0.0 copy-done.4
  38.9 0.0 copy-start.8
  39.0 0.0 copy-start.9
  39.0 2.3 %shard_map.136 = f32[32,16,128]{2,1,0:T(8,128)} custom-call(f32[16,32,128]{2,1,0:T(8,128)S(1)} %get-tuple-element.17.mid_ref, f32[128,1024]{1,0:T(8,128)S(1)} %copy-done.4, f32[512,128]{1,0:T(8,128)S(1)} %copy-done.6), custom_call_target="tpu_custom_call" | custom-call | flops 1000000000 | bytes 1310720 | tf_op jit(solution)/shard_map/pallas_call | solution.py:293
  41.3 0.0 copy-done.8
  41.3 0.0 copy-done.9
  41.3 0.0 copy-start.1
  41.3 0.0 copy-start.7
  41.3 0.0 copy-start.10
  41.3 0.0 copy-start.11
  41.3 1.3 %shard_map.134 = (bf16[2048,256]{1,0:T(8,128)(2,1)S(1)}, f32[32,1024]{1,0:T(8,128)S(1)}) custom-call(f32[8,64,128]{2,1,0:T(8,128)S(1)} %all_to_all.15.recv_ref, f32[64,256]{1,0:T(8,128)S(1)} %copy-done.8, f32[32,256]{1,0:T(8,128)S(1)} %get-tuple-element.11.own_ref, f32[64,256]{1,0:T(8,128)S(1)} %copy-done.9), custom_call_target="tpu_custom_call" | custom-call | flops 1000000000 | bytes 1605632 | tf_op jit(solution)/shard_map/pallas_call | solution.py:293
  42.6 0.8 %all-to-all-done.2.recv_ref = f32[16,32,128]{2,1,0:T(8,128)S(1)} async-done(((f32[16,32,128]{2,1,0:T(8,128)}), f32[16,32,128]{2,1,0:T(8,128)S(1)}, u32[]{:S(2)}, u32[]{:S(2)}) %all-to-all-start.2) | async-done | bytes 262176 | tf_op jit(solution)/shard_map/all_to_all | solution.py:310
  43.4 0.0 copy-done.1
  43.4 0.0 copy-done.7
  43.4 0.0 copy-done.10
  43.4 0.0 copy-done.11
  43.4 2.5 %shard_map.135 = f32[4,32,64]{2,1,0:T(8,128)} custom-call(f32[16,32,128]{2,1,0:T(8,128)S(1)} %all-to-all-done.2.recv_ref, bf16[2048,256]{1,0:T(8,128)(2,1)S(1)} %get-tuple-element.15.v_ref, f32[32,1024]{1,0:T(8,128)S(1)} %get-tuple-element.16.gate_ref, f32[64,256]{1,0:T(8,128)S(1)} %bitcast.3, f32[4,32,64]{2,1,0:T(8,128)S(1)} %copy-done.1, ...), custom_call_target="tpu_custom_call" | custom-call | flops 500000000 | bytes 1769472 | tf_op jit(solution)/shard_map/pallas_call | solution.py:293
Async XLA Ops:
  0.6 0.8 %copy-start = (f32[4,32,64]{2,1,0:T(8,128)S(1)}, f32[4,32,64]{2,1,0:T(8,128)}, u32[]{:S(2)}) copy-start(f32[4,32,64]{2,1,0:T(8,128)} %x_ref.3) | copy-start | bytes 98308
  1.7 10.9 %copy-start.2 = (f32[64,64]{1,0:T(8,128)S(1)}, f32[64,64]{1,0:T(8,128)}, u32[]{:S(2)}) copy-start(f32[64,64]{1,0:T(8,128)} %w_ref.1) | copy-start | bytes 49156
  12.6 15.8 %copy-start.12 = (f32[128,8]{0,1:T(8,128)S(1)}, f32[128,8]{0,1:T(8,128)}, u32[]{:S(2)}) copy-start(f32[128,8]{0,1:T(8,128)} %param.18) | copy-start | bytes 12292
  13.3 15.2 %copy-start.3 = (f32[1024,128]{1,0:T(8,128)S(1)}, f32[1024,128]{1,0:T(8,128)}, u32[]{:S(2)}) copy-start(f32[1024,128]{1,0:T(8,128)} %t_ref.1) | copy-start | bytes 1572868
  13.3 15.2 %copy-start.5 = (f32[32,16,128]{2,1,0:T(8,128)S(1)}, f32[32,16,128]{2,1,0:T(8,128)}, u32[]{:S(2)}) copy-start(f32[32,16,128]{2,1,0:T(8,128)} %pair_ref.1) | copy-start | bytes 786436
  28.5 10.4 %copy-start.6 = (f32[512,128]{1,0:T(8,128)S(1)}, f32[512,128]{1,0:T(8,128)}, u32[]{:S(2)}) copy-start(f32[512,128]{1,0:T(8,128)} %shrink_ref.1) | copy-start | bytes 786436
  31.5 7.5 %copy-start.4 = (f32[128,1024]{1,0:T(8,128)S(1)}, f32[128,1024]{1,0:T(8,128)}, u32[]{:S(2)}) copy-start(f32[128,1024]{1,0:T(8,128)} %expand_ref.3) | copy-start | bytes 1572868
  31.5 11.9 %all-to-all-start.2 = ((f32[16,32,128]{2,1,0:T(8,128)}), f32[16,32,128]{2,1,0:T(8,128)S(1)}, u32[]{:S(2)}, u32[]{:S(2)}) async-start(f32[16,32,128]{2,1,0:T(8,128)} %get-tuple-element.12), calls=%async_computation.2 | async-start | bytes 524288 | tf_op jit(solution)/shard_map/all_to_all | solution.py:310
  38.9 2.4 %copy-start.8 = (f32[64,256]{1,0:T(8,128)S(1)}, f32[64,256]{1,0:T(8,128)}, u32[]{:S(2)}) copy-start(f32[64,256]{1,0:T(8,128)} %wv_ref.1) | copy-start | bytes 196612
  39.0 2.3 %copy-start.9 = (f32[64,256]{1,0:T(8,128)S(1)}, f32[64,256]{1,0:T(8,128)}, u32[]{:S(2)}) copy-start(f32[64,256]{1,0:T(8,128)} %wg_ref.1) | copy-start | bytes 196612
  41.3 2.1 %copy-start.1 = (f32[4,32,64]{2,1,0:T(8,128)S(1)}, f32[4,32,64]{2,1,0:T(8,128)}, u32[]{:S(2)}) copy-start(f32[4,32,64]{2,1,0:T(8,128)} %x_ref.3) | copy-start | bytes 98308
  41.3 2.1 %copy-start.7 = (f32[64,512]{1,0:T(8,128)S(1)}, f32[64,512]{1,0:T(8,128)}, u32[]{:S(2)}) copy-start(f32[64,512]{1,0:T(8,128)} %expand_ref.2) | copy-start | bytes 393220
  41.3 2.1 %copy-start.10 = (f32[256,64]{0,1:T(8,128)S(1)}, f32[256,64]{0,1:T(8,128)}, u32[]{:S(2)}) copy-start(f32[256,64]{0,1:T(8,128)} %param.19) | copy-start | bytes 196612
  41.3 2.1 %copy-start.11 = (f32[256,64]{0,1:T(8,128)S(1)}, f32[256,64]{0,1:T(8,128)}, u32[]{:S(2)}) copy-start(f32[256,64]{0,1:T(8,128)} %param.21) | copy-start | bytes 196612

commit v7 on v6

--- a/solution.py
+++ b/solution.py
@@ -125,7 +125,7 @@
         send_ref[d, 32:, :] = right[at : at + COLS]
 
 
-def values_kernel(recv_ref, wv_ref, own_ref, wg_ref, v_ref, gate_ref):
+def values_part(recv_ref, wv_ref, own_ref, wg_ref, v_ref, gate_ref):
     own = split(own_ref[...])
     for h, wg in enumerate(head_weights(wg_ref[...])):
         gate_ref[:, h * 128 : h * 128 + 128] = 1.0 / (1.0 + jnp.exp(-dot3(own, wg)))
@@ -193,7 +193,10 @@
         send_ref[d] = tile
 
 
-def pair_transition_kernel(mid_ref, expand_ref, shrink_ref, out_ref):
+def window_kernel(
+    mid_ref, expand_ref, shrink_ref, recv_ref, wv_ref, own_ref, wg_ref,
+    result_ref, v_ref, gate_ref, out_ref, sem,
+):
     eh, el = split(expand_ref[...])
     expand3 = jnp.concatenate([eh, eh, el], axis=0)
     sh, sl = split(shrink_ref[...])
@@ -210,6 +213,10 @@
         out = mid + wide[:, :128] + wide[:, 128:] + dot(al, sh)
         for j in range(step):
             out_ref[:, at + j, :] = out[j * TOK : (j + 1) * TOK]
+    copy = pltpu.make_async_copy(out_ref, result_ref, sem)
+    copy.start()
+    values_part(recv_ref, wv_ref, own_ref, wg_ref, v_ref, gate_ref)
+    copy.wait()
 
 
 def group_all(x, op):
@@ -282,7 +289,7 @@
     out_ref[...] = out.reshape(ROWS, TOK, 64)
 
 
-def call(kernel, outs, *args, specs=None, scratch=(), flops=0):
+def call(kernel, outs, *args, out_specs=None, specs=None, scratch=(), flops=0):
     vmem = pl.BlockSpec(memory_space=pltpu.VMEM)
     in_specs = [vmem] * len(args) if specs is None else [s or vmem for s in specs]
     single = not isinstance(outs, (list, tuple))
@@ -294,7 +301,7 @@
         kernel,
         out_shape=outs,
         in_specs=in_specs,
-        out_specs=[vmem] * len(outs),
+        out_specs=[vmem] * len(outs) if out_specs is None else [o or vmem for o in out_specs],
         scratch_shapes=list(scratch),
         compiler_params=pltpu.CompilerParams(vmem_limit_bytes=24 << 20),
         cost_estimate=pl.CostEstimate(flops=flops, bytes_accessed=moved, transcendentals=0),
@@ -339,22 +346,19 @@
     )
     mid, tokens = lax.optimization_barrier((mid, tokens))
     logits = exchange(logits, "tj", ORDER_LOGITS)
-    couple_result = call(
-        pair_transition_kernel,
-        shape((TOK, COLS, 128)),
+    couple_result, values, gates = call(
+        window_kernel,
+        [shape((TOK, COLS, 128)), shape((2048, 256), BF16), shape((TOK, 1024))],
         mid,
         couple_expand_matrix,
         couple_shrink_matrix,
-        flops=1_000_000_000,
-    )
-    values, gates = call(
-        values_kernel,
-        [shape((2048, 256), BF16), shape((TOK, 1024))],
         tokens,
         mixing_content_matrix,
         own,
         mixing_switch_matrix,
-        flops=1_000_000_000,
+        out_specs=[pl.BlockSpec(memory_space=pl.ANY), None, None],
+        scratch=[pltpu.VMEM((TOK, COLS, 128), F32), pltpu.SemaphoreType.DMA(())],
+        flops=2_000_000_000,
     )
     alignment_result = call(
         last_kernel,

time: 46.3 us -> 46.3 us (level)
  Pallas kernels: 9.91 us -> 8.97 us
  waiting for transfers between devices: 0.78 us -> 1.71 us
    pallas_call x6 -> x5, Pallas kernels: 9.91 us -> 8.97 us  [call(): pl.pallas_call(kernel, out_shape=outs, in_specs=in_specs, out_specs=[vmem...]
    all_to_all x1, waiting for transfers between devices: 0.78 us -> 1.71 us  [exchange(): return lax.all_to_all(x, axis, 0, 0, axis_index_groups=[order], tiled=True)]
  transfers between devices with their start and end apart: 1 -> 1, of which waited for: 1 -> 1; matrix products, arithmetic and copies ran while one was open for 0% -> 0% of each run, Pallas kernels for 8% -> 6%
where the time goes in v7:
time: 46.3 us; the launch traced here: 45.9 us
  blocking collectives  26.1 us (56%)
  Pallas kernels  8.97 us (19%)
  starting transfers between devices  7.46 us (16%)
  waiting for transfers between devices  1.71 us (4%)
  local copies, waits for them, and re-layouts  0.91 us (2%)
  between operations  0.79 us (2%)
    all_to_all x2, blocking collectives, exchange(): return lax.all_to_all(x, axis, 0, 0, axis_index_groups=[order], tiled=True)  26.1 us
    pallas_call x5, Pallas kernels, call(): pl.pallas_call(kernel, out_shape=outs, in_specs=in_specs, out_specs=[vmem...  8.97 us
    all_to_all x1, starting transfers between devices, exchange(): return lax.all_to_all(x, axis, 0, 0, axis_index_groups=[order], tiled=True)  7.46 us
    all_to_all x1, waiting for transfers between devices, exchange(): return lax.all_to_all(x, axis, 0, 0, axis_index_groups=[order], tiled=True)  1.71 us
  transfers between devices with their start and end apart: 1, of which 1 were waited for; matrix products, arithmetic and copies ran while one was open for 0% of the time, Pallas kernels for 6%

profile of v7, /device:TPU:1, one launch (start us, length us, event | category | flops | bytes accessed | tf_op | source)
XLA Modules:
  0.0 45.9 jit_solution(7121743431467812215)
XLA Ops:
  0.6 0.0 copy-start
  0.6 0.8 %copy-done = f32[4,32,64]{2,1,0:T(8,128)S(1)} copy-done((f32[4,32,64]{2,1,0:T(8,128)S(1)}, f32[4,32,64]{2,1,0:T(8,128)}, u32[]{:S(2)}) %copy-start) | copy-done | bytes 32792
  1.5 0.2 shard_map.131
  1.7 0.0 copy-start.2
  1.7 10.9 %all_to_all.15.recv_ref = f32[8,64,128]{2,1,0:T(8,128)S(1)} all-to-all(f32[8,64,128]{2,1,0:T(8,128)S(1)} %get-tuple-element.11), channel_id=1, replica_groups={{96,112,64,80,32,48,0,16},{97,113,65,81,33,49,1,17},{98,114,66,82,34,50..., dimensions={0} | all-to-all | bytes 524288 | tf_op jit(solution)/shard_map/all_to_all | solution.py:317
  12.6 0.0 copy-done.2
  12.6 0.0 copy-start.12
  12.7 0.6 %shard_map.132 = f32[16,48,128]{2,1,0:T(8,128)S(1)} custom-call(f32[8,64,128]{2,1,0:T(8,128)S(1)} %all_to_all.15.recv_ref, f32[32,256]{1,0:T(8,128)S(1)} %get-tuple-element.12.own_ref, f32[64,64]{1,0:T(8,128)S(1)} %copy-done.2), custom_call_target="tpu_custom_call" | custom-call | bytes 704512 | tf_op jit(solution)/shard_map/pallas_call | solution.py:300
  13.3 0.0 copy-start.3
  13.3 0.0 copy-start.5
  13.3 15.2 %all_to_all.16.recv_ref = f32[16,48,128]{2,1,0:T(8,128)S(1)} all-to-all(f32[16,48,128]{2,1,0:T(8,128)S(1)} %shard_map.132), channel_id=1, replica_groups={{11,10,9,8,15,14,13,12,3,2,1,0,7,6,5,4},{27,26,25,24,31,30,29,28,19,18,..., dimensions={0} | all-to-all | bytes 786432 | tf_op jit(solution)/shard_map/all_to_all | solution.py:317
  28.5 0.0 copy-done.12
  28.5 0.0 copy-done.3
  28.5 0.0 copy-done.5
  28.5 0.0 copy-start.6
  28.5 0.0 copy-start.8
  28.5 0.0 copy-start.9
  28.5 3.0 %shard_map.133 = (f32[16,32,128]{2,1,0:T(8,128)S(1)}, f32[16,32,128]{2,1,0:T(8,128)}) custom-call(f32[16,48,128]{2,1,0:T(8,128)S(1)} %all_to_all.16.recv_ref, f32[32,16,128]{2,1,0:T(8,128)S(1)} %copy-done.5, f32[1024,128]{1,0:T(8,128)S(1)} %copy-done.3, f32[8,128]{1,0:T(8,128)S(1)} %bitcast.5), custom_call_target="tpu_custom_call" | custom-call | flops 2000000000 | bytes 1708032 | tf_op jit(solution)/shard_map/pallas_call | solution.py:300
  31.5 0.0 copy-start.4
  31.5 7.5 %all-to-all-start.2 = ((f32[16,32,128]{2,1,0:T(8,128)}), f32[16,32,128]{2,1,0:T(8,128)S(1)}, u32[]{:S(2)}, u32[]{:S(2)}) async-start(f32[16,32,128]{2,1,0:T(8,128)} %get-tuple-element.13), calls=%async_computation.2 | async-start | bytes 524288 | tf_op jit(solution)/shard_map/all_to_all | solution.py:317
  38.9 0.0 copy-done.6
  39.0 0.0 copy-done.8
  39.0 0.0 copy-done.9
  39.0 0.0 copy-done.4
  39.0 0.0 copy-start.1
  39.0 0.0 copy-start.7
  39.0 0.0 copy-start.10
  39.0 0.0 copy-start.11
  39.0 2.7 %shard_map.134 = (f32[32,16,128]{2,1,0:T(8,128)}, bf16[2048,256]{1,0:T(8,128)(2,1)S(1)}, f32[32,1024]{1,0:T(8,128)S(1)}) custom-call(f32[16,32,128]{2,1,0:T(8,128)S(1)} %get-tuple-element.15.mid_ref, f32[128,1024]{1,0:T(8,128)S(1)} %copy-done.4, f32[512,128]{1,0:T(8,128)S(1)} %copy-done.6, f32[8,64,128]{2,1,0:T(8,128)S(1)} %all_to_all.15.recv_ref, ...), custom_call_target="tpu_custom_call" | custom-call | flops 2000000000 | bytes 2916352 | tf_op jit(solution)/shard_map/pallas_call | solution.py:300
  41.7 1.7 %all-to-all-done.2.recv_ref = f32[16,32,128]{2,1,0:T(8,128)S(1)} async-done(((f32[16,32,128]{2,1,0:T(8,128)}), f32[16,32,128]{2,1,0:T(8,128)S(1)}, u32[]{:S(2)}, u32[]{:S(2)}) %all-to-all-start.2) | async-done | bytes 262176 | tf_op jit(solution)/shard_map/all_to_all | solution.py:317
  43.4 0.0 copy-done.1
  43.4 0.0 copy-done.7
  43.4 0.0 copy-done.10
  43.4 0.0 copy-done.11
  43.4 2.5 %shard_map.135 = f32[4,32,64]{2,1,0:T(8,128)} custom-call(f32[16,32,128]{2,1,0:T(8,128)S(1)} %all-to-all-done.2.recv_ref, bf16[2048,256]{1,0:T(8,128)(2,1)S(1)} %get-tuple-element.17.v_ref, f32[32,1024]{1,0:T(8,128)S(1)} %get-tuple-element.18.gate_ref, f32[64,256]{1,0:T(8,128)S(1)} %bitcast.3, f32[4,32,64]{2,1,0:T(8,128)S(1)} %copy-done.1, ...), custom_call_target="tpu_custom_call" | custom-call | flops 500000000 | bytes 1769472 | tf_op jit(solution)/shard_map/pallas_call | solution.py:300
Async XLA Ops:
  0.6 0.8 %copy-start = (f32[4,32,64]{2,1,0:T(8,128)S(1)}, f32[4,32,64]{2,1,0:T(8,128)}, u32[]{:S(2)}) copy-start(f32[4,32,64]{2,1,0:T(8,128)} %x_ref.3) | copy-start | bytes 98308
  1.7 10.9 %copy-start.2 = (f32[64,64]{1,0:T(8,128)S(1)}, f32[64,64]{1,0:T(8,128)}, u32[]{:S(2)}) copy-start(f32[64,64]{1,0:T(8,128)} %w_ref.1) | copy-start | bytes 49156
  12.6 15.8 %copy-start.12 = (f32[128,8]{0,1:T(8,128)S(1)}, f32[128,8]{0,1:T(8,128)}, u32[]{:S(2)}) copy-start(f32[128,8]{0,1:T(8,128)} %param.18) | copy-start | bytes 12292
  13.3 15.2 %copy-start.3 = (f32[1024,128]{1,0:T(8,128)S(1)}, f32[1024,128]{1,0:T(8,128)}, u32[]{:S(2)}) copy-start(f32[1024,128]{1,0:T(8,128)} %t_ref.1) | copy-start | bytes 1572868
  13.3 15.2 %copy-start.5 = (f32[32,16,128]{2,1,0:T(8,128)S(1)}, f32[32,16,128]{2,1,0:T(8,128)}, u32[]{:S(2)}) copy-start(f32[32,16,128]{2,1,0:T(8,128)} %pair_ref.1) | copy-start | bytes 786436
  28.5 10.5 %copy-start.6 = (f32[512,128]{1,0:T(8,128)S(1)}, f32[512,128]{1,0:T(8,128)}, u32[]{:S(2)}) copy-start(f32[512,128]{1,0:T(8,128)} %shrink_ref.1) | copy-start | bytes 786436
  28.5 10.5 %copy-start.8 = (f32[64,256]{1,0:T(8,128)S(1)}, f32[64,256]{1,0:T(8,128)}, u32[]{:S(2)}) copy-start(f32[64,256]{1,0:T(8,128)} %wv_ref.1) | copy-start | bytes 196612
  28.5 10.5 %copy-start.9 = (f32[64,256]{1,0:T(8,128)S(1)}, f32[64,256]{1,0:T(8,128)}, u32[]{:S(2)}) copy-start(f32[64,256]{1,0:T(8,128)} %wg_ref.1) | copy-start | bytes 196612
  31.5 7.5 %copy-start.4 = (f32[128,1024]{1,0:T(8,128)S(1)}, f32[128,1024]{1,0:T(8,128)}, u32[]{:S(2)}) copy-start(f32[128,1024]{1,0:T(8,128)} %expand_ref.2) | copy-start | bytes 1572868
  31.5 11.9 %all-to-all-start.2 = ((f32[16,32,128]{2,1,0:T(8,128)}), f32[16,32,128]{2,1,0:T(8,128)S(1)}, u32[]{:S(2)}, u32[]{:S(2)}) async-start(f32[16,32,128]{2,1,0:T(8,128)} %get-tuple-element.13), calls=%async_computation.2 | async-start | bytes 524288 | tf_op jit(solution)/shard_map/all_to_all | solution.py:317
  39.0 4.4 %copy-start.1 = (f32[4,32,64]{2,1,0:T(8,128)S(1)}, f32[4,32,64]{2,1,0:T(8,128)}, u32[]{:S(2)}) copy-start(f32[4,32,64]{2,1,0:T(8,128)} %x_ref.3) | copy-start | bytes 98308
  39.0 4.4 %copy-start.7 = (f32[64,512]{1,0:T(8,128)S(1)}, f32[64,512]{1,0:T(8,128)}, u32[]{:S(2)}) copy-start(f32[64,512]{1,0:T(8,128)} %expand_ref.3) | copy-start | bytes 393220
  39.0 4.4 %copy-start.10 = (f32[256,64]{0,1:T(8,128)S(1)}, f32[256,64]{0,1:T(8,128)}, u32[]{:S(2)}) copy-start(f32[256,64]{0,1:T(8,128)} %param.19) | copy-start | bytes 196612
  39.0 4.4 %copy-start.11 = (f32[256,64]{0,1:T(8,128)S(1)}, f32[256,64]{0,1:T(8,128)}, u32[]{:S(2)}) copy-start(f32[256,64]{0,1:T(8,128)} %param.21) | copy-start | bytes 196612

commit v8 on v7

--- a/solution.py
+++ b/solution.py
@@ -72,12 +72,10 @@
     return out
 
 
-def first_kernel(x_ref, send_ref, own_ref):
+def first_kernel(x_ref, send_ref):
     x = normed(x_ref[...])
     low = jnp.concatenate([x[0], x[1]], axis=1)
     high = jnp.concatenate([x[2], x[3]], axis=1)
-    own_ref[:, :128] = low
-    own_ref[:, 128:] = high
     for d in range(TI):
         send_ref[d, :TOK, :] = low
         send_ref[d, TOK:, :] = high
@@ -102,7 +100,7 @@
     wr_low = tuple(jnp.concatenate(tiles[:2], axis=0) for tiles in wr)
     wr_high = tuple(jnp.concatenate(tiles[2:], axis=0) for tiles in wr)
     right = dot3(low, wr_low) + dot3(high, wr_high)
-    xs = tuple(jnp.concatenate([part] * 4, axis=0) for part in split(own_ref[...]))
+    xs = tuple(jnp.concatenate([part] * 4, axis=0) for part in split(jnp.concatenate([own_ref[0, :TOK, :], own_ref[0, TOK:, :]], axis=1)))
     pick = (iota((128, 64), 0) // 4 == iota((128, 64), 1)).astype(BF16)
     keep = iota((128, 256), 0) % 4 == iota((128, 256), 1) // 64
     wl = []
@@ -126,7 +124,7 @@
 
 
 def values_part(recv_ref, wv_ref, own_ref, wg_ref, v_ref, gate_ref):
-    own = split(own_ref[...])
+    own = split(jnp.concatenate([own_ref[0, :TOK, :], own_ref[0, TOK:, :]], axis=1))
     for h, wg in enumerate(head_weights(wg_ref[...])):
         gate_ref[:, h * 128 : h * 128 + 128] = 1.0 / (1.0 + jnp.exp(-dot3(own, wg)))
     low, high = all_tokens(recv_ref)
@@ -331,8 +329,8 @@
     couple_expand_matrix,
     couple_shrink_matrix,
 ):
-    send, own = call(first_kernel, [shape((TI, 64, 128)), shape((TOK, 256))], alignment_source)
-    tokens = exchange(send, "ti", ORDER_TI)
+    own = call(first_kernel, shape((TI, 64, 128)), alignment_source)
+    tokens = exchange(own, "ti", ORDER_TI)
     factors = call(factors_kernel, shape((TJ, 48, 128)), tokens, own, tensor_operand_matrix)
     factors = exchange(factors, "tj", ORDER_TJ)
     mid, logits = call(

time: 46.3 us -> 46.3 us (level)
  no operation moved by 1% of the time
where the time goes in v8:
time: 46.3 us; the launch traced here: 46 us
  blocking collectives  26.1 us (56%)
  Pallas kernels  9.02 us (19%)
  starting transfers between devices  7.46 us (16%)
  waiting for transfers between devices  1.7 us (4%)
  local copies, waits for them, and re-layouts  0.91 us (2%)
  between operations  0.79 us (2%)
    all_to_all x2, blocking collectives, exchange(): return lax.all_to_all(x, axis, 0, 0, axis_index_groups=[order], tiled=True)  26.1 us
    pallas_call x5, Pallas kernels, call(): pl.pallas_call(kernel, out_shape=outs, in_specs=in_specs, out_specs=[vmem...  9.02 us
    all_to_all x1, starting transfers between devices, exchange(): return lax.all_to_all(x, axis, 0, 0, axis_index_groups=[order], tiled=True)  7.46 us
    all_to_all x1, waiting for transfers between devices, exchange(): return lax.all_to_all(x, axis, 0, 0, axis_index_groups=[order], tiled=True)  1.7 us
  transfers between devices with their start and end apart: 1, of which 1 were waited for; matrix products, arithmetic and copies ran while one was open for 0% of the time, Pallas kernels for 6%

profile of v8, /device:TPU:1, one launch (start us, length us, event | category | flops | bytes accessed | tf_op | source)
XLA Modules:
  0.0 46.0 jit_solution(10124879633853637145)
XLA Ops:
  0.6 0.0 copy-start
  0.6 0.8 %copy-done = f32[4,32,64]{2,1,0:T(8,128)S(1)} copy-done((f32[4,32,64]{2,1,0:T(8,128)S(1)}, f32[4,32,64]{2,1,0:T(8,128)}, u32[]{:S(2)}) %copy-start) | copy-done | bytes 32792
  1.5 0.2 shard_map.131.own_ref
  1.7 0.0 copy-start.2
  1.7 10.9 %all_to_all.15.recv_ref = f32[8,64,128]{2,1,0:T(8,128)S(1)} all-to-all(f32[8,64,128]{2,1,0:T(8,128)S(1)} %shard_map.131.own_ref), channel_id=1, replica_groups={{96,112,64,80,32,48,0,16},{97,113,65,81,33,49,1,17},{98,114,66,82,34,50..., dimensions={0} | all-to-all | bytes 524288 | tf_op jit(solution)/shard_map/all_to_all | solution.py:315
  12.6 0.0 copy-done.2
  12.6 0.0 copy-start.12
  12.6 0.6 %shard_map.132 = f32[16,48,128]{2,1,0:T(8,128)S(1)} custom-call(f32[8,64,128]{2,1,0:T(8,128)S(1)} %all_to_all.15.recv_ref, f32[8,64,128]{2,1,0:T(8,128)S(1)} %shard_map.131.own_ref, f32[64,64]{1,0:T(8,128)S(1)} %copy-done.2), custom_call_target="tpu_custom_call" | custom-call | bytes 933888 | tf_op jit(solution)/shard_map/pallas_call | solution.py:298
  13.3 0.0 copy-start.3
  13.3 0.0 copy-start.5
  13.3 15.2 %all_to_all.16.recv_ref = f32[16,48,128]{2,1,0:T(8,128)S(1)} all-to-all(f32[16,48,128]{2,1,0:T(8,128)S(1)} %shard_map.132), channel_id=1, replica_groups={{11,10,9,8,15,14,13,12,3,2,1,0,7,6,5,4},{27,26,25,24,31,30,29,28,19,18,..., dimensions={0} | all-to-all | bytes 786432 | tf_op jit(solution)/shard_map/all_to_all | solution.py:315
  28.5 0.0 copy-done.12
  28.5 0.0 copy-done.3
  28.5 0.0 copy-done.5
  28.5 0.0 copy-start.6
  28.5 0.0 copy-start.8
  28.5 0.0 copy-start.9
  28.5 3.0 %shard_map.133 = (f32[16,32,128]{2,1,0:T(8,128)S(1)}, f32[16,32,128]{2,1,0:T(8,128)}) custom-call(f32[16,48,128]{2,1,0:T(8,128)S(1)} %all_to_all.16.recv_ref, f32[32,16,128]{2,1,0:T(8,128)S(1)} %copy-done.5, f32[1024,128]{1,0:T(8,128)S(1)} %copy-done.3, f32[8,128]{1,0:T(8,128)S(1)} %bitcast.5), custom_call_target="tpu_custom_call" | custom-call | flops 2000000000 | bytes 1708032 | tf_op jit(solution)/shard_map/pallas_call | solution.py:298
  31.5 0.0 copy-start.4
  31.5 7.5 %all-to-all-start.2 = ((f32[16,32,128]{2,1,0:T(8,128)}), f32[16,32,128]{2,1,0:T(8,128)S(1)}, u32[]{:S(2)}, u32[]{:S(2)}) async-start(f32[16,32,128]{2,1,0:T(8,128)} %get-tuple-element.9), calls=%async_computation.2 | async-start | bytes 524288 | tf_op jit(solution)/shard_map/all_to_all | solution.py:315
  39.0 0.0 copy-done.6
  39.0 0.0 copy-done.8
  39.0 0.0 copy-done.9
  39.0 0.0 copy-done.4
  39.0 0.0 copy-start.1
  39.0 0.0 copy-start.7
  39.0 0.0 copy-start.10
  39.1 0.0 copy-start.11
  39.1 2.7 %shard_map.134 = (f32[32,16,128]{2,1,0:T(8,128)}, bf16[2048,256]{1,0:T(8,128)(2,1)S(1)}, f32[32,1024]{1,0:T(8,128)S(1)}) custom-call(f32[16,32,128]{2,1,0:T(8,128)S(1)} %get-tuple-element.11.mid_ref, f32[128,1024]{1,0:T(8,128)S(1)} %copy-done.4, f32[512,128]{1,0:T(8,128)S(1)} %copy-done.6, f32[8,64,128]{2,1,0:T(8,128)S(1)} %all_to_all.15.recv_ref, ...), custom_call_target="tpu_custom_call" | custom-call | flops 2000000000 | bytes 3145728 | tf_op jit(solution)/shard_map/pallas_call | solution.py:298
  41.7 1.7 %all-to-all-done.2.recv_ref = f32[16,32,128]{2,1,0:T(8,128)S(1)} async-done(((f32[16,32,128]{2,1,0:T(8,128)}), f32[16,32,128]{2,1,0:T(8,128)S(1)}, u32[]{:S(2)}, u32[]{:S(2)}) %all-to-all-start.2) | async-done | bytes 262176 | tf_op jit(solution)/shard_map/all_to_all | solution.py:315
  43.4 0.0 copy-done.1
  43.4 0.0 copy-done.7
  43.4 0.0 copy-done.10
  43.5 0.0 copy-done.11
  43.5 2.5 %shard_map.135 = f32[4,32,64]{2,1,0:T(8,128)} custom-call(f32[16,32,128]{2,1,0:T(8,128)S(1)} %all-to-all-done.2.recv_ref, bf16[2048,256]{1,0:T(8,128)(2,1)S(1)} %get-tuple-element.13.v_ref, f32[32,1024]{1,0:T(8,128)S(1)} %get-tuple-element.14.gate_ref, f32[64,256]{1,0:T(8,128)S(1)} %bitcast.3, f32[4,32,64]{2,1,0:T(8,128)S(1)} %copy-done.1, ...), custom_call_target="tpu_custom_call" | custom-call | flops 500000000 | bytes 1769472 | tf_op jit(solution)/shard_map/pallas_call | solution.py:298
Async XLA Ops:
  0.6 0.8 %copy-start = (f32[4,32,64]{2,1,0:T(8,128)S(1)}, f32[4,32,64]{2,1,0:T(8,128)}, u32[]{:S(2)}) copy-start(f32[4,32,64]{2,1,0:T(8,128)} %x_ref.3) | copy-start | bytes 98308
  1.7 10.9 %copy-start.2 = (f32[64,64]{1,0:T(8,128)S(1)}, f32[64,64]{1,0:T(8,128)}, u32[]{:S(2)}) copy-start(f32[64,64]{1,0:T(8,128)} %w_ref.1) | copy-start | bytes 49156
  12.6 15.8 %copy-start.12 = (f32[128,8]{0,1:T(8,128)S(1)}, f32[128,8]{0,1:T(8,128)}, u32[]{:S(2)}) copy-start(f32[128,8]{0,1:T(8,128)} %param.18) | copy-start | bytes 12292
  13.3 15.2 %copy-start.3 = (f32[1024,128]{1,0:T(8,128)S(1)}, f32[1024,128]{1,0:T(8,128)}, u32[]{:S(2)}) copy-start(f32[1024,128]{1,0:T(8,128)} %t_ref.1) | copy-start | bytes 1572868
  13.3 15.2 %copy-start.5 = (f32[32,16,128]{2,1,0:T(8,128)S(1)}, f32[32,16,128]{2,1,0:T(8,128)}, u32[]{:S(2)}) copy-start(f32[32,16,128]{2,1,0:T(8,128)} %pair_ref.1) | copy-start | bytes 786436
  28.5 10.5 %copy-start.6 = (f32[512,128]{1,0:T(8,128)S(1)}, f32[512,128]{1,0:T(8,128)}, u32[]{:S(2)}) copy-start(f32[512,128]{1,0:T(8,128)} %shrink_ref.1) | copy-start | bytes 786436
  28.5 10.5 %copy-start.8 = (f32[64,256]{1,0:T(8,128)S(1)}, f32[64,256]{1,0:T(8,128)}, u32[]{:S(2)}) copy-start(f32[64,256]{1,0:T(8,128)} %wv_ref.1) | copy-start | bytes 196612
  28.5 10.5 %copy-start.9 = (f32[64,256]{1,0:T(8,128)S(1)}, f32[64,256]{1,0:T(8,128)}, u32[]{:S(2)}) copy-start(f32[64,256]{1,0:T(8,128)} %wg_ref.1) | copy-start | bytes 196612
  31.5 7.5 %copy-start.4 = (f32[128,1024]{1,0:T(8,128)S(1)}, f32[128,1024]{1,0:T(8,128)}, u32[]{:S(2)}) copy-start(f32[128,1024]{1,0:T(8,128)} %expand_ref.2) | copy-start | bytes 1572868
  31.5 11.9 %all-to-all-start.2 = ((f32[16,32,128]{2,1,0:T(8,128)}), f32[16,32,128]{2,1,0:T(8,128)S(1)}, u32[]{:S(2)}, u32[]{:S(2)}) async-start(f32[16,32,128]{2,1,0:T(8,128)} %get-tuple-element.9), calls=%async_computation.2 | async-start | bytes 524288 | tf_op jit(solution)/shard_map/all_to_all | solution.py:315
  39.0 4.4 %copy-start.1 = (f32[4,32,64]{2,1,0:T(8,128)S(1)}, f32[4,32,64]{2,1,0:T(8,128)}, u32[]{:S(2)}) copy-start(f32[4,32,64]{2,1,0:T(8,128)} %x_ref.3) | copy-start | bytes 98308
  39.0 4.4 %copy-start.7 = (f32[64,512]{1,0:T(8,128)S(1)}, f32[64,512]{1,0:T(8,128)}, u32[]{:S(2)}) copy-start(f32[64,512]{1,0:T(8,128)} %expand_ref.3) | copy-start | bytes 393220
  39.0 4.4 %copy-start.10 = (f32[256,64]{0,1:T(8,128)S(1)}, f32[256,64]{0,1:T(8,128)}, u32[]{:S(2)}) copy-start(f32[256,64]{0,1:T(8,128)} %param.19) | copy-start | bytes 196612
  39.1 4.4 %copy-start.11 = (f32[256,64]{0,1:T(8,128)S(1)}, f32[256,64]{0,1:T(8,128)}, u32[]{:S(2)}) copy-start(f32[256,64]{0,1:T(8,128)} %param.21) | copy-start | bytes 196612

commit v9 on v7

--- a/solution.py
+++ b/solution.py
@@ -14,8 +14,8 @@
 TOK = 32
 COLS = 16
 ORDER_TI = [k ^ 6 for k in range(8)]
-ORDER_TJ = [k ^ 11 for k in range(16)]
-ORDER_LOGITS = [k ^ 10 for k in range(16)]
+ORDER_TJ = [11, 10, 9, 8, 15, 14, 13, 12, 3, 2, 1, 0, 7, 5, 6, 4]
+ORDER_LOGITS = [10, 11, 8, 9, 14, 15, 12, 13, 3, 2, 0, 1, 6, 7, 4, 5]
 NN = (((1,), (0,)), ((), ()))
 NT = (((1,), (1,)), ((), ()))
 

time: 46.3 us -> 46.2 us (level)
  no operation moved by 1% of the time
where the time goes in v9:
time: 46.2 us; the launch traced here: 45.8 us
  blocking collectives  26.1 us (56%)
  Pallas kernels  8.97 us (19%)
  starting transfers between devices  7.43 us (16%)
  waiting for transfers between devices  1.61 us (3%)
  local copies, waits for them, and re-layouts  0.91 us (2%)
  between operations  0.79 us (2%)
    all_to_all x2, blocking collectives, exchange(): return lax.all_to_all(x, axis, 0, 0, axis_index_groups=[order], tiled=True)  26.1 us
    pallas_call x5, Pallas kernels, call(): pl.pallas_call(kernel, out_shape=outs, in_specs=in_specs, out_specs=[vmem...  8.97 us
    all_to_all x1, starting transfers between devices, exchange(): return lax.all_to_all(x, axis, 0, 0, axis_index_groups=[order], tiled=True)  7.43 us
    all_to_all x1, waiting for transfers between devices, exchange(): return lax.all_to_all(x, axis, 0, 0, axis_index_groups=[order], tiled=True)  1.61 us
  transfers between devices with their start and end apart: 1, of which 1 were waited for; matrix products, arithmetic and copies ran while one was open for 0% of the time, Pallas kernels for 6%

profile of v9, /device:TPU:1, one launch (start us, length us, event | category | flops | bytes accessed | tf_op | source)
XLA Modules:
  0.0 45.8 jit_solution(1310326976276072770)
XLA Ops:
  0.6 0.0 copy-start
  0.6 0.8 %copy-done = f32[4,32,64]{2,1,0:T(8,128)S(1)} copy-done((f32[4,32,64]{2,1,0:T(8,128)S(1)}, f32[4,32,64]{2,1,0:T(8,128)}, u32[]{:S(2)}) %copy-start) | copy-done | bytes 32792
  1.5 0.2 shard_map.131
  1.7 0.0 copy-start.2
  1.7 10.9 %all_to_all.15.recv_ref = f32[8,64,128]{2,1,0:T(8,128)S(1)} all-to-all(f32[8,64,128]{2,1,0:T(8,128)S(1)} %get-tuple-element.11), channel_id=1, replica_groups={{96,112,64,80,32,48,0,16},{97,113,65,81,33,49,1,17},{98,114,66,82,34,50..., dimensions={0} | all-to-all | bytes 524288 | tf_op jit(solution)/shard_map/all_to_all | solution.py:317
  12.6 0.0 copy-done.2
  12.6 0.0 copy-start.12
  12.7 0.6 %shard_map.132 = f32[16,48,128]{2,1,0:T(8,128)S(1)} custom-call(f32[8,64,128]{2,1,0:T(8,128)S(1)} %all_to_all.15.recv_ref, f32[32,256]{1,0:T(8,128)S(1)} %get-tuple-element.12.own_ref, f32[64,64]{1,0:T(8,128)S(1)} %copy-done.2), custom_call_target="tpu_custom_call" | custom-call | bytes 704512 | tf_op jit(solution)/shard_map/pallas_call | solution.py:300
  13.3 0.0 copy-start.3
  13.3 0.0 copy-start.5
  13.3 15.2 %all_to_all.16.recv_ref = f32[16,48,128]{2,1,0:T(8,128)S(1)} all-to-all(f32[16,48,128]{2,1,0:T(8,128)S(1)} %shard_map.132), channel_id=1, replica_groups={{11,10,9,8,15,14,13,12,3,2,1,0,7,5,6,4},{27,26,25,24,31,30,29,28,19,18,..., dimensions={0} | all-to-all | bytes 786432 | tf_op jit(solution)/shard_map/all_to_all | solution.py:317
  28.5 0.0 copy-done.12
  28.5 0.0 copy-done.3
  28.5 0.0 copy-done.5
  28.5 0.0 copy-start.6
  28.5 0.0 copy-start.8
  28.5 0.0 copy-start.9
  28.5 3.0 %shard_map.133 = (f32[16,32,128]{2,1,0:T(8,128)S(1)}, f32[16,32,128]{2,1,0:T(8,128)}) custom-call(f32[16,48,128]{2,1,0:T(8,128)S(1)} %all_to_all.16.recv_ref, f32[32,16,128]{2,1,0:T(8,128)S(1)} %copy-done.5, f32[1024,128]{1,0:T(8,128)S(1)} %copy-done.3, f32[8,128]{1,0:T(8,128)S(1)} %bitcast.5), custom_call_target="tpu_custom_call" | custom-call | flops 2000000000 | bytes 1708032 | tf_op jit(solution)/shard_map/pallas_call | solution.py:300
  31.5 0.0 copy-start.4
  31.5 7.4 %all-to-all-start.2 = ((f32[16,32,128]{2,1,0:T(8,128)}), f32[16,32,128]{2,1,0:T(8,128)S(1)}, u32[]{:S(2)}, u32[]{:S(2)}) async-start(f32[16,32,128]{2,1,0:T(8,128)} %get-tuple-element.13), calls=%async_computation.2 | async-start | bytes 524288 | tf_op jit(solution)/shard_map/all_to_all | solution.py:317
  38.9 0.0 copy-done.6
  38.9 0.0 copy-done.8
  38.9 0.0 copy-done.9
  38.9 0.0 copy-done.4
  39.0 0.0 copy-start.1
  39.0 0.0 copy-start.7
  39.0 0.0 copy-start.10
  39.0 0.0 copy-start.11
  39.0 2.7 %shard_map.134 = (f32[32,16,128]{2,1,0:T(8,128)}, bf16[2048,256]{1,0:T(8,128)(2,1)S(1)}, f32[32,1024]{1,0:T(8,128)S(1)}) custom-call(f32[16,32,128]{2,1,0:T(8,128)S(1)} %get-tuple-element.15.mid_ref, f32[128,1024]{1,0:T(8,128)S(1)} %copy-done.4, f32[512,128]{1,0:T(8,128)S(1)} %copy-done.6, f32[8,64,128]{2,1,0:T(8,128)S(1)} %all_to_all.15.recv_ref, ...), custom_call_target="tpu_custom_call" | custom-call | flops 2000000000 | bytes 2916352 | tf_op jit(solution)/shard_map/pallas_call | solution.py:300
  41.7 1.6 %all-to-all-done.2.recv_ref = f32[16,32,128]{2,1,0:T(8,128)S(1)} async-done(((f32[16,32,128]{2,1,0:T(8,128)}), f32[16,32,128]{2,1,0:T(8,128)S(1)}, u32[]{:S(2)}, u32[]{:S(2)}) %all-to-all-start.2) | async-done | bytes 262176 | tf_op jit(solution)/shard_map/all_to_all | solution.py:317
  43.3 0.0 copy-done.1
  43.3 0.0 copy-done.7
  43.3 0.0 copy-done.10
  43.3 0.0 copy-done.11
  43.3 2.5 %shard_map.135 = f32[4,32,64]{2,1,0:T(8,128)} custom-call(f32[16,32,128]{2,1,0:T(8,128)S(1)} %all-to-all-done.2.recv_ref, bf16[2048,256]{1,0:T(8,128)(2,1)S(1)} %get-tuple-element.17.v_ref, f32[32,1024]{1,0:T(8,128)S(1)} %get-tuple-element.18.gate_ref, f32[64,256]{1,0:T(8,128)S(1)} %bitcast.3, f32[4,32,64]{2,1,0:T(8,128)S(1)} %copy-done.1, ...), custom_call_target="tpu_custom_call" | custom-call | flops 500000000 | bytes 1769472 | tf_op jit(solution)/shard_map/pallas_call | solution.py:300
Async XLA Ops:
  0.6 0.8 %copy-start = (f32[4,32,64]{2,1,0:T(8,128)S(1)}, f32[4,32,64]{2,1,0:T(8,128)}, u32[]{:S(2)}) copy-start(f32[4,32,64]{2,1,0:T(8,128)} %x_ref.3) | copy-start | bytes 98308
  1.7 10.9 %copy-start.2 = (f32[64,64]{1,0:T(8,128)S(1)}, f32[64,64]{1,0:T(8,128)}, u32[]{:S(2)}) copy-start(f32[64,64]{1,0:T(8,128)} %w_ref.1) | copy-start | bytes 49156
  12.6 15.8 %copy-start.12 = (f32[128,8]{0,1:T(8,128)S(1)}, f32[128,8]{0,1:T(8,128)}, u32[]{:S(2)}) copy-start(f32[128,8]{0,1:T(8,128)} %param.18) | copy-start | bytes 12292
  13.3 15.2 %copy-start.3 = (f32[1024,128]{1,0:T(8,128)S(1)}, f32[1024,128]{1,0:T(8,128)}, u32[]{:S(2)}) copy-start(f32[1024,128]{1,0:T(8,128)} %t_ref.1) | copy-start | bytes 1572868
  13.3 15.2 %copy-start.5 = (f32[32,16,128]{2,1,0:T(8,128)S(1)}, f32[32,16,128]{2,1,0:T(8,128)}, u32[]{:S(2)}) copy-start(f32[32,16,128]{2,1,0:T(8,128)} %pair_ref.1) | copy-start | bytes 786436
  28.5 10.4 %copy-start.6 = (f32[512,128]{1,0:T(8,128)S(1)}, f32[512,128]{1,0:T(8,128)}, u32[]{:S(2)}) copy-start(f32[512,128]{1,0:T(8,128)} %shrink_ref.1) | copy-start | bytes 786436
  28.5 10.4 %copy-start.8 = (f32[64,256]{1,0:T(8,128)S(1)}, f32[64,256]{1,0:T(8,128)}, u32[]{:S(2)}) copy-start(f32[64,256]{1,0:T(8,128)} %wv_ref.1) | copy-start | bytes 196612
  28.5 10.4 %copy-start.9 = (f32[64,256]{1,0:T(8,128)S(1)}, f32[64,256]{1,0:T(8,128)}, u32[]{:S(2)}) copy-start(f32[64,256]{1,0:T(8,128)} %wg_ref.1) | copy-start | bytes 196612
  31.5 7.5 %copy-start.4 = (f32[128,1024]{1,0:T(8,128)S(1)}, f32[128,1024]{1,0:T(8,128)}, u32[]{:S(2)}) copy-start(f32[128,1024]{1,0:T(8,128)} %expand_ref.2) | copy-start | bytes 1572868
  31.5 11.8 %all-to-all-start.2 = ((f32[16,32,128]{2,1,0:T(8,128)}), f32[16,32,128]{2,1,0:T(8,128)S(1)}, u32[]{:S(2)}, u32[]{:S(2)}) async-start(f32[16,32,128]{2,1,0:T(8,128)} %get-tuple-element.13), calls=%async_computation.2 | async-start | bytes 524288 | tf_op jit(solution)/shard_map/all_to_all | solution.py:317
  39.0 4.3 %copy-start.1 = (f32[4,32,64]{2,1,0:T(8,128)S(1)}, f32[4,32,64]{2,1,0:T(8,128)}, u32[]{:S(2)}) copy-start(f32[4,32,64]{2,1,0:T(8,128)} %x_ref.3) | copy-start | bytes 98308
  39.0 4.3 %copy-start.7 = (f32[64,512]{1,0:T(8,128)S(1)}, f32[64,512]{1,0:T(8,128)}, u32[]{:S(2)}) copy-start(f32[64,512]{1,0:T(8,128)} %expand_ref.3) | copy-start | bytes 393220
  39.0 4.3 %copy-start.10 = (f32[256,64]{0,1:T(8,128)S(1)}, f32[256,64]{0,1:T(8,128)}, u32[]{:S(2)}) copy-start(f32[256,64]{0,1:T(8,128)} %param.19) | copy-start | bytes 196612
  39.0 4.3 %copy-start.11 = (f32[256,64]{0,1:T(8,128)S(1)}, f32[256,64]{0,1:T(8,128)}, u32[]{:S(2)}) copy-start(f32[256,64]{0,1:T(8,128)} %param.21) | copy-start | bytes 196612
